TPU v7x, 512 devices: a whole 4x8x8 slice. The times are simulated.
512 devices in a mesh: grid: 256 (over x, y_lo, z, core), layer: 2 (over y_hi).
Axes of the slice: x: 4, y: 8 (y_hi: 2, y_lo: 4; y = y_hi * 4 + y_lo), z: 8, core: 2. Of those that a mesh axis runs over, the one named last changes fastest.
Arguments:
- x_tiles: bfloat16 [256, 512, 512], P('grid'), may hold values from -1.03 to 1.03, as said below
- pattern: int32 [256, 8, 8], P('grid'), may hold values from 0 to 1, as said below
Outputs:
- signed: bfloat16 [256, 128, 512], P('grid', 'layer')
Inputs may be any that keep to these rules, and one draw needn't show every extreme that they name: `x_tiles`: tile (j, i) is the transpose of tile (i, j). symmetric: the block pattern of the whole matrix is its own transpose, and every diagonal block is kept.
All inputs are finite; a program needn't handle non-finite values.
Results may differ from a plain program's by a relative error of at most 0.013.
Values may be sent and summed in bfloat16 or wider, within the bound.
No kernel may reach another device: no remote copies, remote signals or barrier semaphores. Data moves between devices by JAX's collectives and lax.ppermute only.
A program may use at most 64 MiB of HBM per device.

v0:
```python
import math

import jax
import jax.numpy as jnp
from jax import lax
from jax.sharding import PartitionSpec as P

SLAB = 128


def from_partner(block, axis, apart):
    count = lax.axis_size(axis)
    route = []
    for low in range(count):
        high = low | 1 << apart
        if high != low and high < count:
            route += [(low, high), (high, low)]
    return lax.ppermute(block, axis, route)


def row_move(tile, level):
    return from_partner(tile, "grid", level)


def col_move(tile, level):
    return from_partner(tile, "grid", level)


def tile_product(left, right):
    occupied = jnp.any(left != 0) & jnp.any(right != 0)

    def multiply(operands):
        return jnp.dot(operands[0], operands[1], preferred_element_type=jnp.float32)

    def nothing(operands):
        return jnp.zeros((operands[0].shape[0], operands[1].shape[1]), jnp.float32)

    return lax.cond(occupied, multiply, nothing, (left, right))


def lowest_bit(number):
    level = 0
    while number >> level & 1 == 0:
        level = level + 1
    return level


def gray_flips(turns):
    flips = []
    for inner in range(min(turns, 8)):
        if inner > 0:
            flips.append(lowest_bit(inner))
    return flips


def align_left(left, amount, bit_count):
    for level in range(bit_count):
        moved = row_move(left, level)
        left = jnp.where(amount >> level & 1 == 1, moved, left)
    return left


def walk(left, right, flips, bit_count):
    total = tile_product(left, right)
    for level in flips:
        left = row_move(left, level)
        right = col_move(right, level + bit_count)
        total = total + tile_product(left, right)
    return (total, right)


def shards(x_tiles, pattern):
    side = math.isqrt(lax.axis_size("grid"))
    bit_count = side.bit_length() - 1
    layers = lax.axis_size("layer")
    position = lax.axis_index("grid")
    row_index = position // side
    column = position % side
    layer_index = lax.axis_index("layer")
    blocks = pattern.shape[1]
    width = x_tiles.shape[1]
    span = width // blocks
    mask = jnp.broadcast_to(pattern[0][:, None, :, None], (blocks, span, blocks, span))
    mask = mask.reshape(width, width).astype(jnp.bfloat16)
    matrix = x_tiles[0] * mask
    slab = matrix[:SLAB]
    share = SLAB // layers
    own = lax.dynamic_slice_in_dim(slab, layer_index * share, share, 0)
    turns = side // layers
    start = layer_index * turns
    flips = gray_flips(turns)
    finish = start ^ turns // 2
    left = align_left(slab, row_index ^ start, bit_count)
    right = matrix
    right_amount = column ^ start
    for level in range(bit_count):
        moved = col_move(right, level + bit_count)
        right = jnp.where(right_amount >> level & 1 == 1, moved, right)
    partial_value, ending = walk(left, right, flips, bit_count)
    squared = lax.psum(partial_value.astype(jnp.bfloat16), "layer")
    second_left = align_left(squared, row_index ^ finish, bit_count)
    partial_next, unused = walk(second_left, ending, flips[::-1], bit_count)
    cubed = lax.psum_scatter(
        partial_next.astype(jnp.bfloat16), "layer", scatter_dimension=0, tiled=True
    ).astype(jnp.float32)
    signed = (1.5 * own.astype(jnp.float32) - 0.5 * cubed).astype(jnp.bfloat16)
    return signed[None]


def solution(mesh):
    in_specs = (P("grid", None, None), P("grid", None, None))
    out_specs = P("grid", "layer", None)
    return jax.shard_map(shards, mesh=mesh, in_specs=in_specs, out_specs=out_specs, check_vma=False)
```

profile of v0, /device:TPU:1, one launch (start us, length us, event | category | flops | bytes accessed | tf_op | source)
XLA Modules:
  0.0 429.2 jit_solution(11489509818046499767)
XLA Ops:
  8.5 4.0 collective-permute-start.4
  12.6 6.8 %collective-permute-done.4 = bf16[512,512]{1,0:T(8,128)(2,1)S(1)} collective-permute-done((bf16[512,512]{1,0:T(8,128)(2,1)S(1)}, bf16[512,512]{1,0:T(8,128)(2,1)S(1)}, u32[]{:S(2)}, u32[]{:S(2)}) %collective-permute-start.4) | collective-permute-done | bytes 524320 | tf_op jit(solution)/shard_map/ppermute | solution.py:18
  19.4 8.9 %collective-permute-start.5 = (bf16[512,512]{1,0:T(8,128)(2,1)S(1)}, bf16[512,512]{1,0:T(8,128)(2,1)S(1)}, u32[]{:S(2)}, u32[]{:S(2)}) collective-permute-start(bf16[512,512]{1,0:T(8,128)(2,1)S(1)} %broadcast_select_fusion), channel_id=1, source_target_pairs={{0,64},{64,0},{2,66},{66,2},{4,68},{68,4},{6,70},{70,6},{8,72},{72... | collective-permute-start | bytes 1572872 | tf_op jit(solution)/shard_map/ppermute | solution.py:18
  28.4 22.6 %collective-permute-done.5 = bf16[512,512]{1,0:T(8,128)(2,1)S(1)} collective-permute-done((bf16[512,512]{1,0:T(8,128)(2,1)S(1)}, bf16[512,512]{1,0:T(8,128)(2,1)S(1)}, u32[]{:S(2)}, u32[]{:S(2)}) %collective-permute-start.5) | collective-permute-done | bytes 524320 | tf_op jit(solution)/shard_map/ppermute | solution.py:18
  51.0 3.2 collective-permute-start.6
  54.2 10.7 %collective-permute-done.6 = bf16[512,512]{1,0:T(8,128)(2,1)S(1)} collective-permute-done((bf16[512,512]{1,0:T(8,128)(2,1)S(1)}, bf16[512,512]{1,0:T(8,128)(2,1)S(1)}, u32[]{:S(2)}, u32[]{:S(2)}) %collective-permute-start.6) | collective-permute-done | bytes 524320 | tf_op jit(solution)/shard_map/ppermute | solution.py:18
  64.9 4.7 %collective-permute-start.7 = (bf16[512,512]{1,0:T(8,128)(2,1)S(1)}, bf16[512,512]{1,0:T(8,128)(2,1)S(1)}, u32[]{:S(2)}, u32[]{:S(2)}) collective-permute-start(bf16[512,512]{1,0:T(8,128)(2,1)S(1)} %broadcast_select_fusion.2), channel_id=1, source_target_pairs={{0,256},{256,0},{2,258},{258,2},{4,260},{260,4},{6,262},{262,6},{8... | collective-permute-start | bytes 1572872 | tf_op jit(solution)/shard_map/ppermute | solution.py:18
  69.6 9.8 %collective-permute-done.7 = bf16[512,512]{1,0:T(8,128)(2,1)S(1)} collective-permute-done((bf16[512,512]{1,0:T(8,128)(2,1)S(1)}, bf16[512,512]{1,0:T(8,128)(2,1)S(1)}, u32[]{:S(2)}, u32[]{:S(2)}) %collective-permute-start.7) | collective-permute-done | bytes 524320 | tf_op jit(solution)/shard_map/ppermute | solution.py:18
  80.2 5.4 %collective-permute-start.9 = (bf16[512,512]{1,0:T(8,128)(2,1)S(1)}, bf16[512,512]{1,0:T(8,128)(2,1)S(1)}, u32[]{:S(2)}, u32[]{:S(2)}) collective-permute-start(bf16[512,512]{1,0:T(8,128)(2,1)S(1)} %get-tuple-element.152), channel_id=1, source_target_pairs={{0,32},{32,0},{2,34},{34,2},{4,36},{36,4},{6,38},{38,6},{8,40},{40... | collective-permute-start | bytes 1572872 | tf_op jit(solution)/shard_map/ppermute | solution.py:18
  85.7 4.4 %collective-permute-start = (bf16[128,512]{1,0:T(8,128)(2,1)S(1)}, bf16[128,512]{1,0:T(8,128)(2,1)S(1)}, u32[]{:S(2)}, u32[]{:S(2)}) collective-permute-start(bf16[128,512]{1,0:T(8,128)(2,1)S(1)} %slice.4), channel_id=1, source_target_pairs={{0,2},{2,0},{4,6},{6,4},{8,10},{10,8},{12,14},{14,12},{16,18},{18,... | collective-permute-start | bytes 393224 | tf_op jit(solution)/shard_map/ppermute | solution.py:18
  90.1 5.6 %collective-permute-done.9 = bf16[512,512]{1,0:T(8,128)(2,1)S(1)} collective-permute-done((bf16[512,512]{1,0:T(8,128)(2,1)S(1)}, bf16[512,512]{1,0:T(8,128)(2,1)S(1)}, u32[]{:S(2)}, u32[]{:S(2)}) %collective-permute-start.9) | collective-permute-done | bytes 524320 | tf_op jit(solution)/shard_map/ppermute | solution.py:18
  95.7 5.0 %collective-permute-start.11 = (bf16[512,512]{1,0:T(8,128)(2,1)S(1)}, bf16[512,512]{1,0:T(8,128)(2,1)S(1)}, u32[]{:S(2)}, u32[]{:S(2)}) collective-permute-start(bf16[512,512]{1,0:T(8,128)(2,1)S(1)} %collective-permute-done.9), channel_id=1, source_target_pairs={{0,64},{64,0},{2,66},{66,2},{4,68},{68,4},{6,70},{70,6},{8,72},{72... | collective-permute-start | bytes 1572872 | tf_op jit(solution)/shard_map/ppermute | solution.py:18
  100.8 4.0 collective-permute-start.1
  107.1 5.8 %collective-permute-start.2 = (bf16[128,512]{1,0:T(8,128)(2,1)S(1)}, bf16[128,512]{1,0:T(8,128)(2,1)S(1)}, u32[]{:S(2)}, u32[]{:S(2)}) collective-permute-start(bf16[128,512]{1,0:T(8,128)(2,1)S(1)} %broadcast_select_fusion.5), channel_id=1, source_target_pairs={{0,8},{8,0},{2,10},{10,2},{4,12},{12,4},{6,14},{14,6},{16,24},{24,... | collective-permute-start | bytes 393224 | tf_op jit(solution)/shard_map/ppermute | solution.py:18
  112.9 10.5 %collective-permute-done.11 = bf16[512,512]{1,0:T(8,128)(2,1)S(1)} collective-permute-done((bf16[512,512]{1,0:T(8,128)(2,1)S(1)}, bf16[512,512]{1,0:T(8,128)(2,1)S(1)}, u32[]{:S(2)}, u32[]{:S(2)}) %collective-permute-start.11) | collective-permute-done | bytes 524320 | tf_op jit(solution)/shard_map/ppermute | solution.py:18
  123.4 3.2 collective-permute-start.13
  126.7 10.6 %collective-permute-start.3 = (bf16[128,512]{1,0:T(8,128)(2,1)S(1)}, bf16[128,512]{1,0:T(8,128)(2,1)S(1)}, u32[]{:S(2)}, u32[]{:S(2)}) collective-permute-start(bf16[128,512]{1,0:T(8,128)(2,1)S(1)} %broadcast_select_fusion.6), channel_id=1, source_target_pairs={{0,16},{16,0},{2,18},{18,2},{4,20},{20,4},{6,22},{22,6},{8,24},{24... | collective-permute-start | bytes 393224 | tf_op jit(solution)/shard_map/ppermute | solution.py:18
  137.3 3.1 collective-permute-done.3
  141.1 3.5 collective-permute-start.8
  144.6 3.1 collective-permute-start.15
  147.7 6.0 %collective-permute-start.10 = (bf16[128,512]{1,0:T(8,128)(2,1)S(1)}, bf16[128,512]{1,0:T(8,128)(2,1)S(1)}, u32[]{:S(2)}, u32[]{:S(2)}) collective-permute-start(bf16[128,512]{1,0:T(8,128)(2,1)S(1)} %collective-permute-done.8), channel_id=1, source_target_pairs={{0,4},{4,0},{2,6},{6,2},{8,12},{12,8},{10,14},{14,10},{16,20},{20,... | collective-permute-start | bytes 393224 | tf_op jit(solution)/shard_map/ppermute | solution.py:18
  153.7 3.6 collective-permute-done.10
  157.2 2.8 collective-permute-start.12
  161.0 4.2 collective-permute-start.14
  165.2 6.1 %collective-permute-done.14 = bf16[128,512]{1,0:T(8,128)(2,1)S(1)} collective-permute-done((bf16[128,512]{1,0:T(8,128)(2,1)S(1)}, bf16[128,512]{1,0:T(8,128)(2,1)S(1)}, u32[]{:S(2)}, u32[]{:S(2)}) %collective-permute-start.14) | collective-permute-done | bytes 131104 | tf_op jit(solution)/shard_map/ppermute | solution.py:18
  171.3 3.1 collective-permute-start.16
  181.6 3.3 collective-permute-done.18
  184.9 3.0 collective-permute-start.20
  189.8 5.0 %collective-permute-start.19 = (bf16[512,512]{1,0:T(8,128)(2,1)S(1)}, bf16[512,512]{1,0:T(8,128)(2,1)}, u32[]{:S(2)}, u32[]{:S(2)}) collective-permute-start(bf16[512,512]{1,0:T(8,128)(2,1)S(1)} %collective-permute-done.17), channel_id=1, source_target_pairs={{0,64},{64,0},{2,66},{66,2},{4,68},{68,4},{6,70},{70,6},{8,72},{72... | collective-permute-start | bytes 1572872 | tf_op jit(solution)/shard_map/ppermute | solution.py:18
  202.9 15.3 %collective-permute-done.19 = bf16[512,512]{1,0:T(8,128)(2,1)} collective-permute-done((bf16[512,512]{1,0:T(8,128)(2,1)S(1)}, bf16[512,512]{1,0:T(8,128)(2,1)}, u32[]{:S(2)}, u32[]{:S(2)}) %collective-permute-start.19) | collective-permute-done | bytes 524320 | tf_op jit(solution)/shard_map/ppermute | solution.py:18
  239.5 7.8 %collective-permute-done.27 = bf16[512,512]{1,0:T(8,128)(2,1)S(1)} collective-permute-done((bf16[512,512]{1,0:T(8,128)(2,1)S(1)}, bf16[512,512]{1,0:T(8,128)(2,1)S(1)}, u32[]{:S(2)}, u32[]{:S(2)}) %collective-permute-start.27) | collective-permute-done | bytes 524320 | tf_op jit(solution)/shard_map/ppermute | solution.py:18
  249.2 35.5 %all-reduce.2.cloned.1.call-done = bf16[128,512]{1,0:T(8,128)(2,1)} async-done(((bf16[128,512]{1,0:T(8,128)(2,1)}), bf16[128,512]{1,0:T(8,128)(2,1)}) %all-reduce.2.cloned.1.call-update) | async-done | bytes 131088 | tf_op jit(solution)/shard_map/psum | solution.py:100
  289.3 3.3 collective-permute-start.23
  295.9 4.3 %collective-permute-start.24 = (bf16[128,512]{1,0:T(8,128)(2,1)S(1)}, bf16[128,512]{1,0:T(8,128)(2,1)S(1)}, u32[]{:S(2)}, u32[]{:S(2)}) collective-permute-start(bf16[128,512]{1,0:T(8,128)(2,1)S(1)} %broadcast_select_fusion.9), channel_id=1, source_target_pairs={{0,8},{8,0},{2,10},{10,2},{4,12},{12,4},{6,14},{14,6},{16,24},{24,... | collective-permute-start | bytes 393224 | tf_op jit(solution)/shard_map/ppermute | solution.py:18
  300.2 5.7 %collective-permute-done.24 = bf16[128,512]{1,0:T(8,128)(2,1)S(1)} collective-permute-done((bf16[128,512]{1,0:T(8,128)(2,1)S(1)}, bf16[128,512]{1,0:T(8,128)(2,1)S(1)}, u32[]{:S(2)}, u32[]{:S(2)}) %collective-permute-start.24) | collective-permute-done | bytes 131104 | tf_op jit(solution)/shard_map/ppermute | solution.py:18
  305.9 8.5 %collective-permute-start.25 = (bf16[128,512]{1,0:T(8,128)(2,1)S(1)}, bf16[128,512]{1,0:T(8,128)(2,1)S(1)}, u32[]{:S(2)}, u32[]{:S(2)}) collective-permute-start(bf16[128,512]{1,0:T(8,128)(2,1)S(1)} %broadcast_select_fusion.10), channel_id=1, source_target_pairs={{0,16},{16,0},{2,18},{18,2},{4,20},{20,4},{6,22},{22,6},{8,24},{24... | collective-permute-start | bytes 393224 | tf_op jit(solution)/shard_map/ppermute | solution.py:18
  314.5 3.1 collective-permute-start.33
  318.4 6.0 %collective-permute-start.26 = (bf16[128,512]{1,0:T(8,128)(2,1)S(1)}, bf16[128,512]{1,0:T(8,128)(2,1)S(1)}, u32[]{:S(2)}, u32[]{:S(2)}) collective-permute-start(bf16[128,512]{1,0:T(8,128)(2,1)S(1)} %get-tuple-element.150), channel_id=1, source_target_pairs={{0,2},{2,0},{4,6},{6,4},{8,10},{10,8},{12,14},{14,12},{16,18},{18,... | collective-permute-start | bytes 393224 | tf_op jit(solution)/shard_map/ppermute | solution.py:18
  327.2 4.8 %collective-permute-done.28 = bf16[128,512]{1,0:T(8,128)(2,1)} collective-permute-done((bf16[128,512]{1,0:T(8,128)(2,1)S(1)}, bf16[128,512]{1,0:T(8,128)(2,1)}, u32[]{:S(2)}, u32[]{:S(2)}) %collective-permute-start.28) | collective-permute-done | bytes 131104 | tf_op jit(solution)/shard_map/ppermute | solution.py:18
  332.0 3.1 collective-permute-start.30
  339.4 3.4 collective-permute-start.32
  347.5 3.1 collective-permute-done.32
  350.6 2.6 collective-permute-start.34
  363.6 3.5 collective-permute-done.36
  367.1 2.9 collective-permute-start.38
  374.0 10.1 %collective-permute-done.37 = bf16[512,512]{1,0:T(8,128)(2,1)} collective-permute-done((bf16[512,512]{1,0:T(8,128)(2,1)S(1)}, bf16[512,512]{1,0:T(8,128)(2,1)}, u32[]{:S(2)}, u32[]{:S(2)}) %collective-permute-start.37) | collective-permute-done | bytes 524320 | tf_op jit(solution)/shard_map/ppermute | solution.py:18
  395.8 2.9 collective-permute-done.39
  402.0 18.8 %reduce-scatter.2.cloned.1.call-done = bf16[64,512]{1,0:T(8,128)(2,1)} async-done(((bf16[128,512]{1,0:T(8,128)(2,1)}), bf16[64,512]{1,0:T(8,128)(2,1)}) %reduce-scatter.2.cloned.1.call-update) | async-done | bytes 65552 | tf_op jit(solution)/shard_map/reduce_scatter | solution.py:103
  (184 shorter events, 85.1 us)
Async XLA Ops:
  6.5 278.2 %all-reduce.2.cloned.1.call-start = ((), (), s32[]{:S(2)}) async-start(), calls=%async_computation.1 | async-start | bytes 262144 | tf_op jit(solution)/shard_map/psum | solution.py:100
  8.5 10.8 %collective-permute-start.4 = (bf16[512,512]{1,0:T(8,128)(2,1)S(1)}, bf16[512,512]{1,0:T(8,128)(2,1)S(1)}, u32[]{:S(2)}, u32[]{:S(2)}) collective-permute-start(bf16[512,512]{1,0:T(8,128)(2,1)S(1)} %bitcast_multiply_fusion), channel_id=1, source_target_pairs={{0,32},{32,0},{2,34},{34,2},{4,36},{36,4},{6,38},{38,6},{8,40},{40... | collective-permute-start | bytes 1572872 | tf_op jit(solution)/shard_map/ppermute | solution.py:18
  19.4 31.5 %collective-permute-start.5 = (bf16[512,512]{1,0:T(8,128)(2,1)S(1)}, bf16[512,512]{1,0:T(8,128)(2,1)S(1)}, u32[]{:S(2)}, u32[]{:S(2)}) collective-permute-start(bf16[512,512]{1,0:T(8,128)(2,1)S(1)} %broadcast_select_fusion), channel_id=1, source_target_pairs={{0,64},{64,0},{2,66},{66,2},{4,68},{68,4},{6,70},{70,6},{8,72},{72... | collective-permute-start | bytes 1572872 | tf_op jit(solution)/shard_map/ppermute | solution.py:18
  51.0 13.9 %collective-permute-start.6 = (bf16[512,512]{1,0:T(8,128)(2,1)S(1)}, bf16[512,512]{1,0:T(8,128)(2,1)S(1)}, u32[]{:S(2)}, u32[]{:S(2)}) collective-permute-start(bf16[512,512]{1,0:T(8,128)(2,1)S(1)} %broadcast_select_fusion.1), channel_id=1, source_target_pairs={{0,128},{128,0},{2,130},{130,2},{4,132},{132,4},{6,134},{134,6},{8... | collective-permute-start | bytes 1572872 | tf_op jit(solution)/shard_map/ppermute | solution.py:18
  64.9 14.5 %collective-permute-start.7 = (bf16[512,512]{1,0:T(8,128)(2,1)S(1)}, bf16[512,512]{1,0:T(8,128)(2,1)S(1)}, u32[]{:S(2)}, u32[]{:S(2)}) collective-permute-start(bf16[512,512]{1,0:T(8,128)(2,1)S(1)} %broadcast_select_fusion.2), channel_id=1, source_target_pairs={{0,256},{256,0},{2,258},{258,2},{4,260},{260,4},{6,262},{262,6},{8... | collective-permute-start | bytes 1572872 | tf_op jit(solution)/shard_map/ppermute | solution.py:18
  80.2 15.5 %collective-permute-start.9 = (bf16[512,512]{1,0:T(8,128)(2,1)S(1)}, bf16[512,512]{1,0:T(8,128)(2,1)S(1)}, u32[]{:S(2)}, u32[]{:S(2)}) collective-permute-start(bf16[512,512]{1,0:T(8,128)(2,1)S(1)} %get-tuple-element.152), channel_id=1, source_target_pairs={{0,32},{32,0},{2,34},{34,2},{4,36},{36,4},{6,38},{38,6},{8,40},{40... | collective-permute-start | bytes 1572872 | tf_op jit(solution)/shard_map/ppermute | solution.py:18
  85.7 15.1 %collective-permute-start = (bf16[128,512]{1,0:T(8,128)(2,1)S(1)}, bf16[128,512]{1,0:T(8,128)(2,1)S(1)}, u32[]{:S(2)}, u32[]{:S(2)}) collective-permute-start(bf16[128,512]{1,0:T(8,128)(2,1)S(1)} %slice.4), channel_id=1, source_target_pairs={{0,2},{2,0},{4,6},{6,4},{8,10},{10,8},{12,14},{14,12},{16,18},{18,... | collective-permute-start | bytes 393224 | tf_op jit(solution)/shard_map/ppermute | solution.py:18
  95.7 27.7 %collective-permute-start.11 = (bf16[512,512]{1,0:T(8,128)(2,1)S(1)}, bf16[512,512]{1,0:T(8,128)(2,1)S(1)}, u32[]{:S(2)}, u32[]{:S(2)}) collective-permute-start(bf16[512,512]{1,0:T(8,128)(2,1)S(1)} %collective-permute-done.9), channel_id=1, source_target_pairs={{0,64},{64,0},{2,66},{66,2},{4,68},{68,4},{6,70},{70,6},{8,72},{72... | collective-permute-start | bytes 1572872 | tf_op jit(solution)/shard_map/ppermute | solution.py:18
  100.8 6.4 %collective-permute-start.1 = (bf16[128,512]{1,0:T(8,128)(2,1)S(1)}, bf16[128,512]{1,0:T(8,128)(2,1)S(1)}, u32[]{:S(2)}, u32[]{:S(2)}) collective-permute-start(bf16[128,512]{1,0:T(8,128)(2,1)S(1)} %broadcast_select_fusion.4), channel_id=1, source_target_pairs={{0,4},{4,0},{2,6},{6,2},{8,12},{12,8},{10,14},{14,10},{16,20},{20,... | collective-permute-start | bytes 393224 | tf_op jit(solution)/shard_map/ppermute | solution.py:18
  107.1 19.5 %collective-permute-start.2 = (bf16[128,512]{1,0:T(8,128)(2,1)S(1)}, bf16[128,512]{1,0:T(8,128)(2,1)S(1)}, u32[]{:S(2)}, u32[]{:S(2)}) collective-permute-start(bf16[128,512]{1,0:T(8,128)(2,1)S(1)} %broadcast_select_fusion.5), channel_id=1, source_target_pairs={{0,8},{8,0},{2,10},{10,2},{4,12},{12,4},{6,14},{14,6},{16,24},{24,... | collective-permute-start | bytes 393224 | tf_op jit(solution)/shard_map/ppermute | solution.py:18
  123.4 21.1 %collective-permute-start.13 = (bf16[512,512]{1,0:T(8,128)(2,1)S(1)}, bf16[512,512]{1,0:T(8,128)(2,1)S(1)}, u32[]{:S(2)}, u32[]{:S(2)}) collective-permute-start(bf16[512,512]{1,0:T(8,128)(2,1)S(1)} %collective-permute-done.11), channel_id=1, source_target_pairs={{0,32},{32,0},{2,34},{34,2},{4,36},{36,4},{6,38},{38,6},{8,40},{40... | collective-permute-start | bytes 1572872 | tf_op jit(solution)/shard_map/ppermute | solution.py:18
  126.7 13.7 %collective-permute-start.3 = (bf16[128,512]{1,0:T(8,128)(2,1)S(1)}, bf16[128,512]{1,0:T(8,128)(2,1)S(1)}, u32[]{:S(2)}, u32[]{:S(2)}) collective-permute-start(bf16[128,512]{1,0:T(8,128)(2,1)S(1)} %broadcast_select_fusion.6), channel_id=1, source_target_pairs={{0,16},{16,0},{2,18},{18,2},{4,20},{20,4},{6,22},{22,6},{8,24},{24... | collective-permute-start | bytes 393224 | tf_op jit(solution)/shard_map/ppermute | solution.py:18
  141.1 56.4 %copy-start.1 = (bf16[512,512]{1,0:T(8,128)(2,1)S(1)}, bf16[512,512]{1,0:T(8,128)(2,1)}, u32[]{:S(2)}) copy-start(bf16[512,512]{1,0:T(8,128)(2,1)} %copy-done) | copy-start | bytes 1572868
  141.1 6.6 %collective-permute-start.8 = (bf16[128,512]{1,0:T(8,128)(2,1)S(1)}, bf16[128,512]{1,0:T(8,128)(2,1)S(1)}, u32[]{:S(2)}, u32[]{:S(2)}) collective-permute-start(bf16[128,512]{1,0:T(8,128)(2,1)S(1)} %get-tuple-element.154), channel_id=1, source_target_pairs={{0,2},{2,0},{4,6},{6,4},{8,10},{10,8},{12,14},{14,12},{16,18},{18,... | collective-permute-start | bytes 393224 | tf_op jit(solution)/shard_map/ppermute | solution.py:18
  144.6 29.8 %collective-permute-start.15 = (bf16[512,512]{1,0:T(8,128)(2,1)S(1)}, bf16[512,512]{1,0:T(8,128)(2,1)S(1)}, u32[]{:S(2)}, u32[]{:S(2)}) collective-permute-start(bf16[512,512]{1,0:T(8,128)(2,1)S(1)} %collective-permute-done.13), channel_id=1, source_target_pairs={{0,128},{128,0},{2,130},{130,2},{4,132},{132,4},{6,134},{134,6},{8... | collective-permute-start | bytes 1572872 | tf_op jit(solution)/shard_map/ppermute | solution.py:18
  147.7 47.8 %copy-start.25 = (bf16[128,512]{1,0:T(8,128)(2,1)}, bf16[128,512]{1,0:T(8,128)(2,1)S(1)}, u32[]{:S(2)}) copy-start(bf16[128,512]{1,0:T(8,128)(2,1)S(1)} %collective-permute-done.8) | copy-start | bytes 393220
  147.7 9.5 %collective-permute-start.10 = (bf16[128,512]{1,0:T(8,128)(2,1)S(1)}, bf16[128,512]{1,0:T(8,128)(2,1)S(1)}, u32[]{:S(2)}, u32[]{:S(2)}) collective-permute-start(bf16[128,512]{1,0:T(8,128)(2,1)S(1)} %collective-permute-done.8), channel_id=1, source_target_pairs={{0,4},{4,0},{2,6},{6,2},{8,12},{12,8},{10,14},{14,10},{16,20},{20,... | collective-permute-start | bytes 393224 | tf_op jit(solution)/shard_map/ppermute | solution.py:18
  157.2 21.0 %copy-start.21 = (bf16[128,512]{1,0:T(8,128)(2,1)}, bf16[128,512]{1,0:T(8,128)(2,1)S(1)}, u32[]{:S(2)}) copy-start(bf16[128,512]{1,0:T(8,128)(2,1)S(1)} %collective-permute-done.10) | copy-start | bytes 393220
  157.2 3.7 collective-permute-start.12
  161.0 19.2 %copy-start.17 = (bf16[128,512]{1,0:T(8,128)(2,1)}, bf16[128,512]{1,0:T(8,128)(2,1)S(1)}, u32[]{:S(2)}) copy-start(bf16[128,512]{1,0:T(8,128)(2,1)S(1)} %collective-permute-done.12) | copy-start | bytes 393220
  161.0 10.3 %collective-permute-start.14 = (bf16[128,512]{1,0:T(8,128)(2,1)S(1)}, bf16[128,512]{1,0:T(8,128)(2,1)S(1)}, u32[]{:S(2)}, u32[]{:S(2)}) collective-permute-start(bf16[128,512]{1,0:T(8,128)(2,1)S(1)} %collective-permute-done.12), channel_id=1, source_target_pairs={{0,8},{8,0},{2,10},{10,2},{4,12},{12,4},{6,14},{14,6},{16,24},{24,... | collective-permute-start | bytes 393224 | tf_op jit(solution)/shard_map/ppermute | solution.py:18
  171.3 7.0 %collective-permute-start.16 = (bf16[128,512]{1,0:T(8,128)(2,1)S(1)}, bf16[128,512]{1,0:T(8,128)(2,1)S(1)}, u32[]{:S(2)}, u32[]{:S(2)}) collective-permute-start(bf16[128,512]{1,0:T(8,128)(2,1)S(1)} %collective-permute-done.14), channel_id=1, source_target_pairs={{0,2},{2,0},{4,6},{6,4},{8,10},{10,8},{12,14},{14,12},{16,18},{18,... | collective-permute-start | bytes 393224 | tf_op jit(solution)/shard_map/ppermute | solution.py:18
  174.4 15.4 %collective-permute-start.17 = (bf16[512,512]{1,0:T(8,128)(2,1)S(1)}, bf16[512,512]{1,0:T(8,128)(2,1)S(1)}, u32[]{:S(2)}, u32[]{:S(2)}) collective-permute-start(bf16[512,512]{1,0:T(8,128)(2,1)S(1)} %collective-permute-done.15), channel_id=1, source_target_pairs={{0,32},{32,0},{2,34},{34,2},{4,36},{36,4},{6,38},{38,6},{8,40},{40... | collective-permute-start | bytes 1572872 | tf_op jit(solution)/shard_map/ppermute | solution.py:18
  178.3 6.6 %collective-permute-start.18 = (bf16[128,512]{1,0:T(8,128)(2,1)S(1)}, bf16[128,512]{1,0:T(8,128)(2,1)S(1)}, u32[]{:S(2)}, u32[]{:S(2)}) collective-permute-start(bf16[128,512]{1,0:T(8,128)(2,1)S(1)} %collective-permute-done.16), channel_id=1, source_target_pairs={{0,4},{4,0},{2,6},{6,2},{8,12},{12,8},{10,14},{14,10},{16,20},{20,... | collective-permute-start | bytes 393224 | tf_op jit(solution)/shard_map/ppermute | solution.py:18
  184.9 10.6 %collective-permute-start.20 = (bf16[128,512]{1,0:T(8,128)(2,1)S(1)}, bf16[128,512]{1,0:T(8,128)(2,1)S(1)}, u32[]{:S(2)}, u32[]{:S(2)}) collective-permute-start(bf16[128,512]{1,0:T(8,128)(2,1)S(1)} %collective-permute-done.18), channel_id=1, source_target_pairs={{0,2},{2,0},{4,6},{6,4},{8,10},{10,8},{12,14},{14,12},{16,18},{18,... | collective-permute-start | bytes 393224 | tf_op jit(solution)/shard_map/ppermute | solution.py:18
  189.8 28.4 %collective-permute-start.19 = (bf16[512,512]{1,0:T(8,128)(2,1)S(1)}, bf16[512,512]{1,0:T(8,128)(2,1)}, u32[]{:S(2)}, u32[]{:S(2)}) collective-permute-start(bf16[512,512]{1,0:T(8,128)(2,1)S(1)} %collective-permute-done.17), channel_id=1, source_target_pairs={{0,64},{64,0},{2,66},{66,2},{4,68},{68,4},{6,70},{70,6},{8,72},{72... | collective-permute-start | bytes 1572872 | tf_op jit(solution)/shard_map/ppermute | solution.py:18
  202.9 19.2 %copy-start.18 = (bf16[128,512]{1,0:T(8,128)(2,1)S(1)}, bf16[128,512]{1,0:T(8,128)(2,1)}, u32[]{:S(2)}) copy-start(bf16[128,512]{1,0:T(8,128)(2,1)} %copy-done.17) | copy-start | bytes 393220
  218.2 15.1 %collective-permute-start.21 = (bf16[512,512]{1,0:T(8,128)(2,1)}, bf16[512,512]{1,0:T(8,128)(2,1)S(1)}, u32[]{:S(2)}, u32[]{:S(2)}) collective-permute-start(bf16[512,512]{1,0:T(8,128)(2,1)} %collective-permute-done.19), channel_id=1, source_target_pairs={{0,32},{32,0},{2,34},{34,2},{4,36},{36,4},{6,38},{38,6},{8,40},{40... | collective-permute-start | bytes 1572872 | tf_op jit(solution)/shard_map/ppermute | solution.py:18
  233.3 14.0 %collective-permute-start.27 = (bf16[512,512]{1,0:T(8,128)(2,1)S(1)}, bf16[512,512]{1,0:T(8,128)(2,1)S(1)}, u32[]{:S(2)}, u32[]{:S(2)}) collective-permute-start(bf16[512,512]{1,0:T(8,128)(2,1)S(1)} %collective-permute-done.21), channel_id=1, source_target_pairs={{0,32},{32,0},{2,34},{34,2},{4,36},{36,4},{6,38},{38,6},{8,40},{40... | collective-permute-start | bytes 1572872 | tf_op jit(solution)/shard_map/ppermute | solution.py:18
  239.5 181.4 %reduce-scatter.2.cloned.1.call-start = ((), (), s32[]{:S(2)}) async-start(), calls=%async_computation.2 | async-start | bytes 196608 | tf_op jit(solution)/shard_map/reduce_scatter | solution.py:103
  247.3 45.2 %collective-permute-start.29 = (bf16[512,512]{1,0:T(8,128)(2,1)S(1)}, bf16[512,512]{1,0:T(8,128)(2,1)S(1)}, u32[]{:S(2)}, u32[]{:S(2)}) collective-permute-start(bf16[512,512]{1,0:T(8,128)(2,1)S(1)} %collective-permute-done.27), channel_id=1, source_target_pairs={{0,64},{64,0},{2,66},{66,2},{4,68},{68,4},{6,70},{70,6},{8,72},{72... | collective-permute-start | bytes 1572872 | tf_op jit(solution)/shard_map/ppermute | solution.py:18
  284.7 3.6 collective-permute-start.22
  289.3 6.6 %collective-permute-start.23 = (bf16[128,512]{1,0:T(8,128)(2,1)S(1)}, bf16[128,512]{1,0:T(8,128)(2,1)S(1)}, u32[]{:S(2)}, u32[]{:S(2)}) collective-permute-start(bf16[128,512]{1,0:T(8,128)(2,1)S(1)} %broadcast_select_fusion.8), channel_id=1, source_target_pairs={{0,4},{4,0},{2,6},{6,2},{8,12},{12,8},{10,14},{14,10},{16,20},{20,... | collective-permute-start | bytes 393224 | tf_op jit(solution)/shard_map/ppermute | solution.py:18
  292.5 21.9 %collective-permute-start.31 = (bf16[512,512]{1,0:T(8,128)(2,1)S(1)}, bf16[512,512]{1,0:T(8,128)(2,1)S(1)}, u32[]{:S(2)}, u32[]{:S(2)}) collective-permute-start(bf16[512,512]{1,0:T(8,128)(2,1)S(1)} %collective-permute-done.29), channel_id=1, source_target_pairs={{0,32},{32,0},{2,34},{34,2},{4,36},{36,4},{6,38},{38,6},{8,40},{40... | collective-permute-start | bytes 1572872 | tf_op jit(solution)/shard_map/ppermute | solution.py:18
  295.9 10.0 %collective-permute-start.24 = (bf16[128,512]{1,0:T(8,128)(2,1)S(1)}, bf16[128,512]{1,0:T(8,128)(2,1)S(1)}, u32[]{:S(2)}, u32[]{:S(2)}) collective-permute-start(bf16[128,512]{1,0:T(8,128)(2,1)S(1)} %broadcast_select_fusion.9), channel_id=1, source_target_pairs={{0,8},{8,0},{2,10},{10,2},{4,12},{12,4},{6,14},{14,6},{16,24},{24,... | collective-permute-start | bytes 393224 | tf_op jit(solution)/shard_map/ppermute | solution.py:18
  305.9 11.7 %collective-permute-start.25 = (bf16[128,512]{1,0:T(8,128)(2,1)S(1)}, bf16[128,512]{1,0:T(8,128)(2,1)S(1)}, u32[]{:S(2)}, u32[]{:S(2)}) collective-permute-start(bf16[128,512]{1,0:T(8,128)(2,1)S(1)} %broadcast_select_fusion.10), channel_id=1, source_target_pairs={{0,16},{16,0},{2,18},{18,2},{4,20},{20,4},{6,22},{22,6},{8,24},{24... | collective-permute-start | bytes 393224 | tf_op jit(solution)/shard_map/ppermute | solution.py:18
  314.5 20.7 %collective-permute-start.33 = (bf16[512,512]{1,0:T(8,128)(2,1)S(1)}, bf16[512,512]{1,0:T(8,128)(2,1)S(1)}, u32[]{:S(2)}, u32[]{:S(2)}) collective-permute-start(bf16[512,512]{1,0:T(8,128)(2,1)S(1)} %collective-permute-done.31), channel_id=1, source_target_pairs={{0,128},{128,0},{2,130},{130,2},{4,132},{132,4},{6,134},{134,6},{8... | collective-permute-start | bytes 1572872 | tf_op jit(solution)/shard_map/ppermute | solution.py:18
  318.4 6.9 %collective-permute-start.26 = (bf16[128,512]{1,0:T(8,128)(2,1)S(1)}, bf16[128,512]{1,0:T(8,128)(2,1)S(1)}, u32[]{:S(2)}, u32[]{:S(2)}) collective-permute-start(bf16[128,512]{1,0:T(8,128)(2,1)S(1)} %get-tuple-element.150), channel_id=1, source_target_pairs={{0,2},{2,0},{4,6},{6,4},{8,10},{10,8},{12,14},{14,12},{16,18},{18,... | collective-permute-start | bytes 393224 | tf_op jit(solution)/shard_map/ppermute | solution.py:18
  325.3 6.7 %collective-permute-start.28 = (bf16[128,512]{1,0:T(8,128)(2,1)S(1)}, bf16[128,512]{1,0:T(8,128)(2,1)}, u32[]{:S(2)}, u32[]{:S(2)}) collective-permute-start(bf16[128,512]{1,0:T(8,128)(2,1)S(1)} %collective-permute-done.26), channel_id=1, source_target_pairs={{0,4},{4,0},{2,6},{6,2},{8,12},{12,8},{10,14},{14,10},{16,20},{20,... | collective-permute-start | bytes 393224 | tf_op jit(solution)/shard_map/ppermute | solution.py:18
  332.0 7.4 %collective-permute-start.30 = (bf16[128,512]{1,0:T(8,128)(2,1)}, bf16[128,512]{1,0:T(8,128)(2,1)}, u32[]{:S(2)}, u32[]{:S(2)}) collective-permute-start(bf16[128,512]{1,0:T(8,128)(2,1)} %collective-permute-done.28), channel_id=1, source_target_pairs={{0,2},{2,0},{4,6},{6,4},{8,10},{10,8},{12,14},{14,12},{16,18},{18,... | collective-permute-start | bytes 393224 | tf_op jit(solution)/shard_map/ppermute | solution.py:18
  335.1 21.3 %collective-permute-start.35 = (bf16[512,512]{1,0:T(8,128)(2,1)S(1)}, bf16[512,512]{1,0:T(8,128)(2,1)S(1)}, u32[]{:S(2)}, u32[]{:S(2)}) collective-permute-start(bf16[512,512]{1,0:T(8,128)(2,1)S(1)} %collective-permute-done.33), channel_id=1, source_target_pairs={{0,32},{32,0},{2,34},{34,2},{4,36},{36,4},{6,38},{38,6},{8,40},{40... | collective-permute-start | bytes 1572872 | tf_op jit(solution)/shard_map/ppermute | solution.py:18
  339.4 11.1 %collective-permute-start.32 = (bf16[128,512]{1,0:T(8,128)(2,1)}, bf16[128,512]{1,0:T(8,128)(2,1)S(1)}, u32[]{:S(2)}, u32[]{:S(2)}) collective-permute-start(bf16[128,512]{1,0:T(8,128)(2,1)} %collective-permute-done.30), channel_id=1, source_target_pairs={{0,8},{8,0},{2,10},{10,2},{4,12},{12,4},{6,14},{14,6},{16,24},{24,... | collective-permute-start | bytes 393224 | tf_op jit(solution)/shard_map/ppermute | solution.py:18
  350.6 9.7 %collective-permute-start.34 = (bf16[128,512]{1,0:T(8,128)(2,1)S(1)}, bf16[128,512]{1,0:T(8,128)(2,1)S(1)}, u32[]{:S(2)}, u32[]{:S(2)}) collective-permute-start(bf16[128,512]{1,0:T(8,128)(2,1)S(1)} %collective-permute-done.32), channel_id=1, source_target_pairs={{0,2},{2,0},{4,6},{6,4},{8,10},{10,8},{12,14},{14,12},{16,18},{18,... | collective-permute-start | bytes 393224 | tf_op jit(solution)/shard_map/ppermute | solution.py:18
  356.5 27.6 %collective-permute-start.37 = (bf16[512,512]{1,0:T(8,128)(2,1)S(1)}, bf16[512,512]{1,0:T(8,128)(2,1)}, u32[]{:S(2)}, u32[]{:S(2)}) collective-permute-start(bf16[512,512]{1,0:T(8,128)(2,1)S(1)} %collective-permute-done.35), channel_id=1, source_target_pairs={{0,64},{64,0},{2,66},{66,2},{4,68},{68,4},{6,70},{70,6},{8,72},{72... | collective-permute-start | bytes 1572872 | tf_op jit(solution)/shard_map/ppermute | solution.py:18
  360.3 6.7 %collective-permute-start.36 = (bf16[128,512]{1,0:T(8,128)(2,1)S(1)}, bf16[128,512]{1,0:T(8,128)(2,1)S(1)}, u32[]{:S(2)}, u32[]{:S(2)}) collective-permute-start(bf16[128,512]{1,0:T(8,128)(2,1)S(1)} %collective-permute-done.34), channel_id=1, source_target_pairs={{0,4},{4,0},{2,6},{6,2},{8,12},{12,8},{10,14},{14,10},{16,20},{20,... | collective-permute-start | bytes 393224 | tf_op jit(solution)/shard_map/ppermute | solution.py:18
  367.1 18.9 %collective-permute-start.38 = (bf16[128,512]{1,0:T(8,128)(2,1)S(1)}, bf16[128,512]{1,0:T(8,128)(2,1)S(1)}, u32[]{:S(2)}, u32[]{:S(2)}) collective-permute-start(bf16[128,512]{1,0:T(8,128)(2,1)S(1)} %collective-permute-done.36), channel_id=1, source_target_pairs={{0,2},{2,0},{4,6},{6,4},{8,10},{10,8},{12,14},{14,12},{16,18},{18,... | collective-permute-start | bytes 393224 | tf_op jit(solution)/shard_map/ppermute | solution.py:18
  384.1 14.7 %collective-permute-start.39 = (bf16[512,512]{1,0:T(8,128)(2,1)}, bf16[512,512]{1,0:T(8,128)(2,1)S(1)}, u32[]{:S(2)}, u32[]{:S(2)}) collective-permute-start(bf16[512,512]{1,0:T(8,128)(2,1)} %collective-permute-done.37), channel_id=1, source_target_pairs={{0,32},{32,0},{2,34},{34,2},{4,36},{36,4},{6,38},{38,6},{8,40},{40... | collective-permute-start | bytes 1572872 | tf_op jit(solution)/shard_map/ppermute | solution.py:18
  402.0 18.9 %copy-start.32 = (bf16[128,512]{1,0:T(8,128)(2,1)S(1)}, bf16[128,512]{1,0:T(8,128)(2,1)}, u32[]{:S(2)}) copy-start(bf16[128,512]{1,0:T(8,128)(2,1)} %copy-done.31) | copy-start | bytes 393220
  (27 other events, 120.3 us)
Sparse Core Ops, SparseCore 0:
  239.6 45.0 all-reduce.1
  402.2 18.6 reduce-scatter.1
where the time goes:
time: 431 us; the launch traced here: 429 us
  waiting for transfers between devices  199 us (46%)
  starting transfers between devices  152 us (35%)
  between operations  34.7 us (8%)
  other arithmetic  32.9 us (8%)
  matrix products  7.29 us (2%)
    ppermute x40, starting transfers between devices, from_partner(): return lax.ppermute(block, axis, route)  152 us
    ppermute x40, waiting for transfers between devices, from_partner(): return lax.ppermute(block, axis, route)  145 us
    psum x1, waiting for transfers between devices, shards(): squared = lax.psum(partial_value.astype(jnp.bfloat16), 'layer')  35.5 us
    reduce_or x31, other arithmetic, tile_product(): occupied = jnp.any(left != 0) & jnp.any(right != 0)  27.8 us
    reduce_scatter x1, waiting for transfers between devices, shards(): lax.psum_scatter(partial_next.astype(jnp.bfloat16), 'layer', scatter_dime...  18.8 us
  transfers between devices with their start and end apart: 42, of which 28 were waited for; matrix products, arithmetic and copies ran while one was open for 8% of the time, Pallas kernels for 0%

commit v1 on v0

v1 whole, which is shorter than its diff:
```python
import jax
import jax.numpy as jnp
from jax import lax
from jax.sharding import Mesh, PartitionSpec as P

SIZES = {"x": 4, "y": 4, "z": 8, "c": 2, "l": 2}


def exchange(blocks, axis):
    return lax.all_to_all(blocks, axis, 0, 0, tiled=True)


def gather(block, axis):
    count = lax.axis_size(axis)
    return exchange(jnp.broadcast_to(block[None], (count,) + block.shape), axis)


def scatter_sum(blocks, axis):
    return jnp.sum(exchange(blocks, axis).astype(jnp.float32), axis=0)


def shards(x_tiles, pattern):
    half = jnp.bfloat16
    width = x_tiles.shape[1]
    slab = width // 4
    share = slab // 4
    blocks = pattern.shape[1]
    span = width // blocks
    nx, ny, nz = (lax.axis_size(a) for a in "xyz")
    core = lax.axis_index("c")
    layer = lax.axis_index("l")
    mask = jnp.broadcast_to(pattern[0][:, None, :, None], (blocks, span, blocks, span))
    tile = x_tiles[0] * mask.reshape(width, width).astype(half)
    other = lax.ppermute(tile, "c", [(0, 1), (1, 0)])
    pair = jnp.concatenate(
        [jnp.where(core == 0, tile, other), jnp.where(core == 0, other, tile)], axis=1
    )
    own = lax.dynamic_slice_in_dim(pair, (layer * 2 + core) * share, share, 0)
    rows = gather(gather(own, "y"), "x").reshape(nx * ny * share, 2 * width)
    partial = lax.dot_general(
        rows, pair, (((1,), (1,)), ((), ())), preferred_element_type=jnp.float32
    ).astype(half)
    squared = scatter_sum(partial.reshape(nz, -1, width), "z").astype(half)
    squared = gather(squared, "z").reshape(nx * ny * share, width)
    partial = jnp.dot(squared, pair, preferred_element_type=jnp.float32).astype(half)
    partial = scatter_sum(partial.reshape(nx, ny * share, 2 * width), "x").astype(half)
    cubed = scatter_sum(partial.reshape(ny, share, 2 * width), "y")
    signed = (1.5 * own.astype(jnp.float32) - 0.5 * cubed).astype(half)
    mine = jnp.where(core == 0, signed[:, :width], signed[:, width:])
    theirs = jnp.where(core == 0, signed[:, width:], signed[:, :width])
    back = lax.ppermute(theirs, "c", [(0, 1), (1, 0)])
    out = jnp.concatenate(
        [jnp.where(core == 0, mine, back), jnp.where(core == 0, back, mine)], axis=0
    )
    return out[None]


def solution(mesh, sizes=SIZES):
    fine = Mesh(mesh.devices.reshape(tuple(sizes.values())), tuple(sizes))
    grid = ("x", "y", "z", "c")
    specs = (P(grid, None, None), P(grid, None, None))
    return jax.shard_map(
        shards, mesh=fine, in_specs=specs, out_specs=P(grid, "l", None), check_vma=False
    )
```

time: 431 us -> 112 us (0.26)
  waiting for transfers between devices: 199 us -> 2.34 us
  starting transfers between devices: 152 us -> 18.3 us
  blocking collectives: 0 us -> 86.4 us
  between operations: 34.7 us -> 0.13 us
  other arithmetic: 32.9 us -> 1.82 us
  matrix products: 7.29 us -> 1.45 us
    ppermute x40 -> x2, waiting for transfers between devices: 145 us -> 2.34 us  [the longest x1 1.51 us: shards(): other = lax.ppermute(tile, 'c', [(0, 1), (1, 0)])]
    ppermute x40 -> x2, starting transfers between devices: 152 us -> 18.3 us  [the longest x1 9.52 us: shards(): back = lax.ppermute(theirs, 'c', [(0, 1), (1, 0)])]
    all_to_all x0 -> x6, blocking collectives: none -> 86.4 us  [exchange(): return lax.all_to_all(blocks, axis, 0, 0, tiled=True)]
    psum x1 -> x0, waiting for transfers between devices: 35.5 us -> none  [shards(): squared = lax.psum(partial_value.astype(jnp.bfloat16), 'layer')]
    reduce_or x31 -> x0, other arithmetic: 27.8 us -> none  [tile_product(): occupied = jnp.any(left != 0) & jnp.any(right != 0)]
    reduce_scatter x1 -> x0, waiting for transfers between devices: 18.8 us -> none  [shards(): lax.psum_scatter(partial_next.astype(jnp.bfloat16), 'layer', scatter_dime...]
    dot_general x15 -> x2, matrix products: 7.29 us -> 1.45 us  [the longest x1 0.74 us: shards(): lax.dot_general(rows, pair, (((1,), (1,)), ((), ())), preferred_element_t...]
  transfers between devices with their start and end apart: 42 -> 2, of which waited for: 28 -> 2; matrix products, arithmetic and copies ran while one was open for 8% -> 0% of each run, Pallas kernels for 0% -> 0%
where the time goes in v1:
time: 112 us
  blocking collectives  86.4 us (77%)
  starting transfers between devices  18.3 us (16%)
  waiting for transfers between devices  2.34 us (2%)
  other arithmetic  1.82 us (2%)
  matrix products  1.45 us (1%)
  local copies, waits for them, and re-layouts  1.41 us (1%)
    all_to_all x6, blocking collectives, exchange(): return lax.all_to_all(blocks, axis, 0, 0, tiled=True)  86.4 us
    ppermute x1, starting transfers between devices, shards(): back = lax.ppermute(theirs, 'c', [(0, 1), (1, 0)])  9.52 us
    ppermute x1, starting transfers between devices, shards(): other = lax.ppermute(tile, 'c', [(0, 1), (1, 0)])  8.75 us
  transfers between devices with their start and end apart: 2, of which 2 were waited for; matrix products, arithmetic and copies ran while one was open for 0% of the time, Pallas kernels for 0%

profile of v1, /device:TPU:1, one launch (start us, length us, event | category | flops | bytes accessed | tf_op | source)
XLA Modules:
  0.0 111.8 jit_solution(8545561991606454629)
XLA Ops:
  0.0 0.7 convert_bitcast_fusion
  0.7 0.2 broadcast_in_dim.10
  0.9 0.0 copy-start
  0.9 0.6 convert_element_type.31
  1.5 0.4 copy-done
  1.9 0.1 bitcast_multiply_fusion
  2.0 8.7 %collective-permute-start = (bf16[512,512]{1,0:T(8,128)(2,1)S(1)}, bf16[512,512]{1,0:T(8,128)(2,1)S(1)}, u32[]{:S(2)}, u32[]{:S(2)}) collective-permute-start(bf16[512,512]{1,0:T(8,128)(2,1)S(1)} %bitcast_multiply_fusion), channel_id=1, source_target_pairs={{0,2},{2,0},{1,3},{3,1},{4,6},{6,4},{5,7},{7,5},{8,10},{10,8},{9,1... | collective-permute-start | bytes 1572872 | tf_op jit(solution)/shard_map/ppermute | solution.py:34
  10.8 1.5 %collective-permute-done = bf16[512,512]{1,0:T(8,128)(2,1)S(1)} collective-permute-done((bf16[512,512]{1,0:T(8,128)(2,1)S(1)}, bf16[512,512]{1,0:T(8,128)(2,1)S(1)}, u32[]{:S(2)}, u32[]{:S(2)}) %collective-permute-start) | collective-permute-done | bytes 524320 | tf_op jit(solution)/shard_map/ppermute | solution.py:34
  12.3 0.1 broadcast_select_fusion
  12.4 10.6 %all_to_all.30 = bf16[4,32,1024]{2,1,0:T(8,128)(2,1)S(1)} all-to-all(bf16[4,32,1024]{2,1,0:T(8,128)(2,1)S(1)} %broadcast_in_dim.11), channel_id=1, replica_groups=mesh['x'=4,'y'=4,'z'=8,'c'=2,'l'=2] {'y'}, dimensions={0} | all-to-all | bytes 524288 | tf_op jit(solution)/shard_map/all_to_all | solution.py:10
  23.0 0.1 broadcast_in_dim.12
  23.2 15.9 %all_to_all.31 = bf16[4,4,32,1024]{3,2,1,0:T(8,128)(2,1)S(1)} all-to-all(bf16[4,4,32,1024]{3,2,1,0:T(8,128)(2,1)S(1)} %broadcast_in_dim.12), channel_id=1, replica_groups=mesh['x'=4,'y'=4,'z'=8,'c'=2,'l'=2] {'x'}, dimensions={0} | all-to-all | bytes 2097152 | tf_op jit(solution)/shard_map/all_to_all | solution.py:10
  39.1 0.7 convolution_convert_fusion.1
  39.8 18.4 %all_to_all.32 = bf16[8,64,512]{2,1,0:T(8,128)(2,1)S(1)} all-to-all(bf16[8,64,512]{2,1,0:T(8,128)(2,1)S(1)} %bitcast.19), channel_id=1, replica_groups=mesh['x'=4,'y'=4,'z'=8,'c'=2,'l'=2] {'z'}, dimensions={0} | all-to-all | bytes 1048576 | tf_op jit(solution)/shard_map/all_to_all | solution.py:10
  58.2 0.1 reduce_sum.33
  58.3 15.5 %all_to_all.33 = bf16[8,64,512]{2,1,0:T(8,128)(2,1)S(1)} all-to-all(bf16[8,64,512]{2,1,0:T(8,128)(2,1)S(1)} %broadcast_in_dim.13), channel_id=1, replica_groups=mesh['x'=4,'y'=4,'z'=8,'c'=2,'l'=2] {'z'}, dimensions={0} | all-to-all | bytes 1048576 | tf_op jit(solution)/shard_map/all_to_all | solution.py:10
  73.8 0.7 convolution_convert_fusion
  74.6 12.2 %all_to_all.34 = bf16[4,128,1024]{2,1,0:T(8,128)(2,1)S(1)} all-to-all(bf16[4,128,1024]{2,1,0:T(8,128)(2,1)S(1)} %bitcast.16), channel_id=1, replica_groups=mesh['x'=4,'y'=4,'z'=8,'c'=2,'l'=2] {'x'}, dimensions={0} | all-to-all | bytes 2097152 | tf_op jit(solution)/shard_map/all_to_all | solution.py:10
  86.7 0.2 reduce_sum.34
  86.9 13.8 %all_to_all.35 = bf16[4,32,1024]{2,1,0:T(8,128)(2,1)S(1)} all-to-all(bf16[4,32,1024]{2,1,0:T(8,128)(2,1)S(1)} %bitcast.15), channel_id=1, replica_groups=mesh['x'=4,'y'=4,'z'=8,'c'=2,'l'=2] {'y'}, dimensions={0} | all-to-all | bytes 524288 | tf_op jit(solution)/shard_map/all_to_all | solution.py:10
  100.8 9.5 %collective-permute-start.1 = (bf16[32,512]{1,0:T(8,128)(2,1)S(1)}, bf16[32,512]{1,0:T(8,128)(2,1)S(1)}, u32[]{:S(2)}, u32[]{:S(2)}) collective-permute-start(bf16[32,512]{1,0:T(8,128)(2,1)S(1)} %broadcast_select_fusion.4), channel_id=1, source_target_pairs={{0,2},{2,0},{1,3},{3,1},{4,6},{6,4},{5,7},{7,5},{8,10},{10,8},{9,1... | collective-permute-start | bytes 98312 | tf_op jit(solution)/shard_map/ppermute | solution.py:51
  110.4 0.8 collective-permute-done.1
  111.2 0.6 maximum_bitcast_fusion
  (7 shorter events, 0.2 us)
Async XLA Ops:
  0.9 1.0 copy-start
  2.0 10.3 %collective-permute-start = (bf16[512,512]{1,0:T(8,128)(2,1)S(1)}, bf16[512,512]{1,0:T(8,128)(2,1)S(1)}, u32[]{:S(2)}, u32[]{:S(2)}) collective-permute-start(bf16[512,512]{1,0:T(8,128)(2,1)S(1)} %bitcast_multiply_fusion), channel_id=1, source_target_pairs={{0,2},{2,0},{1,3},{3,1},{4,6},{6,4},{5,7},{7,5},{8,10},{10,8},{9,1... | collective-permute-start | bytes 1572872 | tf_op jit(solution)/shard_map/ppermute | solution.py:34
  100.8 10.4 %collective-permute-start.1 = (bf16[32,512]{1,0:T(8,128)(2,1)S(1)}, bf16[32,512]{1,0:T(8,128)(2,1)S(1)}, u32[]{:S(2)}, u32[]{:S(2)}) collective-permute-start(bf16[32,512]{1,0:T(8,128)(2,1)S(1)} %broadcast_select_fusion.4), channel_id=1, source_target_pairs={{0,2},{2,0},{1,3},{3,1},{4,6},{6,4},{5,7},{7,5},{8,10},{10,8},{9,1... | collective-permute-start | bytes 98312 | tf_op jit(solution)/shard_map/ppermute | solution.py:51

commit v2 on v1

v2 whole, which is shorter than its diff:
```python
import jax
import jax.numpy as jnp
from jax import lax
from jax.sharding import Mesh, PartitionSpec as P


SIZES = {"x": 4, "h": 2, "p": 2, "z": 8, "c": 2, "l": 2}
NEAR = ("h", "p", "c")
SWAP = ((0, 1), (1, 0))


def exchange(blocks, axis):
    return lax.all_to_all(blocks, axis, 0, 0, tiled=True)


def gather(block, axis):
    count = lax.axis_size(axis)
    return exchange(jnp.broadcast_to(block[None], (count,) + block.shape), axis)


def total(blocks):
    return jnp.sum(blocks.astype(jnp.float32), axis=0)


def masked(tile, pattern):
    width, blocks = tile.shape[0], pattern.shape[0]
    span = width // blocks
    mask = jnp.broadcast_to(pattern[:, None, :, None], (blocks, span, blocks, span))
    return tile * mask.reshape(width, width).astype(tile.dtype)


def step(x_tiles, pattern):
    half = jnp.bfloat16
    width = x_tiles.shape[1]
    share = width // 32
    nx, nz = lax.axis_size("x"), lax.axis_size("z")
    first = lax.axis_index("c") == 0
    tile = masked(x_tiles[0], pattern[0])
    below = lax.ppermute(tile, "p", SWAP)
    beside = lax.ppermute(tile, "c", SWAP)
    corner = lax.ppermute(below, "c", SWAP)
    own = lax.dynamic_slice_in_dim(tile, lax.axis_index("l") * 4 * share, 4 * share, 0)

    parts = jnp.broadcast_to(own.reshape(1, 4, share, width), (2, 4, share, width))
    parts = exchange(parts.reshape(8, share, width), NEAR).reshape(4, 2, share, width)
    left, right = parts[:, 0], parts[:, 1]
    rows = jnp.concatenate(
        [jnp.where(first, left, right), jnp.where(first, right, left)], axis=2
    )
    rows = gather(rows, "x").reshape(-1, 2 * width)

    block = jnp.concatenate(
        [
            jnp.concatenate([tile, beside], axis=1),
            jnp.concatenate([below, corner], axis=1),
        ],
        axis=0,
    )
    partial = lax.dot_general(
        rows, block, (((1,), (1,)), ((), ())), preferred_element_type=jnp.float32
    ).astype(half)
    squared = total(exchange(partial.reshape(nz, -1, 2 * width), "z")).astype(half)
    squared = gather(squared, "z").reshape(-1, 2 * width)
    partial = jnp.dot(squared, block, preferred_element_type=jnp.float32).astype(half)
    partial = total(exchange(partial.reshape(nx, -1, 2 * width), "x")).astype(half)
    partial = partial.reshape(4, share, 2 * width)
    left, right = partial[:, :, :width], partial[:, :, width:]
    parts = jnp.stack(
        [jnp.where(first, left, right), jnp.where(first, right, left)], axis=1
    )
    parts = exchange(parts.reshape(8, share, width), NEAR)
    cubed = total(parts.reshape(2, 4 * share, width))
    signed = 1.5 * own.astype(jnp.float32) - 0.5 * cubed
    return signed.astype(half)[None]


def solution(mesh, sizes=SIZES):
    fine = Mesh(mesh.devices.reshape(tuple(sizes.values())), tuple(sizes))
    grid = ("x", "h", "p", "z", "c")
    specs = (P(grid, None, None), P(grid, None, None))
    return jax.shard_map(
        step, mesh=fine, in_specs=specs, out_specs=P(grid, "l", None), check_vma=False
    )
```

time: 112 us -> 108 us (0.964)
  blocking collectives: 86.4 us -> 66 us
  waiting for transfers between devices: 2.34 us -> 14.3 us
  starting transfers between devices: 18.3 us -> 21 us
  local copies, waits for them, and re-layouts: 1.41 us -> 2.8 us
    all_to_all x6 -> x4, blocking collectives: 86.4 us -> 66 us  [exchange(): return lax.all_to_all(blocks, axis, 0, 0, tiled=True)]
    all_to_all x0 -> x2, waiting for transfers between devices: none -> 14.3 us  [exchange(): return lax.all_to_all(blocks, axis, 0, 0, tiled=True)]
    all_to_all x0 -> x2, starting transfers between devices: none -> 12 us  [exchange(): return lax.all_to_all(blocks, axis, 0, 0, tiled=True)]
    ppermute x2 -> x3, starting transfers between devices: 18.3 us -> 8.97 us  [the longest x1 4.02 us: step(): below = lax.ppermute(tile, 'p', SWAP)]
    ppermute x2 -> x3, waiting for transfers between devices: 2.34 us -> 0.01 us  [the longest x1 0.01 us: step(): corner = lax.ppermute(below, 'c', SWAP)]
  transfers between devices with their start and end apart: 2 -> 5, of which waited for: 2 -> 2; matrix products, arithmetic and copies ran while one was open for 0% -> 1% of each run, Pallas kernels for 0% -> 0%
where the time goes in v2:
time: 108 us; the launch traced here: 107 us
  blocking collectives  66 us (61%)
  starting transfers between devices  21 us (19%)
  waiting for transfers between devices  14.3 us (13%)
  local copies, waits for them, and re-layouts  2.8 us (3%)
  other arithmetic  1.65 us (2%)
  matrix products  1.44 us (1%)
    all_to_all x4, blocking collectives, exchange(): return lax.all_to_all(blocks, axis, 0, 0, tiled=True)  66 us
    all_to_all x2, waiting for transfers between devices, exchange(): return lax.all_to_all(blocks, axis, 0, 0, tiled=True)  14.3 us
    all_to_all x2, starting transfers between devices, exchange(): return lax.all_to_all(blocks, axis, 0, 0, tiled=True)  12 us
    ppermute x1, starting transfers between devices, step(): below = lax.ppermute(tile, 'p', SWAP)  4.02 us
    ppermute x1, starting transfers between devices, step(): corner = lax.ppermute(below, 'c', SWAP)  2.95 us
  transfers between devices with their start and end apart: 5, of which 2 were waited for; matrix products, arithmetic and copies ran while one was open for 1% of the time, Pallas kernels for 0%

profile of v2, /device:TPU:1, one launch (start us, length us, event | category | flops | bytes accessed | tf_op | source)
XLA Modules:
  0.0 107.3 jit_solution(11298937922938355473)
XLA Ops:
  0.0 0.7 convert_bitcast_fusion
  0.7 0.2 broadcast_in_dim.12
  0.9 0.0 copy-start
  0.9 0.6 convert_element_type.34
  1.5 0.4 copy-done
  1.9 0.1 bitcast_multiply_fusion
  2.0 4.0 %collective-permute-start.1 = (bf16[512,512]{1,0:T(8,128)(2,1)S(1)}, bf16[512,512]{1,0:T(8,128)(2,1)S(1)}, u32[]{:S(2)}, u32[]{:S(2)}) collective-permute-start(bf16[512,512]{1,0:T(8,128)(2,1)S(1)} %bitcast_multiply_fusion), channel_id=1, source_target_pairs={{0,32},{32,0},{1,33},{33,1},{2,34},{34,2},{3,35},{35,3},{4,36},{36... | collective-permute-start | bytes 1572872 | tf_op jit(solution)/shard_map/ppermute | solution.py:39
  6.1 0.7 broadcast_in_dim.14
  6.7 8.0 %all-to-all-start = ((bf16[8,16,512]{2,1,0:T(8,128)(2,1)}), bf16[8,16,512]{2,1,0:T(8,128)(2,1)S(1)}, u32[]{:S(2)}, u32[]{:S(2)}) async-start(bf16[8,16,512]{2,1,0:T(8,128)(2,1)} %bitcast.3), calls=%async_computation | async-start | bytes 262144 | tf_op jit(solution)/shard_map/all_to_all | solution.py:13
  14.7 2.0 %collective-permute-start = (bf16[512,512]{1,0:T(8,128)(2,1)S(1)}, bf16[512,512]{1,0:T(8,128)(2,1)S(1)}, u32[]{:S(2)}, u32[]{:S(2)}) collective-permute-start(bf16[512,512]{1,0:T(8,128)(2,1)S(1)} %bitcast_multiply_fusion), channel_id=1, source_target_pairs={{0,2},{2,0},{1,3},{3,1},{4,6},{6,4},{5,7},{7,5},{8,10},{10,8},{9,1... | collective-permute-start | bytes 1572872 | tf_op jit(solution)/shard_map/ppermute | solution.py:40
  16.8 5.0 %all-to-all-done = bf16[8,16,512]{2,1,0:T(8,128)(2,1)S(1)} async-done(((bf16[8,16,512]{2,1,0:T(8,128)(2,1)}), bf16[8,16,512]{2,1,0:T(8,128)(2,1)S(1)}, u32[]{:S(2)}, u32[]{:S(2)}) %all-to-all-start) | async-done | bytes 131104 | tf_op jit(solution)/shard_map/all_to_all | solution.py:13
  21.8 0.0 collective-permute-done.1
  21.8 2.9 %collective-permute-start.2 = (bf16[512,512]{1,0:T(8,128)(2,1)S(1)}, bf16[512,512]{1,0:T(8,128)(2,1)S(1)}, u32[]{:S(2)}, u32[]{:S(2)}) collective-permute-start(bf16[512,512]{1,0:T(8,128)(2,1)S(1)} %collective-permute-done.1), channel_id=1, source_target_pairs={{0,2},{2,0},{1,3},{3,1},{4,6},{6,4},{5,7},{7,5},{8,10},{10,8},{9,1... | collective-permute-start | bytes 1572872 | tf_op jit(solution)/shard_map/ppermute | solution.py:41
  24.8 0.8 broadcast_in_dim.30
  25.7 4.0 %all-to-all-start.1 = ((bf16[4,4,16,1024]{3,2,1,0:T(8,128)(2,1)}), bf16[4,4,16,1024]{3,2,1,0:T(8,128)(2,1)S(1)}, u32[]{:S(2)}, u32[]{:S(2)}) async-start(bf16[4,4,16,1024]{3,2,1,0:T(8,128)(2,1)} %broadcast_in_dim.30), calls=%async_computation.1 | async-start | bytes 1048576 | tf_op jit(solution)/shard_map/all_to_all | solution.py:13
  29.7 0.0 collective-permute-done
  29.7 9.3 %all-to-all-done.1 = bf16[4,4,16,1024]{3,2,1,0:T(8,128)(2,1)S(1)} async-done(((bf16[4,4,16,1024]{3,2,1,0:T(8,128)(2,1)}), bf16[4,4,16,1024]{3,2,1,0:T(8,128)(2,1)S(1)}, u32[]{:S(2)}, u32[]{:S(2)}) %all-to-all-start.1) | async-done | bytes 524320 | tf_op jit(solution)/shard_map/all_to_all | solution.py:13
  39.0 0.0 collective-permute-done.2
  39.0 0.7 convolution_convert_fusion.1
  39.7 25.4 %all_to_all.30 = bf16[8,32,1024]{2,1,0:T(8,128)(2,1)S(1)} all-to-all(bf16[8,32,1024]{2,1,0:T(8,128)(2,1)S(1)} %bitcast.50), channel_id=1, replica_groups=mesh['x'=4,'h'=2,'p'=2,'z'=8,'c'=2,'l'=2] {'z'}, dimensions={0} | all-to-all | bytes 1048576 | tf_op jit(solution)/shard_map/all_to_all | solution.py:13
  65.1 0.1 reduce_sum.33
  65.2 0.1 broadcast_in_dim.31
  65.3 17.3 %all_to_all.31 = bf16[8,32,1024]{2,1,0:T(8,128)(2,1)S(1)} all-to-all(bf16[8,32,1024]{2,1,0:T(8,128)(2,1)S(1)} %broadcast_in_dim.31), channel_id=1, replica_groups=mesh['x'=4,'h'=2,'p'=2,'z'=8,'c'=2,'l'=2] {'z'}, dimensions={0} | all-to-all | bytes 1048576 | tf_op jit(solution)/shard_map/all_to_all | solution.py:13
  82.6 0.7 convolution_convert_fusion
  83.3 9.3 %all_to_all.32 = bf16[4,64,1024]{2,1,0:T(8,128)(2,1)S(1)} all-to-all(bf16[4,64,1024]{2,1,0:T(8,128)(2,1)S(1)} %bitcast.49), channel_id=1, replica_groups=mesh['x'=4,'h'=2,'p'=2,'z'=8,'c'=2,'l'=2] {'x'}, dimensions={0} | all-to-all | bytes 1048576 | tf_op jit(solution)/shard_map/all_to_all | solution.py:13
  92.6 0.1 reduce_sum.34
  92.8 13.9 %all_to_all.33 = bf16[8,16,512]{2,1,0:T(8,128)(2,1)S(1)} all-to-all(bf16[8,16,512]{2,1,0:T(8,128)(2,1)S(1)} %bitcast.51), channel_id=1, replica_groups=mesh['x'=4,'h'=2,'p'=2,'z'=8,'c'=2,'l'=2] {'h','p','c'}, dimensions={0} | all-to-all | bytes 262144 | tf_op jit(solution)/shard_map/all_to_all | solution.py:13
  106.7 0.7 fusion.1
  (7 shorter events, 0.1 us)
Async XLA Ops:
  0.9 1.0 copy-start
  2.0 19.8 %collective-permute-start.1 = (bf16[512,512]{1,0:T(8,128)(2,1)S(1)}, bf16[512,512]{1,0:T(8,128)(2,1)S(1)}, u32[]{:S(2)}, u32[]{:S(2)}) collective-permute-start(bf16[512,512]{1,0:T(8,128)(2,1)S(1)} %bitcast_multiply_fusion), channel_id=1, source_target_pairs={{0,32},{32,0},{1,33},{33,1},{2,34},{34,2},{3,35},{35,3},{4,36},{36... | collective-permute-start | bytes 1572872 | tf_op jit(solution)/shard_map/ppermute | solution.py:39
  6.7 15.1 %all-to-all-start = ((bf16[8,16,512]{2,1,0:T(8,128)(2,1)}), bf16[8,16,512]{2,1,0:T(8,128)(2,1)S(1)}, u32[]{:S(2)}, u32[]{:S(2)}) async-start(bf16[8,16,512]{2,1,0:T(8,128)(2,1)} %bitcast.3), calls=%async_computation | async-start | bytes 262144 | tf_op jit(solution)/shard_map/all_to_all | solution.py:13
  14.7 14.9 %collective-permute-start = (bf16[512,512]{1,0:T(8,128)(2,1)S(1)}, bf16[512,512]{1,0:T(8,128)(2,1)S(1)}, u32[]{:S(2)}, u32[]{:S(2)}) collective-permute-start(bf16[512,512]{1,0:T(8,128)(2,1)S(1)} %bitcast_multiply_fusion), channel_id=1, source_target_pairs={{0,2},{2,0},{1,3},{3,1},{4,6},{6,4},{5,7},{7,5},{8,10},{10,8},{9,1... | collective-permute-start | bytes 1572872 | tf_op jit(solution)/shard_map/ppermute | solution.py:40
  21.8 17.1 %collective-permute-start.2 = (bf16[512,512]{1,0:T(8,128)(2,1)S(1)}, bf16[512,512]{1,0:T(8,128)(2,1)S(1)}, u32[]{:S(2)}, u32[]{:S(2)}) collective-permute-start(bf16[512,512]{1,0:T(8,128)(2,1)S(1)} %collective-permute-done.1), channel_id=1, source_target_pairs={{0,2},{2,0},{1,3},{3,1},{4,6},{6,4},{5,7},{7,5},{8,10},{10,8},{9,1... | collective-permute-start | bytes 1572872 | tf_op jit(solution)/shard_map/ppermute | solution.py:41
  25.7 13.3 %all-to-all-start.1 = ((bf16[4,4,16,1024]{3,2,1,0:T(8,128)(2,1)}), bf16[4,4,16,1024]{3,2,1,0:T(8,128)(2,1)S(1)}, u32[]{:S(2)}, u32[]{:S(2)}) async-start(bf16[4,4,16,1024]{3,2,1,0:T(8,128)(2,1)} %broadcast_in_dim.30), calls=%async_computation.1 | async-start | bytes 1048576 | tf_op jit(solution)/shard_map/all_to_all | solution.py:13

commit v3 on v2

--- a/solution.py
+++ b/solution.py
@@ -42,7 +42,8 @@
     own = lax.dynamic_slice_in_dim(tile, lax.axis_index("l") * 4 * share, 4 * share, 0)
 
     parts = jnp.broadcast_to(own.reshape(1, 4, share, width), (2, 4, share, width))
-    parts = exchange(parts.reshape(8, share, width), NEAR).reshape(4, 2, share, width)
+    parts = exchange(parts.reshape(8, share, width), NEAR)
+    parts = parts.reshape(4, 2, share, width)
     left, right = parts[:, 0], parts[:, 1]
     rows = jnp.concatenate(
         [jnp.where(first, left, right), jnp.where(first, right, left)], axis=2
@@ -62,14 +63,13 @@
     squared = total(exchange(partial.reshape(nz, -1, 2 * width), "z")).astype(half)
     squared = gather(squared, "z").reshape(-1, 2 * width)
     partial = jnp.dot(squared, block, preferred_element_type=jnp.float32).astype(half)
-    partial = total(exchange(partial.reshape(nx, -1, 2 * width), "x")).astype(half)
-    partial = partial.reshape(4, share, 2 * width)
+    partial = partial.reshape(4 * nx, share, 2 * width)
     left, right = partial[:, :, :width], partial[:, :, width:]
     parts = jnp.stack(
         [jnp.where(first, left, right), jnp.where(first, right, left)], axis=1
     )
-    parts = exchange(parts.reshape(8, share, width), NEAR)
-    cubed = total(parts.reshape(2, 4 * share, width))
+    parts = exchange(parts.reshape(8 * nx, share, width), ("x",) + NEAR)
+    cubed = total(parts.reshape(2 * nx, 4 * share, width))
     signed = 1.5 * own.astype(jnp.float32) - 0.5 * cubed
     return signed.astype(half)[None]
 

time: 108 us -> 109 us (level)
  blocking collectives: 66 us -> 67.2 us
    all_to_all x4 -> x3, blocking collectives: 66 us -> 67.2 us  [exchange(): return lax.all_to_all(blocks, axis, 0, 0, tiled=True)]
where the time goes in v3:
time: 109 us
  blocking collectives  67.2 us (62%)
  starting transfers between devices  21 us (19%)
  waiting for transfers between devices  14.3 us (13%)
  local copies, waits for them, and re-layouts  2.8 us (3%)
  other arithmetic  1.68 us (2%)
  matrix products  1.44 us (1%)
    all_to_all x3, blocking collectives, exchange(): return lax.all_to_all(blocks, axis, 0, 0, tiled=True)  67.2 us
    all_to_all x2, waiting for transfers between devices, exchange(): return lax.all_to_all(blocks, axis, 0, 0, tiled=True)  14.3 us
    all_to_all x2, starting transfers between devices, exchange(): return lax.all_to_all(blocks, axis, 0, 0, tiled=True)  12 us
    ppermute x1, starting transfers between devices, step(): below = lax.ppermute(tile, 'p', SWAP)  4.02 us
    ppermute x1, starting transfers between devices, step(): corner = lax.ppermute(below, 'c', SWAP)  2.95 us
  transfers between devices with their start and end apart: 5, of which 2 were waited for; matrix products, arithmetic and copies ran while one was open for 1% of the time, Pallas kernels for 0%

profile of v3, /device:TPU:1, one launch (start us, length us, event | category | flops | bytes accessed | tf_op | source)
XLA Modules:
  0.0 108.7 jit_solution(3740414579801935969)
XLA Ops:
  0.0 0.7 convert_bitcast_fusion
  0.7 0.2 broadcast_in_dim.12
  0.9 0.0 copy-start
  0.9 0.6 convert_element_type.32
  1.5 0.4 copy-done
  1.9 0.1 bitcast_multiply_fusion
  2.0 4.0 %collective-permute-start.1 = (bf16[512,512]{1,0:T(8,128)(2,1)S(1)}, bf16[512,512]{1,0:T(8,128)(2,1)S(1)}, u32[]{:S(2)}, u32[]{:S(2)}) collective-permute-start(bf16[512,512]{1,0:T(8,128)(2,1)S(1)} %bitcast_multiply_fusion), channel_id=1, source_target_pairs={{0,32},{32,0},{1,33},{33,1},{2,34},{34,2},{3,35},{35,3},{4,36},{36... | collective-permute-start | bytes 1572872 | tf_op jit(solution)/shard_map/ppermute | solution.py:39
  6.1 0.7 broadcast_in_dim.14
  6.7 8.0 %all-to-all-start = ((bf16[8,16,512]{2,1,0:T(8,128)(2,1)}), bf16[8,16,512]{2,1,0:T(8,128)(2,1)S(1)}, u32[]{:S(2)}, u32[]{:S(2)}) async-start(bf16[8,16,512]{2,1,0:T(8,128)(2,1)} %bitcast.3), calls=%async_computation | async-start | bytes 262144 | tf_op jit(solution)/shard_map/all_to_all | solution.py:13
  14.7 2.0 %collective-permute-start = (bf16[512,512]{1,0:T(8,128)(2,1)S(1)}, bf16[512,512]{1,0:T(8,128)(2,1)S(1)}, u32[]{:S(2)}, u32[]{:S(2)}) collective-permute-start(bf16[512,512]{1,0:T(8,128)(2,1)S(1)} %bitcast_multiply_fusion), channel_id=1, source_target_pairs={{0,2},{2,0},{1,3},{3,1},{4,6},{6,4},{5,7},{7,5},{8,10},{10,8},{9,1... | collective-permute-start | bytes 1572872 | tf_op jit(solution)/shard_map/ppermute | solution.py:40
  16.8 5.0 %all-to-all-done = bf16[8,16,512]{2,1,0:T(8,128)(2,1)S(1)} async-done(((bf16[8,16,512]{2,1,0:T(8,128)(2,1)}), bf16[8,16,512]{2,1,0:T(8,128)(2,1)S(1)}, u32[]{:S(2)}, u32[]{:S(2)}) %all-to-all-start) | async-done | bytes 131104 | tf_op jit(solution)/shard_map/all_to_all | solution.py:13
  21.8 0.0 collective-permute-done.1
  21.8 2.9 %collective-permute-start.2 = (bf16[512,512]{1,0:T(8,128)(2,1)S(1)}, bf16[512,512]{1,0:T(8,128)(2,1)S(1)}, u32[]{:S(2)}, u32[]{:S(2)}) collective-permute-start(bf16[512,512]{1,0:T(8,128)(2,1)S(1)} %collective-permute-done.1), channel_id=1, source_target_pairs={{0,2},{2,0},{1,3},{3,1},{4,6},{6,4},{5,7},{7,5},{8,10},{10,8},{9,1... | collective-permute-start | bytes 1572872 | tf_op jit(solution)/shard_map/ppermute | solution.py:41
  24.8 0.9 broadcast_in_dim.30
  25.7 4.0 %all-to-all-start.1 = ((bf16[4,4,16,1024]{3,2,1,0:T(8,128)(2,1)}), bf16[4,4,16,1024]{3,2,1,0:T(8,128)(2,1)S(1)}, u32[]{:S(2)}, u32[]{:S(2)}) async-start(bf16[4,4,16,1024]{3,2,1,0:T(8,128)(2,1)} %broadcast_in_dim.30), calls=%async_computation.1 | async-start | bytes 1048576 | tf_op jit(solution)/shard_map/all_to_all | solution.py:13
  29.7 0.0 collective-permute-done
  29.7 9.3 %all-to-all-done.1 = bf16[4,4,16,1024]{3,2,1,0:T(8,128)(2,1)S(1)} async-done(((bf16[4,4,16,1024]{3,2,1,0:T(8,128)(2,1)}), bf16[4,4,16,1024]{3,2,1,0:T(8,128)(2,1)S(1)}, u32[]{:S(2)}, u32[]{:S(2)}) %all-to-all-start.1) | async-done | bytes 524320 | tf_op jit(solution)/shard_map/all_to_all | solution.py:13
  39.0 0.0 collective-permute-done.2
  39.0 0.7 convolution_convert_fusion.1
  39.7 25.4 %all_to_all.25 = bf16[8,32,1024]{2,1,0:T(8,128)(2,1)S(1)} all-to-all(bf16[8,32,1024]{2,1,0:T(8,128)(2,1)S(1)} %bitcast.50), channel_id=1, replica_groups=mesh['x'=4,'h'=2,'p'=2,'z'=8,'c'=2,'l'=2] {'z'}, dimensions={0} | all-to-all | bytes 1048576 | tf_op jit(solution)/shard_map/all_to_all | solution.py:13
  65.1 0.1 reduce_sum.21
  65.2 0.1 broadcast_in_dim.31
  65.3 17.3 %all_to_all.26 = bf16[8,32,1024]{2,1,0:T(8,128)(2,1)S(1)} all-to-all(bf16[8,32,1024]{2,1,0:T(8,128)(2,1)S(1)} %broadcast_in_dim.31), channel_id=1, replica_groups=mesh['x'=4,'h'=2,'p'=2,'z'=8,'c'=2,'l'=2] {'z'}, dimensions={0} | all-to-all | bytes 1048576 | tf_op jit(solution)/shard_map/all_to_all | solution.py:13
  82.6 0.7 convolution_convert_fusion
  83.4 0.1 pad_maximum_fusion
  83.4 24.5 %all_to_all.27 = bf16[32,16,512]{2,1,0:T(8,128)(2,1)S(1)} all-to-all(bf16[32,16,512]{2,1,0:T(8,128)(2,1)S(1)} %bitcast.45), channel_id=1, replica_groups=mesh['x'=4,'h'=2,'p'=2,'z'=8,'c'=2,'l'=2] {'x','h','p','c'}, dimensions={0} | all-to-all | bytes 1048576 | tf_op jit(solution)/shard_map/all_to_all | solution.py:13
  107.9 0.1 convert_reduce_fusion
  108.0 0.7 fusion.1
  (5 shorter events, 0.1 us)
Async XLA Ops:
  0.9 1.0 copy-start
  2.0 19.8 %collective-permute-start.1 = (bf16[512,512]{1,0:T(8,128)(2,1)S(1)}, bf16[512,512]{1,0:T(8,128)(2,1)S(1)}, u32[]{:S(2)}, u32[]{:S(2)}) collective-permute-start(bf16[512,512]{1,0:T(8,128)(2,1)S(1)} %bitcast_multiply_fusion), channel_id=1, source_target_pairs={{0,32},{32,0},{1,33},{33,1},{2,34},{34,2},{3,35},{35,3},{4,36},{36... | collective-permute-start | bytes 1572872 | tf_op jit(solution)/shard_map/ppermute | solution.py:39
  6.7 15.1 %all-to-all-start = ((bf16[8,16,512]{2,1,0:T(8,128)(2,1)}), bf16[8,16,512]{2,1,0:T(8,128)(2,1)S(1)}, u32[]{:S(2)}, u32[]{:S(2)}) async-start(bf16[8,16,512]{2,1,0:T(8,128)(2,1)} %bitcast.3), calls=%async_computation | async-start | bytes 262144 | tf_op jit(solution)/shard_map/all_to_all | solution.py:13
  14.7 14.9 %collective-permute-start = (bf16[512,512]{1,0:T(8,128)(2,1)S(1)}, bf16[512,512]{1,0:T(8,128)(2,1)S(1)}, u32[]{:S(2)}, u32[]{:S(2)}) collective-permute-start(bf16[512,512]{1,0:T(8,128)(2,1)S(1)} %bitcast_multiply_fusion), channel_id=1, source_target_pairs={{0,2},{2,0},{1,3},{3,1},{4,6},{6,4},{5,7},{7,5},{8,10},{10,8},{9,1... | collective-permute-start | bytes 1572872 | tf_op jit(solution)/shard_map/ppermute | solution.py:40
  21.8 17.1 %collective-permute-start.2 = (bf16[512,512]{1,0:T(8,128)(2,1)S(1)}, bf16[512,512]{1,0:T(8,128)(2,1)S(1)}, u32[]{:S(2)}, u32[]{:S(2)}) collective-permute-start(bf16[512,512]{1,0:T(8,128)(2,1)S(1)} %collective-permute-done.1), channel_id=1, source_target_pairs={{0,2},{2,0},{1,3},{3,1},{4,6},{6,4},{5,7},{7,5},{8,10},{10,8},{9,1... | collective-permute-start | bytes 1572872 | tf_op jit(solution)/shard_map/ppermute | solution.py:41
  25.7 13.3 %all-to-all-start.1 = ((bf16[4,4,16,1024]{3,2,1,0:T(8,128)(2,1)}), bf16[4,4,16,1024]{3,2,1,0:T(8,128)(2,1)S(1)}, u32[]{:S(2)}, u32[]{:S(2)}) async-start(bf16[4,4,16,1024]{3,2,1,0:T(8,128)(2,1)} %broadcast_in_dim.30), calls=%async_computation.1 | async-start | bytes 1048576 | tf_op jit(solution)/shard_map/all_to_all | solution.py:13

commit v4 on v3

v4 whole, which is shorter than its diff:
```python
import jax
import jax.numpy as jnp
from jax import lax
from jax.sharding import Mesh, PartitionSpec as P


SIZES = {"x": 4, "h": 2, "p": 2, "w": 4, "q": 2, "c": 2, "l": 2}
NEAR = ("h", "p", "q", "c")


def exchange(blocks, axis):
    return lax.all_to_all(blocks, axis, 0, 0, tiled=True)


def gather(block, axis):
    count = lax.axis_size(axis)
    return exchange(jnp.broadcast_to(block[None], (count,) + block.shape), axis)


def swap(tile, axis):
    return lax.ppermute(tile, axis, ((0, 1), (1, 0)))


def total(blocks):
    return jnp.sum(blocks.astype(jnp.float32), axis=0)


def masked(tile, pattern):
    width, blocks = tile.shape[0], pattern.shape[0]
    span = width // blocks
    mask = jnp.broadcast_to(pattern[:, None, :, None], (blocks, span, blocks, span))
    return tile * mask.reshape(width, width).astype(tile.dtype)


def turned(parts):
    q = lax.axis_index("q") == 0
    c = lax.axis_index("c") == 0
    a, b = jnp.where(q, parts[0], parts[2]), jnp.where(q, parts[1], parts[3])
    d, e = jnp.where(q, parts[2], parts[0]), jnp.where(q, parts[3], parts[1])
    return jnp.where(c, a, b), jnp.where(c, b, a), jnp.where(c, d, e), jnp.where(c, e, d)


def step(x_tiles, pattern):
    half = jnp.bfloat16
    width = x_tiles.shape[1]
    share = width // 64
    nx, nw = lax.axis_size("x"), lax.axis_size("w")
    upper = lax.axis_index("p") == 0
    tile = masked(x_tiles[0], pattern[0])
    own = lax.dynamic_slice_in_dim(tile, lax.axis_index("l") * 8 * share, 8 * share, 0)

    parts = own.reshape(2, 4, share, width).transpose(1, 0, 2, 3)
    parts = jnp.broadcast_to(parts.reshape(1, 4, 2 * share, width), (4, 4, 2 * share, width))
    parts = exchange(parts.reshape(16, 2 * share, width), NEAR)
    parts = parts.reshape(4, 4, 2 * share, width)
    rows = jnp.concatenate(turned([parts[:, k] for k in range(4)]), axis=2)
    rows = gather(rows, "x").reshape(-1, 4 * width)

    along = swap(tile, "q")
    tiles = [tile, swap(tile, "c"), along, swap(along, "c")]
    below = swap(tile, "p")
    corner = swap(along, "p")
    lower = [below, swap(below, "c"), corner, swap(corner, "c")]

    block = jnp.concatenate(tiles, axis=1)
    partial = lax.dot_general(
        rows, block, (((1,), (1,)), ((), ())), preferred_element_type=jnp.float32
    ).astype(half)
    squared = total(exchange(partial.reshape(nw, -1, width), "w")).astype(half)
    squared = squared.reshape(4, 2, share, width).transpose(1, 0, 2, 3)
    squared = jnp.broadcast_to(
        squared.reshape(2, 1, 4 * share, width), (2, nw, 4 * share, width)
    )
    squared = exchange(squared.reshape(2 * nw, 4 * share, width), ("p", "w"))
    squared = squared.reshape(2, nw * 4 * share, width)
    squared = jnp.concatenate(
        [
            jnp.where(upper, squared[0], squared[1]),
            jnp.where(upper, squared[1], squared[0]),
        ],
        axis=1,
    )
    block = jnp.concatenate([block, jnp.concatenate(lower, axis=1)], axis=0)
    partial = jnp.dot(squared, block, preferred_element_type=jnp.float32).astype(half)
    partial = partial.reshape(4 * nx, share, 4 * width)
    parts = turned([partial[:, :, k * width : (k + 1) * width] for k in range(4)])
    parts = jnp.stack(parts, axis=1).reshape(16 * nx, share, width)
    parts = exchange(parts, ("x",) + NEAR)
    cubed = total(parts.reshape(2 * nx, 8 * share, width))
    signed = 1.5 * own.astype(jnp.float32) - 0.5 * cubed
    return signed.astype(half)[None]


def solution(mesh, sizes=SIZES):
    fine = Mesh(mesh.devices.reshape(tuple(sizes.values())), tuple(sizes))
    grid = ("x", "h", "p", "w", "q", "c")
    specs = (P(grid, None, None), P(grid, None, None))
    return jax.shard_map(
        step, mesh=fine, in_specs=specs, out_specs=P(grid, "l", None), check_vma=False
    )
```

time: 109 us -> 127 us (1.17)
  blocking collectives: 67.2 us -> 23 us
  starting transfers between devices: 21 us -> 52.8 us
  matrix products: 1.44 us -> 19.9 us
  waiting for transfers between devices: 14.3 us -> 24.5 us
    all_to_all x3 -> x1, blocking collectives: 67.2 us -> 23 us  [exchange(): return lax.all_to_all(blocks, axis, 0, 0, tiled=True)]
    dot_general x1, matrix products: 0.7 us -> 18.5 us  [step(): jnp.dot(squared, block, preferred_element_type=jnp.float32).astype(half)]
    all_to_all x2 -> x4, starting transfers between devices: 12 us -> 28.1 us  [exchange(): return lax.all_to_all(blocks, axis, 0, 0, tiled=True)]
    ppermute x3 -> x7, starting transfers between devices: 8.97 us -> 24.7 us  [swap(): return lax.ppermute(tile, axis, ((0, 1), (1, 0)))]
    ppermute x3 -> x7, waiting for transfers between devices: 0.01 us -> 8.27 us  [swap(): return lax.ppermute(tile, axis, ((0, 1), (1, 0)))]
    all_to_all x2 -> x4, waiting for transfers between devices: 14.3 us -> 16.2 us  [exchange(): return lax.all_to_all(blocks, axis, 0, 0, tiled=True)]
  transfers between devices with their start and end apart: 5 -> 11, of which waited for: 2 -> 7; matrix products, arithmetic and copies ran while one was open for 1% -> 2% of each run, Pallas kernels for 0% -> 0%
where the time goes in v4:
time: 127 us; the launch traced here: 126 us
  starting transfers between devices  52.8 us (42%)
  waiting for transfers between devices  24.5 us (19%)
  blocking collectives  23 us (18%)
  matrix products  19.9 us (16%)
  local copies, waits for them, and re-layouts  3.8 us (3%)
  other arithmetic  1.72 us (1%)
    all_to_all x4, starting transfers between devices, exchange(): return lax.all_to_all(blocks, axis, 0, 0, tiled=True)  28.1 us
    ppermute x7, starting transfers between devices, swap(): return lax.ppermute(tile, axis, ((0, 1), (1, 0)))  24.7 us
    all_to_all x1, blocking collectives, exchange(): return lax.all_to_all(blocks, axis, 0, 0, tiled=True)  23 us
    dot_general x1, matrix products, step(): jnp.dot(squared, block, preferred_element_type=jnp.float32).astype(half)  18.5 us
    all_to_all x4, waiting for transfers between devices, exchange(): return lax.all_to_all(blocks, axis, 0, 0, tiled=True)  16.2 us
    ppermute x7, waiting for transfers between devices, swap(): return lax.ppermute(tile, axis, ((0, 1), (1, 0)))  8.27 us
  transfers between devices with their start and end apart: 11, of which 7 were waited for; matrix products, arithmetic and copies ran while one was open for 2% of the time, Pallas kernels for 0%

profile of v4, /device:TPU:1, one launch (start us, length us, event | category | flops | bytes accessed | tf_op | source)
XLA Modules:
  0.0 126.0 jit_solution(13147755212388648645)
XLA Ops:
  0.0 0.7 convert_bitcast_fusion
  0.7 0.2 broadcast_in_dim.28
  0.9 0.0 copy-start
  0.9 0.6 convert_element_type.32
  1.5 0.4 copy-done
  1.9 0.1 bitcast_multiply_fusion
  2.0 0.7 broadcast_in_dim.30
  2.8 10.2 %all-to-all-start = ((bf16[16,16,512]{2,1,0:T(8,128)(2,1)}), bf16[16,16,512]{2,1,0:T(8,128)(2,1)S(1)}, u32[]{:S(2)}, u32[]{:S(2)}) async-start(bf16[16,16,512]{2,1,0:T(8,128)(2,1)} %bitcast.5), calls=%async_computation | async-start | bytes 524288 | tf_op jit(solution)/shard_map/all_to_all | solution.py:12
  12.9 3.3 %collective-permute-start.1 = (bf16[512,512]{1,0:T(8,128)(2,1)S(1)}, bf16[512,512]{1,0:T(8,128)(2,1)S(1)}, u32[]{:S(2)}, u32[]{:S(2)}) collective-permute-start(bf16[512,512]{1,0:T(8,128)(2,1)S(1)} %bitcast_multiply_fusion), channel_id=1, source_target_pairs={{0,4},{4,0},{1,5},{5,1},{2,6},{6,2},{3,7},{7,3},{8,12},{12,8},{9,1... | collective-permute-start | bytes 1572872 | tf_op jit(solution)/shard_map/ppermute | solution.py:21
  16.2 6.3 %all-to-all-done = bf16[16,16,512]{2,1,0:T(8,128)(2,1)S(1)} async-done(((bf16[16,16,512]{2,1,0:T(8,128)(2,1)}), bf16[16,16,512]{2,1,0:T(8,128)(2,1)S(1)}, u32[]{:S(2)}, u32[]{:S(2)}) %all-to-all-start) | async-done | bytes 262176 | tf_op jit(solution)/shard_map/all_to_all | solution.py:12
  22.6 1.1 broadcast_in_dim.31
  23.7 3.5 %all-to-all-start.1 = ((bf16[4,4,16,2048]{3,2,1,0:T(8,128)(2,1)}), bf16[4,4,16,2048]{3,2,1,0:T(8,128)(2,1)S(1)}, u32[]{:S(2)}, u32[]{:S(2)}) async-start(bf16[4,4,16,2048]{3,2,1,0:T(8,128)(2,1)} %broadcast_in_dim.31), calls=%async_computation.1 | async-start | bytes 2097152 | tf_op jit(solution)/shard_map/all_to_all | solution.py:12
  27.2 2.6 %collective-permute-start = (bf16[512,512]{1,0:T(8,128)(2,1)S(1)}, bf16[512,512]{1,0:T(8,128)(2,1)S(1)}, u32[]{:S(2)}, u32[]{:S(2)}) collective-permute-start(bf16[512,512]{1,0:T(8,128)(2,1)S(1)} %bitcast_multiply_fusion), channel_id=1, source_target_pairs={{0,2},{2,0},{1,3},{3,1},{4,6},{6,4},{5,7},{7,5},{8,10},{10,8},{9,1... | collective-permute-start | bytes 1572872 | tf_op jit(solution)/shard_map/ppermute | solution.py:21
  29.8 0.2 collective-permute-done.1
  30.0 2.6 %collective-permute-start.2 = (bf16[512,512]{1,0:T(8,128)(2,1)S(1)}, bf16[512,512]{1,0:T(8,128)(2,1)S(1)}, u32[]{:S(2)}, u32[]{:S(2)}) collective-permute-start(bf16[512,512]{1,0:T(8,128)(2,1)S(1)} %collective-permute-done.1), channel_id=1, source_target_pairs={{0,2},{2,0},{1,3},{3,1},{4,6},{6,4},{5,7},{7,5},{8,10},{10,8},{9,1... | collective-permute-start | bytes 1572872 | tf_op jit(solution)/shard_map/ppermute | solution.py:21
  32.7 0.0 collective-permute-done
  32.7 1.5 %collective-permute-done.2 = bf16[512,512]{1,0:T(8,128)(2,1)S(1)} collective-permute-done((bf16[512,512]{1,0:T(8,128)(2,1)S(1)}, bf16[512,512]{1,0:T(8,128)(2,1)S(1)}, u32[]{:S(2)}, u32[]{:S(2)}) %collective-permute-start.2) | collective-permute-done | bytes 524320 | tf_op jit(solution)/shard_map/ppermute | solution.py:21
  34.2 7.5 %all-to-all-done.1 = bf16[4,4,16,2048]{3,2,1,0:T(8,128)(2,1)S(1)} async-done(((bf16[4,4,16,2048]{3,2,1,0:T(8,128)(2,1)}), bf16[4,4,16,2048]{3,2,1,0:T(8,128)(2,1)S(1)}, u32[]{:S(2)}, u32[]{:S(2)}) %all-to-all-start.1) | async-done | bytes 1048608 | tf_op jit(solution)/shard_map/all_to_all | solution.py:12
  41.7 1.4 %fusion.30 = bf16[256,512]{1,0:T(8,128)(2,1)} fusion(bf16[256,2048]{1,0:T(8,128)(2,1)S(1)} %bitcast.119, bf16[512,512]{1,0:T(8,128)(2,1)S(1)} %collective-permute-done.2, bf16[512,512]{1,0:T(8,128)(2,1)S(1)} %collective-permute-done.1, bf16[512,512]{1,0:T(8,128)(2,1)S(1)} %collective-permute-done, bf16[512,512]{1,0:T(8,128)(2,1)S(1)} %bitcast_multiply_fusion), kind=kOutput, calls=%fused_computation.26 | convolution fusion | flops 545390592 | bytes 3407872 | tf_op jit(solution)/shard_map/dot_general | solution.py:66
  43.1 7.3 %all-to-all-start.2 = ((bf16[4,64,512]{2,1,0:T(8,128)(2,1)}), bf16[4,64,512]{2,1,0:T(8,128)(2,1)S(1)}, u32[]{:S(2)}, u32[]{:S(2)}) async-start(bf16[4,64,512]{2,1,0:T(8,128)(2,1)} %bitcast.18), calls=%async_computation.2 | async-start | bytes 524288 | tf_op jit(solution)/shard_map/all_to_all | solution.py:12
  50.5 3.8 %collective-permute-start.3 = (bf16[512,512]{1,0:T(8,128)(2,1)S(1)}, bf16[512,512]{1,0:T(8,128)(2,1)S(1)}, u32[]{:S(2)}, u32[]{:S(2)}) collective-permute-start(bf16[512,512]{1,0:T(8,128)(2,1)S(1)} %bitcast_multiply_fusion), channel_id=1, source_target_pairs={{0,32},{32,0},{1,33},{33,1},{2,34},{34,2},{3,35},{35,3},{4,36},{36... | collective-permute-start | bytes 1572872 | tf_op jit(solution)/shard_map/ppermute | solution.py:21
  54.2 1.9 %collective-permute-start.5 = (bf16[512,512]{1,0:T(8,128)(2,1)S(1)}, bf16[512,512]{1,0:T(8,128)(2,1)}, u32[]{:S(2)}, u32[]{:S(2)}) collective-permute-start(bf16[512,512]{1,0:T(8,128)(2,1)S(1)} %collective-permute-done.1), channel_id=1, source_target_pairs={{0,32},{32,0},{1,33},{33,1},{2,34},{34,2},{3,35},{35,3},{4,36},{36... | collective-permute-start | bytes 1572872 | tf_op jit(solution)/shard_map/ppermute | solution.py:21
  56.2 2.4 %all-to-all-done.2 = bf16[4,64,512]{2,1,0:T(8,128)(2,1)S(1)} async-done(((bf16[4,64,512]{2,1,0:T(8,128)(2,1)}), bf16[4,64,512]{2,1,0:T(8,128)(2,1)S(1)}, u32[]{:S(2)}, u32[]{:S(2)}) %all-to-all-start.2) | async-done | bytes 262176 | tf_op jit(solution)/shard_map/all_to_all | solution.py:12
  58.7 0.7 broadcast_in_dim.33
  59.4 7.1 %all-to-all-start.3 = ((bf16[8,32,512]{2,1,0:T(8,128)(2,1)}), bf16[8,32,512]{2,1,0:T(8,128)(2,1)S(1)}, u32[]{:S(2)}, u32[]{:S(2)}) async-start(bf16[8,32,512]{2,1,0:T(8,128)(2,1)} %bitcast.22), calls=%async_computation.3 | async-start | bytes 524288 | tf_op jit(solution)/shard_map/all_to_all | solution.py:12
  66.5 0.0 collective-permute-done.3
  66.5 4.6 %collective-permute-start.4 = (bf16[512,512]{1,0:T(8,128)(2,1)S(1)}, bf16[512,512]{1,0:T(8,128)(2,1)}, u32[]{:S(2)}, u32[]{:S(2)}) collective-permute-start(bf16[512,512]{1,0:T(8,128)(2,1)S(1)} %collective-permute-done.3), channel_id=1, source_target_pairs={{0,2},{2,0},{1,3},{3,1},{4,6},{6,4},{5,7},{7,5},{8,10},{10,8},{9,1... | collective-permute-start | bytes 1572872 | tf_op jit(solution)/shard_map/ppermute | solution.py:21
  71.1 4.9 %collective-permute-done.5 = bf16[512,512]{1,0:T(8,128)(2,1)} collective-permute-done((bf16[512,512]{1,0:T(8,128)(2,1)S(1)}, bf16[512,512]{1,0:T(8,128)(2,1)}, u32[]{:S(2)}, u32[]{:S(2)}) %collective-permute-start.5) | collective-permute-done | bytes 524320 | tf_op jit(solution)/shard_map/ppermute | solution.py:21
  76.1 5.9 %collective-permute-start.6 = (bf16[512,512]{1,0:T(8,128)(2,1)}, bf16[512,512]{1,0:T(8,128)(2,1)}, u32[]{:S(2)}, u32[]{:S(2)}) collective-permute-start(bf16[512,512]{1,0:T(8,128)(2,1)} %collective-permute-done.5), channel_id=1, source_target_pairs={{0,2},{2,0},{1,3},{3,1},{4,6},{6,4},{5,7},{7,5},{8,10},{10,8},{9,1... | collective-permute-start | bytes 1572872 | tf_op jit(solution)/shard_map/ppermute | solution.py:21
  81.9 0.0 all-to-all-done.3
  82.0 0.0 collective-permute-done.4
  82.0 1.6 %collective-permute-done.6 = bf16[512,512]{1,0:T(8,128)(2,1)} collective-permute-done((bf16[512,512]{1,0:T(8,128)(2,1)}, bf16[512,512]{1,0:T(8,128)(2,1)}, u32[]{:S(2)}, u32[]{:S(2)}) %collective-permute-start.6) | collective-permute-done | bytes 524320 | tf_op jit(solution)/shard_map/ppermute | solution.py:21
  83.6 18.5 %fusion.19 = bf16[16,8,2048]{2,1,0:T(8,128)(2,1)S(1)} fusion(bf16[512,512]{1,0:T(8,128)(2,1)} %collective-permute-done.6, bf16[512,512]{1,0:T(8,128)(2,1)} %collective-permute-done.5, bf16[512,512]{1,0:T(8,128)(2,1)} %collective-permute-done.4, bf16[512,512]{1,0:T(8,128)(2,1)S(1)} %collective-permute-done.3, ...), kind=kOutput, calls=%fused_computation.17 | convolution fusion | flops 571211776 | bytes 4980736 | tf_op jit(solution)/shard_map/dot_general | solution.py:84
  102.1 0.1 select_bitcast_fusion.3
  102.1 0.1 pad_maximum_fusion
  102.2 23.0 %all_to_all.25 = bf16[64,8,512]{2,1,0:T(8,128)(2,1)S(1)} all-to-all(bf16[64,8,512]{2,1,0:T(8,128)(2,1)S(1)} %bitcast.118), channel_id=1, replica_groups=mesh['x'=4,'h'=2,'p'=2,'w'=4,'q'=2,'c'=2,'l'=2] {'x','h','p','q','c'}, dimensions={0} | all-to-all | bytes 1048576 | tf_op jit(solution)/shard_map/all_to_all | solution.py:12
  125.2 0.1 convert_reduce_fusion
  125.3 0.7 fusion.37
  (8 shorter events, 0.1 us)
Async XLA Ops:
  0.9 1.0 copy-start
  2.8 19.7 %all-to-all-start = ((bf16[16,16,512]{2,1,0:T(8,128)(2,1)}), bf16[16,16,512]{2,1,0:T(8,128)(2,1)S(1)}, u32[]{:S(2)}, u32[]{:S(2)}) async-start(bf16[16,16,512]{2,1,0:T(8,128)(2,1)} %bitcast.5), calls=%async_computation | async-start | bytes 524288 | tf_op jit(solution)/shard_map/all_to_all | solution.py:12
  12.9 17.1 %collective-permute-start.1 = (bf16[512,512]{1,0:T(8,128)(2,1)S(1)}, bf16[512,512]{1,0:T(8,128)(2,1)S(1)}, u32[]{:S(2)}, u32[]{:S(2)}) collective-permute-start(bf16[512,512]{1,0:T(8,128)(2,1)S(1)} %bitcast_multiply_fusion), channel_id=1, source_target_pairs={{0,4},{4,0},{1,5},{5,1},{2,6},{6,2},{3,7},{7,3},{8,12},{12,8},{9,1... | collective-permute-start | bytes 1572872 | tf_op jit(solution)/shard_map/ppermute | solution.py:21
  23.7 18.0 %all-to-all-start.1 = ((bf16[4,4,16,2048]{3,2,1,0:T(8,128)(2,1)}), bf16[4,4,16,2048]{3,2,1,0:T(8,128)(2,1)S(1)}, u32[]{:S(2)}, u32[]{:S(2)}) async-start(bf16[4,4,16,2048]{3,2,1,0:T(8,128)(2,1)} %broadcast_in_dim.31), calls=%async_computation.1 | async-start | bytes 2097152 | tf_op jit(solution)/shard_map/all_to_all | solution.py:12
  27.2 5.5 %collective-permute-start = (bf16[512,512]{1,0:T(8,128)(2,1)S(1)}, bf16[512,512]{1,0:T(8,128)(2,1)S(1)}, u32[]{:S(2)}, u32[]{:S(2)}) collective-permute-start(bf16[512,512]{1,0:T(8,128)(2,1)S(1)} %bitcast_multiply_fusion), channel_id=1, source_target_pairs={{0,2},{2,0},{1,3},{3,1},{4,6},{6,4},{5,7},{7,5},{8,10},{10,8},{9,1... | collective-permute-start | bytes 1572872 | tf_op jit(solution)/shard_map/ppermute | solution.py:21
  30.0 4.2 %collective-permute-start.2 = (bf16[512,512]{1,0:T(8,128)(2,1)S(1)}, bf16[512,512]{1,0:T(8,128)(2,1)S(1)}, u32[]{:S(2)}, u32[]{:S(2)}) collective-permute-start(bf16[512,512]{1,0:T(8,128)(2,1)S(1)} %collective-permute-done.1), channel_id=1, source_target_pairs={{0,2},{2,0},{1,3},{3,1},{4,6},{6,4},{5,7},{7,5},{8,10},{10,8},{9,1... | collective-permute-start | bytes 1572872 | tf_op jit(solution)/shard_map/ppermute | solution.py:21
  43.1 15.5 %all-to-all-start.2 = ((bf16[4,64,512]{2,1,0:T(8,128)(2,1)}), bf16[4,64,512]{2,1,0:T(8,128)(2,1)S(1)}, u32[]{:S(2)}, u32[]{:S(2)}) async-start(bf16[4,64,512]{2,1,0:T(8,128)(2,1)} %bitcast.18), calls=%async_computation.2 | async-start | bytes 524288 | tf_op jit(solution)/shard_map/all_to_all | solution.py:12
  50.5 16.1 %collective-permute-start.3 = (bf16[512,512]{1,0:T(8,128)(2,1)S(1)}, bf16[512,512]{1,0:T(8,128)(2,1)S(1)}, u32[]{:S(2)}, u32[]{:S(2)}) collective-permute-start(bf16[512,512]{1,0:T(8,128)(2,1)S(1)} %bitcast_multiply_fusion), channel_id=1, source_target_pairs={{0,32},{32,0},{1,33},{33,1},{2,34},{34,2},{3,35},{35,3},{4,36},{36... | collective-permute-start | bytes 1572872 | tf_op jit(solution)/shard_map/ppermute | solution.py:21
  54.2 21.8 %collective-permute-start.5 = (bf16[512,512]{1,0:T(8,128)(2,1)S(1)}, bf16[512,512]{1,0:T(8,128)(2,1)}, u32[]{:S(2)}, u32[]{:S(2)}) collective-permute-start(bf16[512,512]{1,0:T(8,128)(2,1)S(1)} %collective-permute-done.1), channel_id=1, source_target_pairs={{0,32},{32,0},{1,33},{33,1},{2,34},{34,2},{3,35},{35,3},{4,36},{36... | collective-permute-start | bytes 1572872 | tf_op jit(solution)/shard_map/ppermute | solution.py:21
  59.4 22.6 %all-to-all-start.3 = ((bf16[8,32,512]{2,1,0:T(8,128)(2,1)}), bf16[8,32,512]{2,1,0:T(8,128)(2,1)S(1)}, u32[]{:S(2)}, u32[]{:S(2)}) async-start(bf16[8,32,512]{2,1,0:T(8,128)(2,1)} %bitcast.22), calls=%async_computation.3 | async-start | bytes 524288 | tf_op jit(solution)/shard_map/all_to_all | solution.py:12
  66.5 15.5 %collective-permute-start.4 = (bf16[512,512]{1,0:T(8,128)(2,1)S(1)}, bf16[512,512]{1,0:T(8,128)(2,1)}, u32[]{:S(2)}, u32[]{:S(2)}) collective-permute-start(bf16[512,512]{1,0:T(8,128)(2,1)S(1)} %collective-permute-done.3), channel_id=1, source_target_pairs={{0,2},{2,0},{1,3},{3,1},{4,6},{6,4},{5,7},{7,5},{8,10},{10,8},{9,1... | collective-permute-start | bytes 1572872 | tf_op jit(solution)/shard_map/ppermute | solution.py:21
  76.1 7.6 %collective-permute-start.6 = (bf16[512,512]{1,0:T(8,128)(2,1)}, bf16[512,512]{1,0:T(8,128)(2,1)}, u32[]{:S(2)}, u32[]{:S(2)}) collective-permute-start(bf16[512,512]{1,0:T(8,128)(2,1)} %collective-permute-done.5), channel_id=1, source_target_pairs={{0,2},{2,0},{1,3},{3,1},{4,6},{6,4},{5,7},{7,5},{8,10},{10,8},{9,1... | collective-permute-start | bytes 1572872 | tf_op jit(solution)/shard_map/ppermute | solution.py:21

commit v5 on v3

v5 whole, which is shorter than its diff:
```python
import jax
import jax.numpy as jnp
from jax import lax
from jax.experimental import pallas as pl
from jax.experimental.pallas import tpu as pltpu
from jax.sharding import Mesh, PartitionSpec as P


SIZES = {"x": 4, "h": 2, "p": 2, "w": 4, "q": 2, "c": 2, "l": 2}
VMEM = pl.BlockSpec(memory_space=pltpu.VMEM)


def exchange(blocks, axis):
    return lax.all_to_all(blocks, axis, 0, 0, tiled=True)


def spread(block, axis):
    count = lax.axis_size(axis)
    return exchange(jnp.broadcast_to(block[None], (count,) + block.shape), axis)


def swap(tile, axis):
    return lax.ppermute(tile, axis, ((0, 1), (1, 0)))


def total(blocks):
    return jnp.sum(blocks.astype(jnp.float32), axis=0)


def masked(tile, pattern):
    width, blocks = tile.shape[0], pattern.shape[0]
    span = width // blocks
    mask = jnp.broadcast_to(pattern[:, None, :, None], (blocks, span, blocks, span))
    return tile * mask.reshape(width, width).astype(tile.dtype)


def product_kernel(place_ref, left_ref, *refs):
    tiles, lower, out_ref = refs[:4], refs[4:8], refs[8]
    width = tiles[0].shape[0]
    share = out_ref.shape[2]
    left = left_ref[:, :width]
    right = left_ref[:, width:]
    place = place_ref[0]
    for k in range(4):
        part = jnp.dot(left, tiles[k][...], preferred_element_type=jnp.float32)
        part += jnp.dot(right, lower[k][...], preferred_element_type=jnp.float32)
        part = part.astype(out_ref.dtype).reshape(-1, share, width)
        out_ref[:, lax.bitwise_xor(place, k)] = part


def product(place, left, tiles, lower, share):
    rows, width = left.shape[0], tiles[0].shape[0]
    return pl.pallas_call(
        product_kernel,
        out_shape=jax.ShapeDtypeStruct((rows // share, 4, share, width), left.dtype),
        in_specs=[pl.BlockSpec(memory_space=pltpu.SMEM)] + [VMEM] * 9,
        out_specs=VMEM,
        compiler_params=pltpu.CompilerParams(vmem_limit_bytes=16 << 20),
        cost_estimate=pl.CostEstimate(
            flops=16 * rows * width * width,
            bytes_accessed=20 * width * width,
            transcendentals=0,
        ),
    )(place, left, *tiles, *lower)


def step(x_tiles, pattern):
    half = jnp.bfloat16
    width = x_tiles.shape[1]
    share = width // 64
    nx = lax.axis_size("x")
    first = lax.axis_index("c") == 0
    tile = masked(x_tiles[0], pattern[0])
    own = lax.dynamic_slice_in_dim(tile, lax.axis_index("l") * 8 * share, 8 * share, 0)

    parts = own.reshape(2, 2, 2, share, width).transpose(0, 2, 1, 3, 4)
    parts = jnp.broadcast_to(
        parts.reshape(1, 4, 2 * share, width), (2, 4, 2 * share, width)
    )
    parts = exchange(parts.reshape(8, 2 * share, width), ("h", "p", "c"))
    parts = parts.reshape(4, 2, 2, share, width)
    left, right = parts[:, 0], parts[:, 1]
    rows = jnp.concatenate(
        [jnp.where(first, left, right), jnp.where(first, right, left)], axis=3
    )
    rows = rows.transpose(1, 0, 2, 3).reshape(8 * share, 2 * width)
    rows = spread(rows, "x").reshape(-1, 2 * width)

    below = swap(tile, "p")
    along = swap(tile, "q")
    corner = swap(along, "p")
    beside = swap(tile, "c")
    below_beside = swap(below, "c")
    tiles = [tile, beside, along, swap(along, "c")]
    lower = [below, below_beside, corner, swap(corner, "c")]

    block = jnp.concatenate(
        [
            jnp.concatenate([tile, beside], axis=1),
            jnp.concatenate([below, below_beside], axis=1),
        ],
        axis=0,
    )
    partial = lax.dot_general(
        rows, block, (((1,), (1,)), ((), ())), preferred_element_type=jnp.float32
    ).astype(half)
    partial = partial.reshape(2 * lax.axis_size("w"), -1, 2 * width)
    squared = total(exchange(partial, ("w", "q"))).astype(half)
    squared = spread(squared, "w").reshape(-1, 2 * width)
    place = lax.axis_index("q") * 2 + lax.axis_index("c")
    parts = product(place.reshape(1), squared, tiles, lower, share)
    parts = parts.reshape(16 * nx, share, width)
    parts = exchange(parts, ("x", "h", "p", "q", "c"))
    cubed = total(parts.reshape(2 * nx, 8 * share, width))
    signed = 1.5 * own.astype(jnp.float32) - 0.5 * cubed
    return signed.astype(half)[None]


def solution(mesh, sizes=SIZES):
    fine = Mesh(mesh.devices.reshape(tuple(sizes.values())), tuple(sizes))
    grid = ("x", "h", "p", "w", "q", "c")
    specs = (P(grid, None, None), P(grid, None, None))
    return jax.shard_map(
        step, mesh=fine, in_specs=specs, out_specs=P(grid, "l", None), check_vma=False
    )
```

time: 109 us -> 114 us (1.046)
  blocking collectives: 67.2 us -> 23.2 us
  starting transfers between devices: 21 us -> 52 us
  waiting for transfers between devices: 14.3 us -> 28 us
  Pallas kernels: 0 us -> 1.92 us
    all_to_all x3 -> x1, blocking collectives: 67.2 us -> 23.2 us  [exchange(): return lax.all_to_all(blocks, axis, 0, 0, tiled=True)]
    all_to_all x2 -> x4, starting transfers between devices: 12 us -> 28.7 us  [exchange(): return lax.all_to_all(blocks, axis, 0, 0, tiled=True)]
    ppermute x3 -> x7, starting transfers between devices: 8.97 us -> 23.3 us  [swap(): return lax.ppermute(tile, axis, ((0, 1), (1, 0)))]
    ppermute x3 -> x7, waiting for transfers between devices: 0.01 us -> 7.78 us  [swap(): return lax.ppermute(tile, axis, ((0, 1), (1, 0)))]
    all_to_all x2 -> x4, waiting for transfers between devices: 14.3 us -> 20.2 us  [exchange(): return lax.all_to_all(blocks, axis, 0, 0, tiled=True)]
    pallas_call x0 -> x1, Pallas kernels: none -> 1.92 us  [product(): pl.pallas_call(product_kernel, out_shape=jax.ShapeDtypeStruct((rows // sh...]
  transfers between devices with their start and end apart: 5 -> 11, of which waited for: 2 -> 4; matrix products, arithmetic and copies ran while one was open for 1% -> 4% of each run, Pallas kernels for 0% -> 0%
where the time goes in v5:
time: 114 us; the launch traced here: 113 us
  starting transfers between devices  52 us (46%)
  waiting for transfers between devices  28 us (25%)
  blocking collectives  23.2 us (20%)
  local copies, waits for them, and re-layouts  3.5 us (3%)
  other arithmetic  2.63 us (2%)
  Pallas kernels  1.92 us (2%)
  matrix products  1.54 us (1%)
    all_to_all x4, starting transfers between devices, exchange(): return lax.all_to_all(blocks, axis, 0, 0, tiled=True)  28.7 us
    ppermute x7, starting transfers between devices, swap(): return lax.ppermute(tile, axis, ((0, 1), (1, 0)))  23.3 us
    all_to_all x1, blocking collectives, exchange(): return lax.all_to_all(blocks, axis, 0, 0, tiled=True)  23.2 us
    all_to_all x4, waiting for transfers between devices, exchange(): return lax.all_to_all(blocks, axis, 0, 0, tiled=True)  20.2 us
    ppermute x7, waiting for transfers between devices, swap(): return lax.ppermute(tile, axis, ((0, 1), (1, 0)))  7.78 us
  transfers between devices with their start and end apart: 11, of which 4 were waited for; matrix products, arithmetic and copies ran while one was open for 4% of the time, Pallas kernels for 0%

profile of v5, /device:TPU:1, one launch (start us, length us, event | category | flops | bytes accessed | tf_op | source)
XLA Modules:
  0.0 113.0 jit_solution(8009384625945906736)
XLA Ops:
  0.0 0.7 convert_bitcast_fusion
  0.7 0.2 broadcast_in_dim.28
  0.9 0.0 copy-start
  0.9 0.6 convert_element_type.29
  1.5 0.4 copy-done
  1.9 0.1 bitcast_multiply_fusion.refs_0_
  2.0 4.0 %collective-permute-start.1 = (bf16[512,512]{1,0:T(8,128)(2,1)S(1)}, bf16[512,512]{1,0:T(8,128)(2,1)S(1)}, u32[]{:S(2)}, u32[]{:S(2)}) collective-permute-start(bf16[512,512]{1,0:T(8,128)(2,1)S(1)} %bitcast_multiply_fusion.refs_0_), channel_id=1, source_target_pairs={{0,32},{32,0},{1,33},{33,1},{2,34},{34,2},{3,35},{35,3},{4,36},{36... | collective-permute-start | bytes 1572872 | tf_op jit(solution)/shard_map/ppermute | solution.py:23
  6.1 0.7 broadcast_in_dim.30
  6.7 8.0 %all-to-all-start = ((bf16[8,16,512]{2,1,0:T(8,128)(2,1)}), bf16[8,16,512]{2,1,0:T(8,128)(2,1)S(1)}, u32[]{:S(2)}, u32[]{:S(2)}) async-start(bf16[8,16,512]{2,1,0:T(8,128)(2,1)} %bitcast.6), calls=%async_computation | async-start | bytes 262144 | tf_op jit(solution)/shard_map/all_to_all | solution.py:14
  14.8 2.0 %collective-permute-start = (bf16[512,512]{1,0:T(8,128)(2,1)S(1)}, bf16[512,512]{1,0:T(8,128)(2,1)S(1)}, u32[]{:S(2)}, u32[]{:S(2)}) collective-permute-start(bf16[512,512]{1,0:T(8,128)(2,1)S(1)} %bitcast_multiply_fusion.refs_0_), channel_id=1, source_target_pairs={{0,2},{2,0},{1,3},{3,1},{4,6},{6,4},{5,7},{7,5},{8,10},{10,8},{9,1... | collective-permute-start | bytes 1572872 | tf_op jit(solution)/shard_map/ppermute | solution.py:23
  16.8 5.0 %all-to-all-done = bf16[8,16,512]{2,1,0:T(8,128)(2,1)S(1)} async-done(((bf16[8,16,512]{2,1,0:T(8,128)(2,1)}), bf16[8,16,512]{2,1,0:T(8,128)(2,1)S(1)}, u32[]{:S(2)}, u32[]{:S(2)}) %all-to-all-start) | async-done | bytes 131104 | tf_op jit(solution)/shard_map/all_to_all | solution.py:14
  21.8 0.0 collective-permute-done.1.refs_4_
  21.8 2.9 %collective-permute-start.2 = (bf16[512,512]{1,0:T(8,128)(2,1)S(1)}, bf16[512,512]{1,0:T(8,128)(2,1)S(1)}, u32[]{:S(2)}, u32[]{:S(2)}) collective-permute-start(bf16[512,512]{1,0:T(8,128)(2,1)S(1)} %collective-permute-done.1.refs_4_), channel_id=1, source_target_pairs={{0,2},{2,0},{1,3},{3,1},{4,6},{6,4},{5,7},{7,5},{8,10},{10,8},{9,1... | collective-permute-start | bytes 1572872 | tf_op jit(solution)/shard_map/ppermute | solution.py:23
  24.8 0.9 broadcast_in_dim.32
  25.7 4.0 %all-to-all-start.1 = ((bf16[4,64,1024]{2,1,0:T(8,128)(2,1)}), bf16[4,64,1024]{2,1,0:T(8,128)(2,1)S(1)}, u32[]{:S(2)}, u32[]{:S(2)}) async-start(bf16[4,64,1024]{2,1,0:T(8,128)(2,1)} %broadcast_in_dim.32), calls=%async_computation.1 | async-start | bytes 1048576 | tf_op jit(solution)/shard_map/all_to_all | solution.py:14
  29.7 4.0 %collective-permute-start.3 = (bf16[512,512]{1,0:T(8,128)(2,1)S(1)}, bf16[512,512]{1,0:T(8,128)(2,1)S(1)}, u32[]{:S(2)}, u32[]{:S(2)}) collective-permute-start(bf16[512,512]{1,0:T(8,128)(2,1)S(1)} %bitcast_multiply_fusion.refs_0_), channel_id=1, source_target_pairs={{0,4},{4,0},{1,5},{5,1},{2,6},{6,2},{3,7},{7,3},{8,12},{12,8},{9,1... | collective-permute-start | bytes 1572872 | tf_op jit(solution)/shard_map/ppermute | solution.py:23
  33.7 0.0 collective-permute-done.refs_1_
  33.7 5.3 %all-to-all-done.1 = bf16[4,64,1024]{2,1,0:T(8,128)(2,1)S(1)} async-done(((bf16[4,64,1024]{2,1,0:T(8,128)(2,1)}), bf16[4,64,1024]{2,1,0:T(8,128)(2,1)S(1)}, u32[]{:S(2)}, u32[]{:S(2)}) %all-to-all-start.1) | async-done | bytes 524320 | tf_op jit(solution)/shard_map/all_to_all | solution.py:14
  39.0 0.0 collective-permute-done.2.refs_5_
  39.0 1.5 %fusion.8 = bf16[256,1024]{1,0:T(8,128)(2,1)} fusion(bf16[256,1024]{1,0:T(8,128)(2,1)S(1)} %bitcast.49, bf16[512,512]{1,0:T(8,128)(2,1)S(1)} %collective-permute-done.2.refs_5_, bf16[512,512]{1,0:T(8,128)(2,1)S(1)} %collective-permute-done.1.refs_4_, bf16[512,512]{1,0:T(8,128)(2,1)S(1)} %collective-permute-done.refs_1_, ...), kind=kOutput, calls=%fused_computation.8 | convolution fusion | flops 545521664 | bytes 3145728 | tf_op jit(solution)/shard_map/dot_general | solution.py:104
  40.5 10.0 %all-to-all-start.2 = ((bf16[8,32,1024]{2,1,0:T(8,128)(2,1)}), bf16[8,32,1024]{2,1,0:T(8,128)(2,1)}, u32[]{:S(2)}, u32[]{:S(2)}) async-start(bf16[8,32,1024]{2,1,0:T(8,128)(2,1)} %bitcast.16), calls=%async_computation.2 | async-start | bytes 1048576 | tf_op jit(solution)/shard_map/all_to_all | solution.py:14
  50.6 0.0 collective-permute-done.3.refs_2_
  50.6 2.5 %collective-permute-start.5 = (bf16[512,512]{1,0:T(8,128)(2,1)S(1)}, bf16[512,512]{1,0:T(8,128)(2,1)S(1)}, u32[]{:S(2)}, u32[]{:S(2)}) collective-permute-start(bf16[512,512]{1,0:T(8,128)(2,1)S(1)} %collective-permute-done.3.refs_2_), channel_id=1, source_target_pairs={{0,32},{32,0},{1,33},{33,1},{2,34},{34,2},{3,35},{35,3},{4,36},{36... | collective-permute-start | bytes 1572872 | tf_op jit(solution)/shard_map/ppermute | solution.py:23
  53.1 3.6 %collective-permute-start.4 = (bf16[512,512]{1,0:T(8,128)(2,1)S(1)}, bf16[512,512]{1,0:T(8,128)(2,1)}, u32[]{:S(2)}, u32[]{:S(2)}) collective-permute-start(bf16[512,512]{1,0:T(8,128)(2,1)S(1)} %collective-permute-done.3.refs_2_), channel_id=1, source_target_pairs={{0,2},{2,0},{1,3},{3,1},{4,6},{6,4},{5,7},{7,5},{8,10},{10,8},{9,1... | collective-permute-start | bytes 1572872 | tf_op jit(solution)/shard_map/ppermute | solution.py:23
  56.8 7.8 %collective-permute-done.5.refs_6_ = bf16[512,512]{1,0:T(8,128)(2,1)S(1)} collective-permute-done((bf16[512,512]{1,0:T(8,128)(2,1)S(1)}, bf16[512,512]{1,0:T(8,128)(2,1)S(1)}, u32[]{:S(2)}, u32[]{:S(2)}) %collective-permute-start.5) | collective-permute-done | bytes 524320 | tf_op jit(solution)/shard_map/ppermute | solution.py:23
  64.5 4.2 %collective-permute-start.6 = (bf16[512,512]{1,0:T(8,128)(2,1)S(1)}, bf16[512,512]{1,0:T(8,128)(2,1)}, u32[]{:S(2)}, u32[]{:S(2)}) collective-permute-start(bf16[512,512]{1,0:T(8,128)(2,1)S(1)} %collective-permute-done.5.refs_6_), channel_id=1, source_target_pairs={{0,2},{2,0},{1,3},{3,1},{4,6},{6,4},{5,7},{7,5},{8,10},{10,8},{9,1... | collective-permute-start | bytes 1572872 | tf_op jit(solution)/shard_map/ppermute | solution.py:23
  68.7 0.0 all-to-all-done.2
  68.7 1.1 reduce_sum.21
  69.8 0.7 broadcast_in_dim.33
  70.6 6.6 %all-to-all-start.3 = ((bf16[4,32,1024]{2,1,0:T(8,128)(2,1)}), bf16[4,32,1024]{2,1,0:T(8,128)(2,1)S(1)}, u32[]{:S(2)}, u32[]{:S(2)}) async-start(bf16[4,32,1024]{2,1,0:T(8,128)(2,1)} %broadcast_in_dim.33), calls=%async_computation.3 | async-start | bytes 524288 | tf_op jit(solution)/shard_map/all_to_all | solution.py:14
  77.2 0.0 collective-permute-done.4.refs_3_
  77.2 0.0 collective-permute-done.6.refs_7_
  77.2 9.9 %all-to-all-done.3 = bf16[4,32,1024]{2,1,0:T(8,128)(2,1)S(1)} async-done(((bf16[4,32,1024]{2,1,0:T(8,128)(2,1)}), bf16[4,32,1024]{2,1,0:T(8,128)(2,1)S(1)}, u32[]{:S(2)}, u32[]{:S(2)}) %all-to-all-start.3) | async-done | bytes 262176 | tf_op jit(solution)/shard_map/all_to_all | solution.py:14
  87.1 1.9 %shard_map.28 = bf16[16,4,8,512]{3,2,1,0:T(8,128)(2,1)S(1)} custom-call(s32[1]{0:T(128)} %bitcast.2.place_ref, bf16[128,1024]{1,0:T(8,128)(2,1)S(1)} %bitcast.44, bf16[512,512]{1,0:T(8,128)(2,1)S(1)} %bitcast_multiply_fusion.refs_0_, bf16[512,512]{1,0:T(8,128)(2,1)S(1)} %collective-permute-done.refs_1_, bf16[512,512]{1,0:T(8,128)(2,1)S(1)} %collective-permute-done.3.refs_2_, ...), custom_call_target="tpu_custom_call" | custom-call | flops 536870912 | bytes 5242880 | tf_op jit(solution)/shard_map/pallas_call | solution.py:53
  89.0 23.2 %all_to_all.25 = bf16[64,8,512]{2,1,0:T(8,128)(2,1)S(1)} all-to-all(bf16[64,8,512]{2,1,0:T(8,128)(2,1)S(1)} %bitcast.43), channel_id=1, replica_groups=mesh['x'=4,'h'=2,'p'=2,'w'=4,'q'=2,'c'=2,'l'=2] {'x','h','p','q','c'}, dimensions={0} | all-to-all | bytes 1048576 | tf_op jit(solution)/shard_map/all_to_all | solution.py:14
  112.3 0.1 convert_reduce_fusion
  112.3 0.7 fusion.12
  (6 shorter events, 0.1 us)
Async XLA Ops:
  0.9 1.0 copy-start
  2.0 19.8 %collective-permute-start.1 = (bf16[512,512]{1,0:T(8,128)(2,1)S(1)}, bf16[512,512]{1,0:T(8,128)(2,1)S(1)}, u32[]{:S(2)}, u32[]{:S(2)}) collective-permute-start(bf16[512,512]{1,0:T(8,128)(2,1)S(1)} %bitcast_multiply_fusion.refs_0_), channel_id=1, source_target_pairs={{0,32},{32,0},{1,33},{33,1},{2,34},{34,2},{3,35},{35,3},{4,36},{36... | collective-permute-start | bytes 1572872 | tf_op jit(solution)/shard_map/ppermute | solution.py:23
  6.7 15.1 %all-to-all-start = ((bf16[8,16,512]{2,1,0:T(8,128)(2,1)}), bf16[8,16,512]{2,1,0:T(8,128)(2,1)S(1)}, u32[]{:S(2)}, u32[]{:S(2)}) async-start(bf16[8,16,512]{2,1,0:T(8,128)(2,1)} %bitcast.6), calls=%async_computation | async-start | bytes 262144 | tf_op jit(solution)/shard_map/all_to_all | solution.py:14
  14.8 18.9 %collective-permute-start = (bf16[512,512]{1,0:T(8,128)(2,1)S(1)}, bf16[512,512]{1,0:T(8,128)(2,1)S(1)}, u32[]{:S(2)}, u32[]{:S(2)}) collective-permute-start(bf16[512,512]{1,0:T(8,128)(2,1)S(1)} %bitcast_multiply_fusion.refs_0_), channel_id=1, source_target_pairs={{0,2},{2,0},{1,3},{3,1},{4,6},{6,4},{5,7},{7,5},{8,10},{10,8},{9,1... | collective-permute-start | bytes 1572872 | tf_op jit(solution)/shard_map/ppermute | solution.py:23
  21.8 17.2 %collective-permute-start.2 = (bf16[512,512]{1,0:T(8,128)(2,1)S(1)}, bf16[512,512]{1,0:T(8,128)(2,1)S(1)}, u32[]{:S(2)}, u32[]{:S(2)}) collective-permute-start(bf16[512,512]{1,0:T(8,128)(2,1)S(1)} %collective-permute-done.1.refs_4_), channel_id=1, source_target_pairs={{0,2},{2,0},{1,3},{3,1},{4,6},{6,4},{5,7},{7,5},{8,10},{10,8},{9,1... | collective-permute-start | bytes 1572872 | tf_op jit(solution)/shard_map/ppermute | solution.py:23
  25.7 13.3 %all-to-all-start.1 = ((bf16[4,64,1024]{2,1,0:T(8,128)(2,1)}), bf16[4,64,1024]{2,1,0:T(8,128)(2,1)S(1)}, u32[]{:S(2)}, u32[]{:S(2)}) async-start(bf16[4,64,1024]{2,1,0:T(8,128)(2,1)} %broadcast_in_dim.32), calls=%async_computation.1 | async-start | bytes 1048576 | tf_op jit(solution)/shard_map/all_to_all | solution.py:14
  29.7 20.9 %collective-permute-start.3 = (bf16[512,512]{1,0:T(8,128)(2,1)S(1)}, bf16[512,512]{1,0:T(8,128)(2,1)S(1)}, u32[]{:S(2)}, u32[]{:S(2)}) collective-permute-start(bf16[512,512]{1,0:T(8,128)(2,1)S(1)} %bitcast_multiply_fusion.refs_0_), channel_id=1, source_target_pairs={{0,4},{4,0},{1,5},{5,1},{2,6},{6,2},{3,7},{7,3},{8,12},{12,8},{9,1... | collective-permute-start | bytes 1572872 | tf_op jit(solution)/shard_map/ppermute | solution.py:23
  40.5 28.2 %all-to-all-start.2 = ((bf16[8,32,1024]{2,1,0:T(8,128)(2,1)}), bf16[8,32,1024]{2,1,0:T(8,128)(2,1)}, u32[]{:S(2)}, u32[]{:S(2)}) async-start(bf16[8,32,1024]{2,1,0:T(8,128)(2,1)} %bitcast.16), calls=%async_computation.2 | async-start | bytes 1048576 | tf_op jit(solution)/shard_map/all_to_all | solution.py:14
  50.6 13.9 %collective-permute-start.5 = (bf16[512,512]{1,0:T(8,128)(2,1)S(1)}, bf16[512,512]{1,0:T(8,128)(2,1)S(1)}, u32[]{:S(2)}, u32[]{:S(2)}) collective-permute-start(bf16[512,512]{1,0:T(8,128)(2,1)S(1)} %collective-permute-done.3.refs_2_), channel_id=1, source_target_pairs={{0,32},{32,0},{1,33},{33,1},{2,34},{34,2},{3,35},{35,3},{4,36},{36... | collective-permute-start | bytes 1572872 | tf_op jit(solution)/shard_map/ppermute | solution.py:23
  53.1 24.1 %collective-permute-start.4 = (bf16[512,512]{1,0:T(8,128)(2,1)S(1)}, bf16[512,512]{1,0:T(8,128)(2,1)}, u32[]{:S(2)}, u32[]{:S(2)}) collective-permute-start(bf16[512,512]{1,0:T(8,128)(2,1)S(1)} %collective-permute-done.3.refs_2_), channel_id=1, source_target_pairs={{0,2},{2,0},{1,3},{3,1},{4,6},{6,4},{5,7},{7,5},{8,10},{10,8},{9,1... | collective-permute-start | bytes 1572872 | tf_op jit(solution)/shard_map/ppermute | solution.py:23
  64.5 12.7 %collective-permute-start.6 = (bf16[512,512]{1,0:T(8,128)(2,1)S(1)}, bf16[512,512]{1,0:T(8,128)(2,1)}, u32[]{:S(2)}, u32[]{:S(2)}) collective-permute-start(bf16[512,512]{1,0:T(8,128)(2,1)S(1)} %collective-permute-done.5.refs_6_), channel_id=1, source_target_pairs={{0,2},{2,0},{1,3},{3,1},{4,6},{6,4},{5,7},{7,5},{8,10},{10,8},{9,1... | collective-permute-start | bytes 1572872 | tf_op jit(solution)/shard_map/ppermute | solution.py:23
  70.6 16.5 %all-to-all-start.3 = ((bf16[4,32,1024]{2,1,0:T(8,128)(2,1)}), bf16[4,32,1024]{2,1,0:T(8,128)(2,1)S(1)}, u32[]{:S(2)}, u32[]{:S(2)}) async-start(bf16[4,32,1024]{2,1,0:T(8,128)(2,1)} %broadcast_in_dim.33), calls=%async_computation.3 | async-start | bytes 524288 | tf_op jit(solution)/shard_map/all_to_all | solution.py:14

commit v6 on v5

v6 whole, which is shorter than its diff:
```python
import jax
import jax.numpy as jnp
from jax import lax
from jax.experimental import pallas as pl
from jax.experimental.pallas import tpu as pltpu
from jax.sharding import Mesh, PartitionSpec as P


SIZES = {"x": 4, "h": 2, "p": 2, "w": 4, "q": 2, "c": 2, "l": 2}
VMEM = pl.BlockSpec(memory_space=pltpu.VMEM)


def exchange(blocks, axis):
    return lax.all_to_all(blocks, axis, 0, 0, tiled=True)


def ring(block, axis):
    count = lax.axis_size(axis)
    got = {0: block}
    for far in sorted(range(1, count), key=lambda d: -min(d, count - d)):
        route = [(i, (i - far) % count) for i in range(count)]
        got[far] = lax.ppermute(block, axis, route)
    return [got[d] for d in range(count)]


def swap(tile, axis):
    return lax.ppermute(tile, axis, ((0, 1), (1, 0)))


def total(blocks):
    return jnp.sum(blocks.astype(jnp.float32), axis=0)


def mask_kernel(layer_ref, tile_ref, pattern_ref, out_ref, parts_ref):
    width = tile_ref.shape[1]
    blocks = pattern_ref.shape[1]
    span, share = width // blocks, width // 64
    number = lax.broadcasted_iota(jnp.int32, (blocks, width), 0)
    place = lax.broadcasted_iota(jnp.int32, (blocks, width), 1)
    inside = (place >= number * span) & (place < number * span + span)
    wide = jnp.dot(
        pattern_ref[0].astype(jnp.float32),
        inside.astype(jnp.float32),
        preferred_element_type=jnp.float32,
    )
    for k in range(blocks):
        rows = pl.ds(k * span, span)
        kept = tile_ref[0, rows, :].astype(jnp.float32) * wide[k : k + 1]
        out_ref[rows, :] = kept.astype(out_ref.dtype)
    first = layer_ref[0] * (8 * share)
    for k in range(8):
        p, q, c = k // 4, k // 2 % 2, k % 2
        start = pl.multiple_of(first + k * share, share)
        piece = out_ref[pl.ds(start, share), :]
        for h in range(2):
            parts_ref[4 * h + 2 * p + c, pl.ds(q * share, share), :] = piece


def masked(layer, tile, pattern):
    width = tile.shape[1]
    return pl.pallas_call(
        mask_kernel,
        out_shape=(
            jax.ShapeDtypeStruct((width, width), tile.dtype),
            jax.ShapeDtypeStruct((8, width // 32, width), tile.dtype),
        ),
        in_specs=[pl.BlockSpec(memory_space=pltpu.SMEM), VMEM, VMEM],
        out_specs=(VMEM, VMEM),
        compiler_params=pltpu.CompilerParams(vmem_limit_bytes=8 << 20),
        name="mask",
    )(layer, tile, pattern)


def first_kernel(*refs):
    count = len(refs) - 6
    chunks, tiles, out_ref, rows_ref = refs[:count], refs[count : count + 4], refs[-2], refs[-1]
    width = tiles[0].shape[0]
    height = chunks[0].shape[0]
    for k in range(count):
        rows_ref[pl.ds(k * height, height), :] = chunks[k][...]
    turned = (((1,), (1,)), ((), ()))
    left, right = rows_ref[:, :width], rows_ref[:, width:]
    for k in range(2):
        part = lax.dot_general(
            left, tiles[2 * k][...], turned, preferred_element_type=jnp.float32
        )
        part += lax.dot_general(
            right, tiles[2 * k + 1][...], turned, preferred_element_type=jnp.float32
        )
        out_ref[:, k * width : (k + 1) * width] = part.astype(out_ref.dtype)


def first_product(chunks, tiles):
    width = tiles[0].shape[0]
    shape = (len(chunks) * chunks[0].shape[0], 2 * width)
    return pl.pallas_call(
        first_kernel,
        out_shape=jax.ShapeDtypeStruct(shape, tiles[0].dtype),
        in_specs=[VMEM] * (len(chunks) + 4),
        out_specs=VMEM,
        scratch_shapes=[pltpu.VMEM(shape, tiles[0].dtype)],
        compiler_params=pltpu.CompilerParams(vmem_limit_bytes=16 << 20),
        name="first",
    )(*chunks, *tiles)


def second_kernel(place_ref, *refs):
    count = len(refs) - 10
    chunks, tiles, lower = refs[:count], refs[count : count + 4], refs[count + 4 : count + 8]
    out_ref, rows_ref = refs[-2], refs[-1]
    width = tiles[0].shape[0]
    height = chunks[0].shape[0]
    for k in range(count):
        rows_ref[pl.ds(k * height, height), :] = chunks[k][...]
    left, right = rows_ref[:, :width], rows_ref[:, width:]
    for k in range(4):
        part = jnp.dot(left, tiles[k][...], preferred_element_type=jnp.float32)
        part += jnp.dot(right, lower[k][...], preferred_element_type=jnp.float32)
        part = part.astype(out_ref.dtype)
        column = lax.bitwise_xor(place_ref[0], k)
        for e in range(count):
            piece = part[e * height : (e + 1) * height]
            piece = piece.reshape(out_ref.shape[1], out_ref.shape[3], width)
            out_ref[lax.rem(place_ref[1] + e, count), :, column] = piece


def second_product(place, chunks, tiles, lower, share):
    count, (height, width) = len(chunks), chunks[0].shape
    half = chunks[0].dtype
    return pl.pallas_call(
        second_kernel,
        out_shape=jax.ShapeDtypeStruct((count, height // share, 4, share, width // 2), half),
        in_specs=[pl.BlockSpec(memory_space=pltpu.SMEM)] + [VMEM] * (count + 8),
        out_specs=VMEM,
        scratch_shapes=[pltpu.VMEM((count * height, width), half)],
        compiler_params=pltpu.CompilerParams(vmem_limit_bytes=16 << 20),
        name="second",
    )(place, *chunks, *tiles, *lower)


def step(x_tiles, pattern):
    half = jnp.bfloat16
    width = x_tiles.shape[1]
    share = width // 64
    nx = lax.axis_size("x")
    first = lax.axis_index("c") == 0
    layer = lax.axis_index("l")
    tile, parts = masked(layer.reshape(1), x_tiles, pattern)
    own = lax.dynamic_slice_in_dim(tile, layer * 8 * share, 8 * share, 0)
    parts = exchange(parts, ("h", "p", "c"))
    parts = parts.reshape(4, 2, 2, share, width)
    left, right = parts[:, 0], parts[:, 1]
    rows = jnp.concatenate(
        [jnp.where(first, left, right), jnp.where(first, right, left)], axis=3
    )
    rows = rows.transpose(1, 0, 2, 3).reshape(8 * share, 2 * width)
    rows = ring(rows, "x")

    below = swap(tile, "p")
    along = swap(tile, "q")
    corner = swap(along, "p")
    beside = swap(tile, "c")
    below_beside = swap(below, "c")
    tiles = [tile, beside, along, swap(along, "c")]
    lower = [below, below_beside, corner, swap(corner, "c")]

    partial = first_product(rows, [tile, beside, below, below_beside])
    partial = partial.reshape(2 * nx, -1, 2 * width)
    squared = total(exchange(partial, ("w", "q"))).astype(half)
    squared = ring(squared, "w")
    turn = lax.rem(lax.axis_index("x") + lax.axis_index("w"), nx)
    place = jnp.stack([lax.axis_index("q") * 2 + lax.axis_index("c"), turn])
    parts = second_product(place.astype(jnp.int32), squared, tiles, lower, share)
    parts = parts.reshape(16 * nx, share, width)
    parts = exchange(parts, ("x", "h", "p", "q", "c"))
    cubed = total(parts.reshape(2 * nx, 8 * share, width))
    signed = 1.5 * own.astype(jnp.float32) - 0.5 * cubed
    return signed.astype(half)[None]


def solution(mesh, sizes=SIZES):
    fine = Mesh(mesh.devices.reshape(tuple(sizes.values())), tuple(sizes))
    grid = ("x", "h", "p", "w", "q", "c")
    specs = (P(grid, None, None), P(grid, None, None))
    return jax.shard_map(
        step, mesh=fine, in_specs=specs, out_specs=P(grid, "l", None), check_vma=False
    )
```

time: 114 us -> 114 us (level)
  blocking collectives: 23.2 us -> 0 us
  waiting for transfers between devices: 28 us -> 40.4 us
  starting transfers between devices: 52 us -> 63.6 us
  Pallas kernels: 1.92 us -> 5.19 us
  local copies, waits for them, and re-layouts: 3.5 us -> 1.74 us
  matrix products: 1.54 us -> 0 us
    all_to_all x1 -> x0, blocking collectives: 23.2 us -> none  [exchange(): return lax.all_to_all(blocks, axis, 0, 0, tiled=True)]
    ppermute x0 -> x6, starting transfers between devices: none -> 18.5 us  [ring(): got[far] = lax.ppermute(block, axis, route)]
    all_to_all x4 -> x3, waiting for transfers between devices: 20.2 us -> 30.9 us  [exchange(): return lax.all_to_all(blocks, axis, 0, 0, tiled=True)]
    ppermute x0 -> x6, waiting for transfers between devices: none -> 9.41 us  [ring(): got[far] = lax.ppermute(block, axis, route)]
    ppermute x7, waiting for transfers between devices: 7.78 us -> 0.02 us  [swap(): return lax.ppermute(tile, axis, ((0, 1), (1, 0)))]
    ppermute x7, starting transfers between devices: 23.3 us -> 19 us  [swap(): return lax.ppermute(tile, axis, ((0, 1), (1, 0)))]
    pallas_call x1 -> x3, Pallas kernels: 1.92 us -> 5.19 us  [the longest x1 2.75 us: second_product(): pl.pallas_call(second_kernel, out_shape=jax.ShapeDtypeStruct((count, heig...]
    all_to_all x4 -> x3, starting transfers between devices: 28.7 us -> 26.1 us  [exchange(): return lax.all_to_all(blocks, axis, 0, 0, tiled=True)]
  transfers between devices with their start and end apart: 11 -> 16, of which waited for: 4 -> 7; matrix products, arithmetic and copies ran while one was open for 4% -> 1% of each run, Pallas kernels for 0% -> 1%
where the time goes in v6:
time: 114 us; the launch traced here: 113 us
  starting transfers between devices  63.6 us (56%)
  waiting for transfers between devices  40.4 us (35%)
  Pallas kernels  5.19 us (5%)
  other arithmetic  1.96 us (2%)
  local copies, waits for them, and re-layouts  1.74 us (2%)
    all_to_all x3, waiting for transfers between devices, exchange(): return lax.all_to_all(blocks, axis, 0, 0, tiled=True)  30.9 us
    all_to_all x3, starting transfers between devices, exchange(): return lax.all_to_all(blocks, axis, 0, 0, tiled=True)  26.1 us
    ppermute x7, starting transfers between devices, swap(): return lax.ppermute(tile, axis, ((0, 1), (1, 0)))  19 us
    ppermute x6, starting transfers between devices, ring(): got[far] = lax.ppermute(block, axis, route)  18.5 us
    ppermute x6, waiting for transfers between devices, ring(): got[far] = lax.ppermute(block, axis, route)  9.41 us
    pallas_call x1, Pallas kernels, second_product(): pl.pallas_call(second_kernel, out_shape=jax.ShapeDtypeStruct((count, heig...  2.75 us
  transfers between devices with their start and end apart: 16, of which 7 were waited for; matrix products, arithmetic and copies ran while one was open for 1% of the time, Pallas kernels for 1%

profile of v6, /device:TPU:1, one launch (start us, length us, event | category | flops | bytes accessed | tf_op | source)
XLA Modules:
  0.0 113.1 jit_solution(8743359881669227897)
XLA Ops:
  0.0 0.0 copy-start.1
  0.0 0.7 copy-done.1
  0.7 0.0 copy-start
  0.7 1.0 copy-done
  1.7 0.9 mask.1
  2.6 4.0 %collective-permute-start.4 = (bf16[512,512]{1,0:T(8,128)(2,1)S(1)}, bf16[512,512]{1,0:T(8,128)(2,1)S(1)}, u32[]{:S(2)}, u32[]{:S(2)}) collective-permute-start(bf16[512,512]{1,0:T(8,128)(2,1)S(1)} %get-tuple-element.7.refs_4_), channel_id=1, source_target_pairs={{0,32},{32,0},{1,33},{33,1},{2,34},{34,2},{3,35},{35,3},{4,36},{36... | collective-permute-start | bytes 1572872 | tf_op jit(solution)/shard_map/ppermute | solution.py:27
  6.6 8.0 %all-to-all-start = ((bf16[8,16,512]{2,1,0:T(8,128)(2,1)}), bf16[8,16,512]{2,1,0:T(8,128)(2,1)S(1)}, u32[]{:S(2)}, u32[]{:S(2)}) async-start(bf16[8,16,512]{2,1,0:T(8,128)(2,1)} %get-tuple-element.8), calls=%async_computation | async-start | bytes 262144 | tf_op jit(solution)/shard_map/all_to_all | solution.py:14
  14.7 2.0 %collective-permute-start.3 = (bf16[512,512]{1,0:T(8,128)(2,1)S(1)}, bf16[512,512]{1,0:T(8,128)(2,1)S(1)}, u32[]{:S(2)}, u32[]{:S(2)}) collective-permute-start(bf16[512,512]{1,0:T(8,128)(2,1)S(1)} %get-tuple-element.7.refs_4_), channel_id=1, source_target_pairs={{0,2},{2,0},{1,3},{3,1},{4,6},{6,4},{5,7},{7,5},{8,10},{10,8},{9,1... | collective-permute-start | bytes 1572872 | tf_op jit(solution)/shard_map/ppermute | solution.py:27
  16.7 1.9 %collective-permute-start.9 = (bf16[512,512]{1,0:T(8,128)(2,1)S(1)}, bf16[512,512]{1,0:T(8,128)(2,1)S(1)}, u32[]{:S(2)}, u32[]{:S(2)}) collective-permute-start(bf16[512,512]{1,0:T(8,128)(2,1)S(1)} %get-tuple-element.7.refs_4_), channel_id=1, source_target_pairs={{0,4},{4,0},{1,5},{5,1},{2,6},{6,2},{3,7},{7,3},{8,12},{12,8},{9,1... | collective-permute-start | bytes 1572872 | tf_op jit(solution)/shard_map/ppermute | solution.py:27
  18.6 3.8 %all-to-all-done = bf16[8,16,512]{2,1,0:T(8,128)(2,1)S(1)} async-done(((bf16[8,16,512]{2,1,0:T(8,128)(2,1)}), bf16[8,16,512]{2,1,0:T(8,128)(2,1)S(1)}, u32[]{:S(2)}, u32[]{:S(2)}) %all-to-all-start) | async-done | bytes 131104 | tf_op jit(solution)/shard_map/all_to_all | solution.py:14
  22.4 0.0 collective-permute-done.4.refs_6_.refs_8_
  22.4 2.9 %collective-permute-start.5 = (bf16[512,512]{1,0:T(8,128)(2,1)S(1)}, bf16[512,512]{1,0:T(8,128)(2,1)S(1)}, u32[]{:S(2)}, u32[]{:S(2)}) collective-permute-start(bf16[512,512]{1,0:T(8,128)(2,1)S(1)} %collective-permute-done.4.refs_6_.refs_8_), channel_id=1, source_target_pairs={{0,2},{2,0},{1,3},{3,1},{4,6},{6,4},{5,7},{7,5},{8,10},{10,8},{9,1... | collective-permute-start | bytes 1572872 | tf_op jit(solution)/shard_map/ppermute | solution.py:27
  25.4 4.4 %collective-permute-start = (bf16[64,1024]{1,0:T(8,128)(2,1)S(1)}, bf16[64,1024]{1,0:T(8,128)(2,1)S(1)}, u32[]{:S(2)}, u32[]{:S(2)}) collective-permute-start(bf16[64,1024]{1,0:T(8,128)(2,1)S(1)} %bitcast.19), channel_id=1, source_target_pairs={{0,384},{128,0},{256,128},{384,256},{1,385},{129,1},{257,129},{385... | collective-permute-start | bytes 393224 | tf_op jit(solution)/shard_map/ppermute | solution.py:22
  29.8 2.4 %collective-permute-start.1 = (bf16[64,1024]{1,0:T(8,128)(2,1)S(1)}, bf16[64,1024]{1,0:T(8,128)(2,1)S(1)}, u32[]{:S(2)}, u32[]{:S(2)}) collective-permute-start(bf16[64,1024]{1,0:T(8,128)(2,1)S(1)} %bitcast.20), channel_id=1, source_target_pairs={{0,256},{128,384},{256,0},{384,128},{1,257},{129,385},{257,1},{385... | collective-permute-start | bytes 393224 | tf_op jit(solution)/shard_map/ppermute | solution.py:22
  32.3 0.4 collective-permute-done.refs_1_
  32.6 2.8 %collective-permute-start.2 = (bf16[64,1024]{1,0:T(8,128)(2,1)S(1)}, bf16[64,1024]{1,0:T(8,128)(2,1)S(1)}, u32[]{:S(2)}, u32[]{:S(2)}) collective-permute-start(bf16[64,1024]{1,0:T(8,128)(2,1)S(1)} %bitcast.21), channel_id=1, source_target_pairs={{0,128},{128,256},{256,384},{384,0},{1,129},{129,257},{257,385},{3... | collective-permute-start | bytes 393224 | tf_op jit(solution)/shard_map/ppermute | solution.py:22
  35.5 0.0 collective-permute-done.9.refs_6_
  35.5 2.5 %collective-permute-start.11 = (bf16[512,512]{1,0:T(8,128)(2,1)S(1)}, bf16[512,512]{1,0:T(8,128)(2,1)S(1)}, u32[]{:S(2)}, u32[]{:S(2)}) collective-permute-start(bf16[512,512]{1,0:T(8,128)(2,1)S(1)} %collective-permute-done.9.refs_6_), channel_id=1, source_target_pairs={{0,32},{32,0},{1,33},{33,1},{2,34},{34,2},{3,35},{35,3},{4,36},{36... | collective-permute-start | bytes 1572872 | tf_op jit(solution)/shard_map/ppermute | solution.py:27
  38.0 0.0 collective-permute-done.1.refs_2_
  38.0 2.9 %collective-permute-done.2.refs_3_ = bf16[64,1024]{1,0:T(8,128)(2,1)S(1)} collective-permute-done((bf16[64,1024]{1,0:T(8,128)(2,1)S(1)}, bf16[64,1024]{1,0:T(8,128)(2,1)S(1)}, u32[]{:S(2)}, u32[]{:S(2)}) %collective-permute-start.2) | collective-permute-done | bytes 131104 | tf_op jit(solution)/shard_map/ppermute | solution.py:22
  40.9 0.0 collective-permute-done.3.refs_5_
  40.9 0.0 collective-permute-done.5.refs_7_.refs_9_
  40.9 1.6 %first.1 = bf16[256,1024]{1,0:T(8,128)(2,1)} custom-call(bf16[64,1024]{1,0:T(8,128)(2,1)S(1)} %bitcast.22, bf16[64,1024]{1,0:T(8,128)(2,1)S(1)} %collective-permute-done.refs_1_, bf16[64,1024]{1,0:T(8,128)(2,1)S(1)} %collective-permute-done.1.refs_2_, bf16[64,1024]{1,0:T(8,128)(2,1)S(1)} %collective-permute-done.2.refs_3_, ...), custom_call_target="tpu_custom_call" | custom-call | tf_op jit(solution)/shard_map/first/pallas_call | solution.py:96
  42.5 10.0 %all-to-all-start.1 = ((bf16[8,32,1024]{2,1,0:T(8,128)(2,1)}), bf16[8,32,1024]{2,1,0:T(8,128)(2,1)}, u32[]{:S(2)}, u32[]{:S(2)}) async-start(bf16[8,32,1024]{2,1,0:T(8,128)(2,1)} %bitcast.9), calls=%async_computation.1 | async-start | bytes 1048576 | tf_op jit(solution)/shard_map/all_to_all | solution.py:14
  52.5 3.6 %collective-permute-start.10 = (bf16[512,512]{1,0:T(8,128)(2,1)S(1)}, bf16[512,512]{1,0:T(8,128)(2,1)}, u32[]{:S(2)}, u32[]{:S(2)}) collective-permute-start(bf16[512,512]{1,0:T(8,128)(2,1)S(1)} %collective-permute-done.9.refs_6_), channel_id=1, source_target_pairs={{0,2},{2,0},{1,3},{3,1},{4,6},{6,4},{5,7},{7,5},{8,10},{10,8},{9,1... | collective-permute-start | bytes 1572872 | tf_op jit(solution)/shard_map/ppermute | solution.py:27
  56.2 0.0 collective-permute-done.11.refs_10_
  56.2 1.9 %collective-permute-start.12 = (bf16[512,512]{1,0:T(8,128)(2,1)S(1)}, bf16[512,512]{1,0:T(8,128)(2,1)}, u32[]{:S(2)}, u32[]{:S(2)}) collective-permute-start(bf16[512,512]{1,0:T(8,128)(2,1)S(1)} %collective-permute-done.11.refs_10_), channel_id=1, source_target_pairs={{0,2},{2,0},{1,3},{3,1},{4,6},{6,4},{5,7},{7,5},{8,10},{10,8},{9,1... | collective-permute-start | bytes 1572872 | tf_op jit(solution)/shard_map/ppermute | solution.py:27
  58.1 10.5 %all-to-all-done.1 = bf16[8,32,1024]{2,1,0:T(8,128)(2,1)} async-done(((bf16[8,32,1024]{2,1,0:T(8,128)(2,1)}), bf16[8,32,1024]{2,1,0:T(8,128)(2,1)}, u32[]{:S(2)}, u32[]{:S(2)}) %all-to-all-start.1) | async-done | bytes 524320 | tf_op jit(solution)/shard_map/all_to_all | solution.py:14
  68.6 1.1 reduce_sum.21.refs_0_
  69.8 3.0 %collective-permute-start.6 = (bf16[32,1024]{1,0:T(8,128)(2,1)S(1)}, bf16[32,1024]{1,0:T(8,128)(2,1)S(1)}, u32[]{:S(2)}, u32[]{:S(2)}) collective-permute-start(bf16[32,1024]{1,0:T(8,128)(2,1)S(1)} %reduce_sum.21.refs_0_), channel_id=1, source_target_pairs={{0,24},{8,0},{16,8},{24,16},{1,25},{9,1},{17,9},{25,17},{2,26},{10... | collective-permute-start | bytes 196616 | tf_op jit(solution)/shard_map/ppermute | solution.py:22
  72.7 3.7 %collective-permute-start.7 = (bf16[32,1024]{1,0:T(8,128)(2,1)S(1)}, bf16[32,1024]{1,0:T(8,128)(2,1)S(1)}, u32[]{:S(2)}, u32[]{:S(2)}) collective-permute-start(bf16[32,1024]{1,0:T(8,128)(2,1)S(1)} %reduce_sum.21.refs_0_), channel_id=1, source_target_pairs={{0,16},{8,24},{16,0},{24,8},{1,17},{9,25},{17,1},{25,9},{2,18},{10... | collective-permute-start | bytes 196616 | tf_op jit(solution)/shard_map/ppermute | solution.py:22
  76.4 2.2 %collective-permute-start.8 = (bf16[32,1024]{1,0:T(8,128)(2,1)S(1)}, bf16[32,1024]{1,0:T(8,128)(2,1)S(1)}, u32[]{:S(2)}, u32[]{:S(2)}) collective-permute-start(bf16[32,1024]{1,0:T(8,128)(2,1)S(1)} %reduce_sum.21.refs_0_), channel_id=1, source_target_pairs={{0,8},{8,16},{16,24},{24,0},{1,9},{9,17},{17,25},{25,1},{2,10},{10... | collective-permute-start | bytes 196616 | tf_op jit(solution)/shard_map/ppermute | solution.py:22
  78.7 0.1 pad_add_fusion.place_ref
  78.7 0.0 collective-permute-done.10.refs_7_
  78.7 0.0 collective-permute-done.12.refs_11_
  78.7 0.0 collective-permute-done.6.refs_1_
  78.8 3.4 %collective-permute-done.7.refs_2_ = bf16[32,1024]{1,0:T(8,128)(2,1)S(1)} collective-permute-done((bf16[32,1024]{1,0:T(8,128)(2,1)S(1)}, bf16[32,1024]{1,0:T(8,128)(2,1)S(1)}, u32[]{:S(2)}, u32[]{:S(2)}) %collective-permute-start.7) | collective-permute-done | bytes 65568 | tf_op jit(solution)/shard_map/ppermute | solution.py:22
  82.2 2.7 %collective-permute-done.8.refs_3_ = bf16[32,1024]{1,0:T(8,128)(2,1)S(1)} collective-permute-done((bf16[32,1024]{1,0:T(8,128)(2,1)S(1)}, bf16[32,1024]{1,0:T(8,128)(2,1)S(1)}, u32[]{:S(2)}, u32[]{:S(2)}) %collective-permute-start.8) | collective-permute-done | bytes 65568 | tf_op jit(solution)/shard_map/ppermute | solution.py:22
  84.9 2.7 %second.1 = bf16[4,4,4,8,512]{4,3,2,1,0:T(8,128)(2,1)} custom-call(s32[2]{0:T(128)S(1)} %pad_add_fusion.place_ref, bf16[32,1024]{1,0:T(8,128)(2,1)S(1)} %reduce_sum.21.refs_0_, bf16[32,1024]{1,0:T(8,128)(2,1)S(1)} %collective-permute-done.6.refs_1_, bf16[32,1024]{1,0:T(8,128)(2,1)S(1)} %collective-permute-done.7.refs_2_, ...), custom_call_target="tpu_custom_call" | custom-call | tf_op jit(solution)/shard_map/second/pallas_call | solution.py:130
  87.6 8.1 %all-to-all-start.2 = ((bf16[64,8,512]{2,1,0:T(8,128)(2,1)}), bf16[64,8,512]{2,1,0:T(8,128)(2,1)S(1)}, u32[]{:S(2)}, u32[]{:S(2)}) async-start(bf16[64,8,512]{2,1,0:T(8,128)(2,1)} %bitcast.10), calls=%async_computation.2 | async-start | bytes 1048576 | tf_op jit(solution)/shard_map/all_to_all | solution.py:14
  95.7 16.6 %all-to-all-done.2 = bf16[64,8,512]{2,1,0:T(8,128)(2,1)S(1)} async-done(((bf16[64,8,512]{2,1,0:T(8,128)(2,1)}), bf16[64,8,512]{2,1,0:T(8,128)(2,1)S(1)}, u32[]{:S(2)}, u32[]{:S(2)}) %all-to-all-start.2) | async-done | bytes 524320 | tf_op jit(solution)/shard_map/all_to_all | solution.py:14
  112.3 0.1 convert_reduce_fusion
  112.4 0.7 fusion
  (3 shorter events, 0.0 us)
Async XLA Ops:
  0.0 0.7 copy-start.1
  0.7 1.0 copy-start
  2.6 19.8 %collective-permute-start.4 = (bf16[512,512]{1,0:T(8,128)(2,1)S(1)}, bf16[512,512]{1,0:T(8,128)(2,1)S(1)}, u32[]{:S(2)}, u32[]{:S(2)}) collective-permute-start(bf16[512,512]{1,0:T(8,128)(2,1)S(1)} %get-tuple-element.7.refs_4_), channel_id=1, source_target_pairs={{0,32},{32,0},{1,33},{33,1},{2,34},{34,2},{3,35},{35,3},{4,36},{36... | collective-permute-start | bytes 1572872 | tf_op jit(solution)/shard_map/ppermute | solution.py:27
  6.6 15.8 %all-to-all-start = ((bf16[8,16,512]{2,1,0:T(8,128)(2,1)}), bf16[8,16,512]{2,1,0:T(8,128)(2,1)S(1)}, u32[]{:S(2)}, u32[]{:S(2)}) async-start(bf16[8,16,512]{2,1,0:T(8,128)(2,1)} %get-tuple-element.8), calls=%async_computation | async-start | bytes 262144 | tf_op jit(solution)/shard_map/all_to_all | solution.py:14
  14.7 26.3 %collective-permute-start.3 = (bf16[512,512]{1,0:T(8,128)(2,1)S(1)}, bf16[512,512]{1,0:T(8,128)(2,1)S(1)}, u32[]{:S(2)}, u32[]{:S(2)}) collective-permute-start(bf16[512,512]{1,0:T(8,128)(2,1)S(1)} %get-tuple-element.7.refs_4_), channel_id=1, source_target_pairs={{0,2},{2,0},{1,3},{3,1},{4,6},{6,4},{5,7},{7,5},{8,10},{10,8},{9,1... | collective-permute-start | bytes 1572872 | tf_op jit(solution)/shard_map/ppermute | solution.py:27
  16.7 18.8 %collective-permute-start.9 = (bf16[512,512]{1,0:T(8,128)(2,1)S(1)}, bf16[512,512]{1,0:T(8,128)(2,1)S(1)}, u32[]{:S(2)}, u32[]{:S(2)}) collective-permute-start(bf16[512,512]{1,0:T(8,128)(2,1)S(1)} %get-tuple-element.7.refs_4_), channel_id=1, source_target_pairs={{0,4},{4,0},{1,5},{5,1},{2,6},{6,2},{3,7},{7,3},{8,12},{12,8},{9,1... | collective-permute-start | bytes 1572872 | tf_op jit(solution)/shard_map/ppermute | solution.py:27
  22.4 18.5 %collective-permute-start.5 = (bf16[512,512]{1,0:T(8,128)(2,1)S(1)}, bf16[512,512]{1,0:T(8,128)(2,1)S(1)}, u32[]{:S(2)}, u32[]{:S(2)}) collective-permute-start(bf16[512,512]{1,0:T(8,128)(2,1)S(1)} %collective-permute-done.4.refs_6_.refs_8_), channel_id=1, source_target_pairs={{0,2},{2,0},{1,3},{3,1},{4,6},{6,4},{5,7},{7,5},{8,10},{10,8},{9,1... | collective-permute-start | bytes 1572872 | tf_op jit(solution)/shard_map/ppermute | solution.py:27
  25.4 7.2 %collective-permute-start = (bf16[64,1024]{1,0:T(8,128)(2,1)S(1)}, bf16[64,1024]{1,0:T(8,128)(2,1)S(1)}, u32[]{:S(2)}, u32[]{:S(2)}) collective-permute-start(bf16[64,1024]{1,0:T(8,128)(2,1)S(1)} %bitcast.19), channel_id=1, source_target_pairs={{0,384},{128,0},{256,128},{384,256},{1,385},{129,1},{257,129},{385... | collective-permute-start | bytes 393224 | tf_op jit(solution)/shard_map/ppermute | solution.py:22
  29.8 8.2 %collective-permute-start.1 = (bf16[64,1024]{1,0:T(8,128)(2,1)S(1)}, bf16[64,1024]{1,0:T(8,128)(2,1)S(1)}, u32[]{:S(2)}, u32[]{:S(2)}) collective-permute-start(bf16[64,1024]{1,0:T(8,128)(2,1)S(1)} %bitcast.20), channel_id=1, source_target_pairs={{0,256},{128,384},{256,0},{384,128},{1,257},{129,385},{257,1},{385... | collective-permute-start | bytes 393224 | tf_op jit(solution)/shard_map/ppermute | solution.py:22
  32.6 8.3 %collective-permute-start.2 = (bf16[64,1024]{1,0:T(8,128)(2,1)S(1)}, bf16[64,1024]{1,0:T(8,128)(2,1)S(1)}, u32[]{:S(2)}, u32[]{:S(2)}) collective-permute-start(bf16[64,1024]{1,0:T(8,128)(2,1)S(1)} %bitcast.21), channel_id=1, source_target_pairs={{0,128},{128,256},{256,384},{384,0},{1,129},{129,257},{257,385},{3... | collective-permute-start | bytes 393224 | tf_op jit(solution)/shard_map/ppermute | solution.py:22
  35.5 20.7 %collective-permute-start.11 = (bf16[512,512]{1,0:T(8,128)(2,1)S(1)}, bf16[512,512]{1,0:T(8,128)(2,1)S(1)}, u32[]{:S(2)}, u32[]{:S(2)}) collective-permute-start(bf16[512,512]{1,0:T(8,128)(2,1)S(1)} %collective-permute-done.9.refs_6_), channel_id=1, source_target_pairs={{0,32},{32,0},{1,33},{33,1},{2,34},{34,2},{3,35},{35,3},{4,36},{36... | collective-permute-start | bytes 1572872 | tf_op jit(solution)/shard_map/ppermute | solution.py:27
  42.5 26.1 %all-to-all-start.1 = ((bf16[8,32,1024]{2,1,0:T(8,128)(2,1)}), bf16[8,32,1024]{2,1,0:T(8,128)(2,1)}, u32[]{:S(2)}, u32[]{:S(2)}) async-start(bf16[8,32,1024]{2,1,0:T(8,128)(2,1)} %bitcast.9), calls=%async_computation.1 | async-start | bytes 1048576 | tf_op jit(solution)/shard_map/all_to_all | solution.py:14
  52.5 26.2 %collective-permute-start.10 = (bf16[512,512]{1,0:T(8,128)(2,1)S(1)}, bf16[512,512]{1,0:T(8,128)(2,1)}, u32[]{:S(2)}, u32[]{:S(2)}) collective-permute-start(bf16[512,512]{1,0:T(8,128)(2,1)S(1)} %collective-permute-done.9.refs_6_), channel_id=1, source_target_pairs={{0,2},{2,0},{1,3},{3,1},{4,6},{6,4},{5,7},{7,5},{8,10},{10,8},{9,1... | collective-permute-start | bytes 1572872 | tf_op jit(solution)/shard_map/ppermute | solution.py:27
  56.2 22.6 %collective-permute-start.12 = (bf16[512,512]{1,0:T(8,128)(2,1)S(1)}, bf16[512,512]{1,0:T(8,128)(2,1)}, u32[]{:S(2)}, u32[]{:S(2)}) collective-permute-start(bf16[512,512]{1,0:T(8,128)(2,1)S(1)} %collective-permute-done.11.refs_10_), channel_id=1, source_target_pairs={{0,2},{2,0},{1,3},{3,1},{4,6},{6,4},{5,7},{7,5},{8,10},{10,8},{9,1... | collective-permute-start | bytes 1572872 | tf_op jit(solution)/shard_map/ppermute | solution.py:27
  69.8 9.0 %collective-permute-start.6 = (bf16[32,1024]{1,0:T(8,128)(2,1)S(1)}, bf16[32,1024]{1,0:T(8,128)(2,1)S(1)}, u32[]{:S(2)}, u32[]{:S(2)}) collective-permute-start(bf16[32,1024]{1,0:T(8,128)(2,1)S(1)} %reduce_sum.21.refs_0_), channel_id=1, source_target_pairs={{0,24},{8,0},{16,8},{24,16},{1,25},{9,1},{17,9},{25,17},{2,26},{10... | collective-permute-start | bytes 196616 | tf_op jit(solution)/shard_map/ppermute | solution.py:22
  72.7 9.4 %collective-permute-start.7 = (bf16[32,1024]{1,0:T(8,128)(2,1)S(1)}, bf16[32,1024]{1,0:T(8,128)(2,1)S(1)}, u32[]{:S(2)}, u32[]{:S(2)}) collective-permute-start(bf16[32,1024]{1,0:T(8,128)(2,1)S(1)} %reduce_sum.21.refs_0_), channel_id=1, source_target_pairs={{0,16},{8,24},{16,0},{24,8},{1,17},{9,25},{17,1},{25,9},{2,18},{10... | collective-permute-start | bytes 196616 | tf_op jit(solution)/shard_map/ppermute | solution.py:22
  76.4 8.5 %collective-permute-start.8 = (bf16[32,1024]{1,0:T(8,128)(2,1)S(1)}, bf16[32,1024]{1,0:T(8,128)(2,1)S(1)}, u32[]{:S(2)}, u32[]{:S(2)}) collective-permute-start(bf16[32,1024]{1,0:T(8,128)(2,1)S(1)} %reduce_sum.21.refs_0_), channel_id=1, source_target_pairs={{0,8},{8,16},{16,24},{24,0},{1,9},{9,17},{17,25},{25,1},{2,10},{10... | collective-permute-start | bytes 196616 | tf_op jit(solution)/shard_map/ppermute | solution.py:22
  87.6 24.7 %all-to-all-start.2 = ((bf16[64,8,512]{2,1,0:T(8,128)(2,1)}), bf16[64,8,512]{2,1,0:T(8,128)(2,1)S(1)}, u32[]{:S(2)}, u32[]{:S(2)}) async-start(bf16[64,8,512]{2,1,0:T(8,128)(2,1)} %bitcast.10), calls=%async_computation.2 | async-start | bytes 1048576 | tf_op jit(solution)/shard_map/all_to_all | solution.py:14

commit v7 on v3

v7 whole, which is shorter than its diff:
```python
import jax
import jax.numpy as jnp
from jax import lax
from jax.experimental import pallas as pl
from jax.experimental.pallas import tpu as pltpu
from jax.sharding import Mesh, PartitionSpec as P


SIZES = {"x": 4, "h": 2, "p": 2, "z": 8, "c": 2, "l": 2}
SMEM = pl.BlockSpec(memory_space=pltpu.SMEM)
VMEM = pl.BlockSpec(memory_space=pltpu.VMEM)
ANY = pl.BlockSpec(memory_space=pl.ANY)


def call(kernel, shape, dtype, specs, flops=0):
    size = 2
    for extent in shape:
        size *= extent
    return pl.pallas_call(
        kernel,
        out_shape=jax.ShapeDtypeStruct(shape, dtype),
        in_specs=specs,
        out_specs=VMEM,
        compiler_params=pltpu.CompilerParams(vmem_limit_bytes=16 << 20),
        cost_estimate=pl.CostEstimate(
            flops=flops, bytes_accessed=2 * size, transcendentals=0
        ),
    )


def exchange(blocks, axis):
    return lax.all_to_all(blocks, axis, 0, 0, tiled=True)


def swap(tile, axis):
    return lax.ppermute(tile, axis, ((0, 1), (1, 0)))


def total(blocks):
    return jnp.sum(blocks.astype(jnp.float32), axis=0)


def masked(tile, pattern):
    width, blocks = tile.shape[0], pattern.shape[0]
    span = width // blocks
    mask = jnp.broadcast_to(pattern[:, None, :, None], (blocks, span, blocks, span))
    return tile * mask.reshape(width, width).astype(tile.dtype)


def send_kernel(layer_ref, tile_ref, pattern_ref, out_ref, own_ref, rows_ref, kept_ref, sems):
    share, width = out_ref.shape[1:]
    blocks = pattern_ref.shape[1]
    height = 4 * share
    span = width // blocks
    start = pl.multiple_of(layer_ref[0] * height, height)
    rows = pltpu.make_async_copy(tile_ref.at[0, pl.ds(start, height)], rows_ref, sems.at[0])
    kept = pltpu.make_async_copy(pattern_ref, kept_ref, sems.at[1])
    rows.start()
    kept.start()
    number = lax.broadcasted_iota(jnp.int32, (blocks, width), 0)
    place = lax.broadcasted_iota(jnp.int32, (blocks, width), 1)
    inside = (place >= number * span) & (place < number * span + span)
    kept.wait()
    wide = jnp.dot(
        kept_ref[0].astype(jnp.float32),
        inside.astype(jnp.float32),
        preferred_element_type=jnp.float32,
    )
    tall = lax.broadcasted_iota(jnp.int32, (height, blocks), 0) + start
    line = lax.broadcasted_iota(jnp.int32, (height, blocks), 1)
    chosen = (tall >= line * span) & (tall < line * span + span)
    mask = jnp.dot(chosen.astype(jnp.float32), wide, preferred_element_type=jnp.float32)
    rows.wait()
    piece = (rows_ref[...].astype(jnp.float32) * mask).astype(out_ref.dtype)
    own_ref[...] = piece
    for k in range(out_ref.shape[0]):
        part = k % 4 * share
        out_ref[k] = piece[part : part + share]


def rows_kernel(core_ref, parts_ref, out_ref):
    share, width = parts_ref.shape[1:]
    for k in range(parts_ref.shape[0] // 2):
        for side in range(2):
            piece = parts_ref[2 * k + lax.bitwise_xor(core_ref[0], side)]
            for far in range(out_ref.shape[0]):
                rows, columns = pl.ds(k * share, share), pl.ds(side * width, width)
                out_ref[far, rows, columns] = piece


def first_kernel(rows_ref, a_ref, b_ref, c_ref, d_ref, out_ref):
    width = a_ref.shape[0]
    turned = (((1,), (1,)), ((), ()))
    left, right = rows_ref[:, :width], rows_ref[:, width:]
    for k, (one, two) in enumerate(((a_ref, b_ref), (c_ref, d_ref))):
        part = lax.dot_general(left, one[...], turned, preferred_element_type=jnp.float32)
        part += lax.dot_general(right, two[...], turned, preferred_element_type=jnp.float32)
        out_ref[:, k] = part.astype(out_ref.dtype).reshape(out_ref.shape[0], -1, width)


def second_kernel(core_ref, left_ref, a_ref, b_ref, c_ref, d_ref, out_ref):
    width = a_ref.shape[0]
    left = left_ref[:, 0].reshape(-1, width)
    right = left_ref[:, 1].reshape(-1, width)
    for k, (one, two) in enumerate(((a_ref, c_ref), (b_ref, d_ref))):
        part = jnp.dot(left, one[...], preferred_element_type=jnp.float32)
        part += jnp.dot(right, two[...], preferred_element_type=jnp.float32)
        part = part.astype(out_ref.dtype).reshape(-1, out_ref.shape[2], width)
        out_ref[:, lax.bitwise_xor(core_ref[0], k)] = part


def step(x_tiles, pattern):
    half = jnp.bfloat16
    width = x_tiles.shape[1]
    share = width // 32
    nx, nz = lax.axis_size("x"), lax.axis_size("z")
    core = lax.axis_index("c").reshape(1)
    layer = lax.axis_index("l").reshape(1)
    height = 4 * nx * share
    flops = 8 * height * width * width

    parts, own = pl.pallas_call(
        send_kernel,
        out_shape=(
            jax.ShapeDtypeStruct((8, share, width), half),
            jax.ShapeDtypeStruct((4 * share, width), half),
        ),
        in_specs=[SMEM, ANY, ANY],
        out_specs=(VMEM, VMEM),
        scratch_shapes=(
            pltpu.VMEM((4 * share, width), half),
            pltpu.VMEM(pattern.shape, jnp.int32),
            pltpu.SemaphoreType.DMA((2,)),
        ),
        name="send",
    )(layer, x_tiles, pattern)
    parts = exchange(parts, ("h", "p", "c"))
    rows = call(rows_kernel, (nx, 4 * share, 2 * width), half, [SMEM, VMEM])
    rows = exchange(rows(core, parts), "x").reshape(height, 2 * width)

    tile = masked(x_tiles[0], pattern[0])
    below = swap(tile, "p")
    tiles = [tile, swap(tile, "c"), below, swap(below, "c")]

    shape = (nz, 2, height // nz, width)
    partial = call(first_kernel, shape, half, [VMEM] * 5, flops)(rows, *tiles)
    partial = partial.reshape(nz, -1, width)
    squared = total(exchange(partial, "z")).astype(half)
    squared = jnp.broadcast_to(squared[None], (nz,) + squared.shape)
    squared = exchange(squared, "z").reshape(shape)
    shape = (4 * nx, 2, share, width)
    parts = call(second_kernel, shape, half, [SMEM] + [VMEM] * 5, flops)
    parts = parts(core, squared, *tiles).reshape(8 * nx, share, width)
    parts = exchange(parts, ("x", "h", "p", "c"))
    cubed = total(parts.reshape(2 * nx, 4 * share, width))
    signed = 1.5 * own.astype(jnp.float32) - 0.5 * cubed
    return signed.astype(half)[None]


def solution(mesh, sizes=SIZES):
    fine = Mesh(mesh.devices.reshape(tuple(sizes.values())), tuple(sizes))
    grid = ("x", "h", "p", "z", "c")
    specs = (P(grid, None, None), P(grid, None, None))
    return jax.shard_map(
        step, mesh=fine, in_specs=specs, out_specs=P(grid, "l", None), check_vma=False
    )
```

time: 109 us -> 109 us (level)
  waiting for transfers between devices: 14.3 us -> 8.2 us
  Pallas kernels: 0 us -> 3.95 us
  blocking collectives: 67.2 us -> 70.7 us
  matrix products: 1.44 us -> 0 us
  starting transfers between devices: 21 us -> 22.3 us
    all_to_all x2, waiting for transfers between devices: 14.3 us -> 8.2 us  [exchange(): return lax.all_to_all(blocks, axis, 0, 0, tiled=True)]
    pallas_call x0 -> x4, Pallas kernels: none -> 3.95 us  [the longest x1 1.68 us: step(): pl.pallas_call(send_kernel, out_shape=(jax.ShapeDtypeStruct((8, share, wi...]
    all_to_all x3, blocking collectives: 67.2 us -> 70.7 us  [exchange(): return lax.all_to_all(blocks, axis, 0, 0, tiled=True)]
    ppermute x3, starting transfers between devices: 8.97 us -> 10.7 us  [swap(): return lax.ppermute(tile, axis, ((0, 1), (1, 0)))]
    broadcast_in_dim x3 -> x1, local copies, waits for them, and re-layouts: 1.56 us -> 0.04 us  [step(): squared = jnp.broadcast_to(squared[None], (nz,) + squared.shape)]
    dot_general x2 -> x0, matrix products: 1.44 us -> none  [the longest x1 0.74 us: step(): lax.dot_general(rows, block, (((1,), (1,)), ((), ())), preferred_element_...]
  transfers between devices with their start and end apart: 5 -> 5, of which waited for: 2 -> 1; matrix products, arithmetic and copies ran while one was open for 1% -> 0% of each run, Pallas kernels for 0% -> 1%
where the time goes in v7:
time: 109 us
  blocking collectives  70.7 us (65%)
  starting transfers between devices  22.3 us (20%)
  waiting for transfers between devices  8.2 us (8%)
  Pallas kernels  3.95 us (4%)
  local copies, waits for them, and re-layouts  2.04 us (2%)
  other arithmetic  1.54 us (1%)
    all_to_all x3, blocking collectives, exchange(): return lax.all_to_all(blocks, axis, 0, 0, tiled=True)  70.7 us
    all_to_all x2, starting transfers between devices, exchange(): return lax.all_to_all(blocks, axis, 0, 0, tiled=True)  11.6 us
    ppermute x3, starting transfers between devices, swap(): return lax.ppermute(tile, axis, ((0, 1), (1, 0)))  10.7 us
    all_to_all x2, waiting for transfers between devices, exchange(): return lax.all_to_all(blocks, axis, 0, 0, tiled=True)  8.2 us
  transfers between devices with their start and end apart: 5, of which 1 were waited for; matrix products, arithmetic and copies ran while one was open for 0% of the time, Pallas kernels for 1%

profile of v7, /device:TPU:1, one launch (start us, length us, event | category | flops | bytes accessed | tf_op | source)
XLA Modules:
  0.0 108.8 jit_solution(2811608277022321530)
XLA Ops:
  0.0 0.7 convert_bitcast_fusion
  0.7 0.2 broadcast_in_dim.6
  0.9 0.0 copy-start
  0.9 0.6 convert_element_type.27
  1.5 0.4 copy-done
  1.9 0.1 bitcast_multiply_fusion.a_ref
  2.0 4.0 %collective-permute-start.1 = (bf16[512,512]{1,0:T(8,128)(2,1)S(1)}, bf16[512,512]{1,0:T(8,128)(2,1)S(1)}, u32[]{:S(2)}, u32[]{:S(2)}) collective-permute-start(bf16[512,512]{1,0:T(8,128)(2,1)S(1)} %bitcast_multiply_fusion.a_ref), channel_id=1, source_target_pairs={{0,32},{32,0},{1,33},{33,1},{2,34},{34,2},{3,35},{35,3},{4,36},{36... | collective-permute-start | bytes 1572872 | tf_op jit(solution)/shard_map/ppermute | solution.py:36
  6.0 1.7 %send.1 = (bf16[8,16,512]{2,1,0:T(8,128)(2,1)}, bf16[64,512]{1,0:T(8,128)(2,1)}) custom-call(s32[1]{0:T(128)} %bitcast.layer_ref, bf16[1,512,512]{2,1,0:T(8,128)(2,1)} %tile_ref.1, s32[1,8,8]{2,1,0:T(8,128)} %pattern_ref.1), custom_call_target="tpu_custom_call" | custom-call | tf_op jit(solution)/shard_map/send/pallas_call | solution.py:122
  7.7 8.0 %all-to-all-start = ((bf16[8,16,512]{2,1,0:T(8,128)(2,1)}), bf16[8,16,512]{2,1,0:T(8,128)(2,1)S(1)}, u32[]{:S(2)}, u32[]{:S(2)}) async-start(bf16[8,16,512]{2,1,0:T(8,128)(2,1)} %get-tuple-element.8), calls=%async_computation | async-start | bytes 262144 | tf_op jit(solution)/shard_map/all_to_all | solution.py:32
  15.8 2.0 %collective-permute-start = (bf16[512,512]{1,0:T(8,128)(2,1)S(1)}, bf16[512,512]{1,0:T(8,128)(2,1)S(1)}, u32[]{:S(2)}, u32[]{:S(2)}) collective-permute-start(bf16[512,512]{1,0:T(8,128)(2,1)S(1)} %bitcast_multiply_fusion.a_ref), channel_id=1, source_target_pairs={{0,2},{2,0},{1,3},{3,1},{4,6},{6,4},{5,7},{7,5},{8,10},{10,8},{9,1... | collective-permute-start | bytes 1572872 | tf_op jit(solution)/shard_map/ppermute | solution.py:36
  17.8 0.0 collective-permute-done.1.c_ref
  17.8 4.6 %collective-permute-start.2 = (bf16[512,512]{1,0:T(8,128)(2,1)S(1)}, bf16[512,512]{1,0:T(8,128)(2,1)S(1)}, u32[]{:S(2)}, u32[]{:S(2)}) collective-permute-start(bf16[512,512]{1,0:T(8,128)(2,1)S(1)} %collective-permute-done.1.c_ref), channel_id=1, source_target_pairs={{0,2},{2,0},{1,3},{3,1},{4,6},{6,4},{5,7},{7,5},{8,10},{10,8},{9,1... | collective-permute-start | bytes 1572872 | tf_op jit(solution)/shard_map/ppermute | solution.py:36
  22.4 0.0 all-to-all-done.parts_ref
  22.4 0.8 shard_map.28
  23.3 3.6 %all-to-all-start.1 = ((bf16[4,64,1024]{2,1,0:T(8,128)(2,1)}), bf16[4,64,1024]{2,1,0:T(8,128)(2,1)S(1)}, u32[]{:S(2)}, u32[]{:S(2)}) async-start(bf16[4,64,1024]{2,1,0:T(8,128)(2,1)} %shard_map.28), calls=%async_computation.1 | async-start | bytes 1048576 | tf_op jit(solution)/shard_map/all_to_all | solution.py:32
  26.9 0.0 collective-permute-done.b_ref
  26.9 8.2 %all-to-all-done.1 = bf16[4,64,1024]{2,1,0:T(8,128)(2,1)S(1)} async-done(((bf16[4,64,1024]{2,1,0:T(8,128)(2,1)}), bf16[4,64,1024]{2,1,0:T(8,128)(2,1)S(1)}, u32[]{:S(2)}, u32[]{:S(2)}) %all-to-all-start.1) | async-done | bytes 524320 | tf_op jit(solution)/shard_map/all_to_all | solution.py:32
  35.1 0.0 collective-permute-done.2.d_ref
  35.1 0.7 shard_map.29
  35.8 24.3 %all_to_all.25 = bf16[8,64,512]{2,1,0:T(8,128)(2,1)S(1)} all-to-all(bf16[8,64,512]{2,1,0:T(8,128)(2,1)S(1)} %bitcast.21), channel_id=1, replica_groups=mesh['x'=4,'h'=2,'p'=2,'z'=8,'c'=2,'l'=2] {'z'}, dimensions={0} | all-to-all | bytes 1048576 | tf_op jit(solution)/shard_map/all_to_all | solution.py:32
  60.2 0.1 reduce_sum.21
  60.3 16.9 %all_to_all.26 = bf16[8,64,512]{2,1,0:T(8,128)(2,1)S(1)} all-to-all(bf16[8,64,512]{2,1,0:T(8,128)(2,1)S(1)} %broadcast_in_dim.7), channel_id=1, replica_groups=mesh['x'=4,'h'=2,'p'=2,'z'=8,'c'=2,'l'=2] {'z'}, dimensions={0} | all-to-all | bytes 1048576 | tf_op jit(solution)/shard_map/all_to_all | solution.py:32
  77.2 0.7 shard_map.30
  77.9 29.4 %all_to_all.27 = bf16[32,16,512]{2,1,0:T(8,128)(2,1)S(1)} all-to-all(bf16[32,16,512]{2,1,0:T(8,128)(2,1)S(1)} %bitcast.20), channel_id=1, replica_groups=mesh['x'=4,'h'=2,'p'=2,'z'=8,'c'=2,'l'=2] {'x','h','p','c'}, dimensions={0} | all-to-all | bytes 1048576 | tf_op jit(solution)/shard_map/all_to_all | solution.py:32
  107.4 0.0 copy-start.1
  107.4 0.1 convert_reduce_fusion
  107.4 0.8 copy-done.1
  108.2 0.7 fusion
  (1 shorter events, 0.0 us)
Async XLA Ops:
  0.9 1.0 copy-start
  2.0 15.8 %collective-permute-start.1 = (bf16[512,512]{1,0:T(8,128)(2,1)S(1)}, bf16[512,512]{1,0:T(8,128)(2,1)S(1)}, u32[]{:S(2)}, u32[]{:S(2)}) collective-permute-start(bf16[512,512]{1,0:T(8,128)(2,1)S(1)} %bitcast_multiply_fusion.a_ref), channel_id=1, source_target_pairs={{0,32},{32,0},{1,33},{33,1},{2,34},{34,2},{3,35},{35,3},{4,36},{36... | collective-permute-start | bytes 1572872 | tf_op jit(solution)/shard_map/ppermute | solution.py:36
  7.7 14.7 %all-to-all-start = ((bf16[8,16,512]{2,1,0:T(8,128)(2,1)}), bf16[8,16,512]{2,1,0:T(8,128)(2,1)S(1)}, u32[]{:S(2)}, u32[]{:S(2)}) async-start(bf16[8,16,512]{2,1,0:T(8,128)(2,1)} %get-tuple-element.8), calls=%async_computation | async-start | bytes 262144 | tf_op jit(solution)/shard_map/all_to_all | solution.py:32
  15.8 11.1 %collective-permute-start = (bf16[512,512]{1,0:T(8,128)(2,1)S(1)}, bf16[512,512]{1,0:T(8,128)(2,1)S(1)}, u32[]{:S(2)}, u32[]{:S(2)}) collective-permute-start(bf16[512,512]{1,0:T(8,128)(2,1)S(1)} %bitcast_multiply_fusion.a_ref), channel_id=1, source_target_pairs={{0,2},{2,0},{1,3},{3,1},{4,6},{6,4},{5,7},{7,5},{8,10},{10,8},{9,1... | collective-permute-start | bytes 1572872 | tf_op jit(solution)/shard_map/ppermute | solution.py:36
  17.8 17.3 %collective-permute-start.2 = (bf16[512,512]{1,0:T(8,128)(2,1)S(1)}, bf16[512,512]{1,0:T(8,128)(2,1)S(1)}, u32[]{:S(2)}, u32[]{:S(2)}) collective-permute-start(bf16[512,512]{1,0:T(8,128)(2,1)S(1)} %collective-permute-done.1.c_ref), channel_id=1, source_target_pairs={{0,2},{2,0},{1,3},{3,1},{4,6},{6,4},{5,7},{7,5},{8,10},{10,8},{9,1... | collective-permute-start | bytes 1572872 | tf_op jit(solution)/shard_map/ppermute | solution.py:36
  23.3 11.8 %all-to-all-start.1 = ((bf16[4,64,1024]{2,1,0:T(8,128)(2,1)}), bf16[4,64,1024]{2,1,0:T(8,128)(2,1)S(1)}, u32[]{:S(2)}, u32[]{:S(2)}) async-start(bf16[4,64,1024]{2,1,0:T(8,128)(2,1)} %shard_map.28), calls=%async_computation.1 | async-start | bytes 1048576 | tf_op jit(solution)/shard_map/all_to_all | solution.py:32
  107.4 0.8 copy-start.1

commit v8 on v7

--- a/solution.py
+++ b/solution.py
@@ -6,7 +6,7 @@
 from jax.sharding import Mesh, PartitionSpec as P
 
 
-SIZES = {"x": 4, "h": 2, "p": 2, "z": 8, "c": 2, "l": 2}
+SIZES = {"x": 4, "h": 2, "p": 2, "w": 4, "q": 2, "c": 2, "l": 2}
 SMEM = pl.BlockSpec(memory_space=pltpu.SMEM)
 VMEM = pl.BlockSpec(memory_space=pltpu.VMEM)
 ANY = pl.BlockSpec(memory_space=pl.ANY)
@@ -51,6 +51,7 @@
     share, width = out_ref.shape[1:]
     blocks = pattern_ref.shape[1]
     height = 4 * share
+    small = share // 2
     span = width // blocks
     start = pl.multiple_of(layer_ref[0] * height, height)
     rows = pltpu.make_async_copy(tile_ref.at[0, pl.ds(start, height)], rows_ref, sems.at[0])
@@ -74,18 +75,31 @@
     piece = (rows_ref[...].astype(jnp.float32) * mask).astype(out_ref.dtype)
     own_ref[...] = piece
     for k in range(out_ref.shape[0]):
-        part = k % 4 * share
-        out_ref[k] = piece[part : part + share]
+        p, c = k // 2 % 2, k % 2
+        for q in range(2):
+            part = (4 * p + 2 * q + c) * small
+            out_ref[k, q * small : (q + 1) * small] = piece[part : part + small]
 
 
 def rows_kernel(core_ref, parts_ref, out_ref):
-    share, width = parts_ref.shape[1:]
-    for k in range(parts_ref.shape[0] // 2):
+    count, share, width = parts_ref.shape
+    small = share // 2
+    for k in range(count // 2):
         for side in range(2):
+            columns = pl.ds(side * width, width)
             piece = parts_ref[2 * k + lax.bitwise_xor(core_ref[0], side)]
-            for far in range(out_ref.shape[0]):
-                rows, columns = pl.ds(k * share, share), pl.ds(side * width, width)
-                out_ref[far, rows, columns] = piece
+            for q in range(2):
+                rows = pl.ds((q * (count // 2) + k) * small, small)
+                for far in range(out_ref.shape[0]):
+                    out_ref[far, rows, columns] = piece[q * small : (q + 1) * small]
+
+
+def sum_kernel(parts_ref, out_ref):
+    value = parts_ref[0].astype(jnp.float32)
+    for k in range(1, parts_ref.shape[0]):
+        value += parts_ref[k].astype(jnp.float32)
+    for k in range(out_ref.shape[0]):
+        out_ref[k] = value.astype(out_ref.dtype)
 
 
 def first_kernel(rows_ref, a_ref, b_ref, c_ref, d_ref, out_ref):
@@ -98,22 +112,23 @@
         out_ref[:, k] = part.astype(out_ref.dtype).reshape(out_ref.shape[0], -1, width)
 
 
-def second_kernel(core_ref, left_ref, a_ref, b_ref, c_ref, d_ref, out_ref):
-    width = a_ref.shape[0]
+def second_kernel(place_ref, left_ref, *refs):
+    tiles, lower, out_ref = refs[:4], refs[4:8], refs[8]
+    width = tiles[0].shape[0]
     left = left_ref[:, 0].reshape(-1, width)
     right = left_ref[:, 1].reshape(-1, width)
-    for k, (one, two) in enumerate(((a_ref, c_ref), (b_ref, d_ref))):
-        part = jnp.dot(left, one[...], preferred_element_type=jnp.float32)
-        part += jnp.dot(right, two[...], preferred_element_type=jnp.float32)
+    for k in range(4):
+        part = jnp.dot(left, tiles[k][...], preferred_element_type=jnp.float32)
+        part += jnp.dot(right, lower[k][...], preferred_element_type=jnp.float32)
         part = part.astype(out_ref.dtype).reshape(-1, out_ref.shape[2], width)
-        out_ref[:, lax.bitwise_xor(core_ref[0], k)] = part
+        out_ref[:, lax.bitwise_xor(place_ref[0], k)] = part
 
 
 def step(x_tiles, pattern):
     half = jnp.bfloat16
     width = x_tiles.shape[1]
     share = width // 32
-    nx, nz = lax.axis_size("x"), lax.axis_size("z")
+    nx, nw = lax.axis_size("x"), lax.axis_size("w")
     core = lax.axis_index("c").reshape(1)
     layer = lax.axis_index("l").reshape(1)
     height = 4 * nx * share
@@ -140,18 +155,23 @@
 
     tile = masked(x_tiles[0], pattern[0])
     below = swap(tile, "p")
-    tiles = [tile, swap(tile, "c"), below, swap(below, "c")]
+    along = swap(tile, "q")
+    corner = swap(along, "p")
+    tiles = [tile, swap(tile, "c"), along, swap(along, "c")]
+    lower = [below, swap(below, "c"), corner, swap(corner, "c")]
 
-    shape = (nz, 2, height // nz, width)
-    partial = call(first_kernel, shape, half, [VMEM] * 5, flops)(rows, *tiles)
-    partial = partial.reshape(nz, -1, width)
-    squared = total(exchange(partial, "z")).astype(half)
-    squared = jnp.broadcast_to(squared[None], (nz,) + squared.shape)
-    squared = exchange(squared, "z").reshape(shape)
-    shape = (4 * nx, 2, share, width)
-    parts = call(second_kernel, shape, half, [SMEM] + [VMEM] * 5, flops)
-    parts = parts(core, squared, *tiles).reshape(8 * nx, share, width)
-    parts = exchange(parts, ("x", "h", "p", "c"))
+    shape = (2 * nw, 2, height // (2 * nw), width)
+    partial = call(first_kernel, shape, half, [VMEM] * 5, flops)
+    partial = partial(rows, tiles[0], tiles[1], lower[0], lower[1])
+    partial = exchange(partial.reshape(2 * nw, -1, width), ("w", "q"))
+    squared = call(sum_kernel, (nw,) + partial.shape[1:], half, [VMEM])(partial)
+    squared = exchange(squared, "w").reshape((nw,) + shape[1:])
+    place = 2 * lax.axis_index("q") + lax.axis_index("c")
+    shape = (4 * nx, 4, share // 2, width)
+    parts = call(second_kernel, shape, half, [SMEM] + [VMEM] * 9, flops)
+    parts = parts(place.reshape(1), squared, *tiles, *lower)
+    parts = parts.reshape(16 * nx, share // 2, width)
+    parts = exchange(parts, ("x", "h", "p", "q", "c"))
     cubed = total(parts.reshape(2 * nx, 4 * share, width))
     signed = 1.5 * own.astype(jnp.float32) - 0.5 * cubed
     return signed.astype(half)[None]
@@ -159,7 +179,7 @@
 
 def solution(mesh, sizes=SIZES):
     fine = Mesh(mesh.devices.reshape(tuple(sizes.values())), tuple(sizes))
-    grid = ("x", "h", "p", "z", "c")
+    grid = ("x", "h", "p", "w", "q", "c")
     specs = (P(grid, None, None), P(grid, None, None))
     return jax.shard_map(
         step, mesh=fine, in_specs=specs, out_specs=P(grid, "l", None), check_vma=False

time: 109 us -> 113 us (1.037)
  blocking collectives: 70.7 us -> 25.9 us
  starting transfers between devices: 22.3 us -> 55.3 us
  waiting for transfers between devices: 8.2 us -> 20.7 us
  Pallas kernels: 3.95 us -> 6.91 us
    all_to_all x3 -> x1, blocking collectives: 70.7 us -> 25.9 us  [exchange(): return lax.all_to_all(blocks, axis, 0, 0, tiled=True)]
    all_to_all x2 -> x4, starting transfers between devices: 11.6 us -> 28.3 us  [exchange(): return lax.all_to_all(blocks, axis, 0, 0, tiled=True)]
    ppermute x3 -> x7, starting transfers between devices: 10.7 us -> 27 us  [swap(): return lax.ppermute(tile, axis, ((0, 1), (1, 0)))]
    ppermute x3 -> x7, waiting for transfers between devices: 0.01 us -> 6.65 us  [swap(): return lax.ppermute(tile, axis, ((0, 1), (1, 0)))]
    all_to_all x2 -> x4, waiting for transfers between devices: 8.2 us -> 14.1 us  [exchange(): return lax.all_to_all(blocks, axis, 0, 0, tiled=True)]
    pallas_call x2 -> x3, Pallas kernels: 1.44 us -> 4.4 us  [the longest x1 2.07 us: step(): parts = parts(place.reshape(1), squared, *tiles, *lower)]
  transfers between devices with their start and end apart: 5 -> 11, of which waited for: 1 -> 3; matrix products, arithmetic and copies ran while one was open for 0% -> 0% of each run, Pallas kernels for 1% -> 3%
where the time goes in v8:
time: 113 us; the launch traced here: 112 us
  starting transfers between devices  55.3 us (49%)
  blocking collectives  25.9 us (23%)
  waiting for transfers between devices  20.7 us (18%)
  Pallas kernels  6.91 us (6%)
  local copies, waits for them, and re-layouts  2 us (2%)
  other arithmetic  1.46 us (1%)
    all_to_all x4, starting transfers between devices, exchange(): return lax.all_to_all(blocks, axis, 0, 0, tiled=True)  28.3 us
    ppermute x7, starting transfers between devices, swap(): return lax.ppermute(tile, axis, ((0, 1), (1, 0)))  27 us
    all_to_all x1, blocking collectives, exchange(): return lax.all_to_all(blocks, axis, 0, 0, tiled=True)  25.9 us
    all_to_all x4, waiting for transfers between devices, exchange(): return lax.all_to_all(blocks, axis, 0, 0, tiled=True)  14.1 us
    ppermute x7, waiting for transfers between devices, swap(): return lax.ppermute(tile, axis, ((0, 1), (1, 0)))  6.65 us
  transfers between devices with their start and end apart: 11, of which 3 were waited for; matrix products, arithmetic and copies ran while one was open for 0% of the time, Pallas kernels for 3%

profile of v8, /device:TPU:1, one launch (start us, length us, event | category | flops | bytes accessed | tf_op | source)
XLA Modules:
  0.0 112.5 jit_solution(10188472440460752464)
XLA Ops:
  0.0 0.7 convert_bitcast_fusion
  0.7 0.2 broadcast_in_dim.8
  0.9 0.0 copy-start
  0.9 0.6 convert_element_type.25
  1.5 0.4 copy-done
  1.9 0.1 bitcast_multiply_fusion.a_ref.refs_0_
  2.0 4.0 %collective-permute-start.1 = (bf16[512,512]{1,0:T(8,128)(2,1)S(1)}, bf16[512,512]{1,0:T(8,128)(2,1)S(1)}, u32[]{:S(2)}, u32[]{:S(2)}) collective-permute-start(bf16[512,512]{1,0:T(8,128)(2,1)S(1)} %bitcast_multiply_fusion.a_ref.refs_0_), channel_id=1, source_target_pairs={{0,32},{32,0},{1,33},{33,1},{2,34},{34,2},{3,35},{35,3},{4,36},{36... | collective-permute-start | bytes 1572872 | tf_op jit(solution)/shard_map/ppermute | solution.py:36
  6.0 1.7 %send.1 = (bf16[8,16,512]{2,1,0:T(8,128)(2,1)}, bf16[64,512]{1,0:T(8,128)(2,1)}) custom-call(s32[1]{0:T(128)} %bitcast.layer_ref, bf16[1,512,512]{2,1,0:T(8,128)(2,1)} %tile_ref.1, s32[1,8,8]{2,1,0:T(8,128)} %pattern_ref.1), custom_call_target="tpu_custom_call" | custom-call | tf_op jit(solution)/shard_map/send/pallas_call | solution.py:137
  7.7 8.0 %all-to-all-start = ((bf16[8,16,512]{2,1,0:T(8,128)(2,1)}), bf16[8,16,512]{2,1,0:T(8,128)(2,1)S(1)}, u32[]{:S(2)}, u32[]{:S(2)}) async-start(bf16[8,16,512]{2,1,0:T(8,128)(2,1)} %get-tuple-element.8), calls=%async_computation | async-start | bytes 262144 | tf_op jit(solution)/shard_map/all_to_all | solution.py:32
  15.8 2.0 %collective-permute-start = (bf16[512,512]{1,0:T(8,128)(2,1)S(1)}, bf16[512,512]{1,0:T(8,128)(2,1)S(1)}, u32[]{:S(2)}, u32[]{:S(2)}) collective-permute-start(bf16[512,512]{1,0:T(8,128)(2,1)S(1)} %bitcast_multiply_fusion.a_ref.refs_0_), channel_id=1, source_target_pairs={{0,2},{2,0},{1,3},{3,1},{4,6},{6,4},{5,7},{7,5},{8,10},{10,8},{9,1... | collective-permute-start | bytes 1572872 | tf_op jit(solution)/shard_map/ppermute | solution.py:36
  17.8 0.0 collective-permute-done.1.c_ref.refs_4_
  17.8 4.6 %collective-permute-start.2 = (bf16[512,512]{1,0:T(8,128)(2,1)S(1)}, bf16[512,512]{1,0:T(8,128)(2,1)S(1)}, u32[]{:S(2)}, u32[]{:S(2)}) collective-permute-start(bf16[512,512]{1,0:T(8,128)(2,1)S(1)} %collective-permute-done.1.c_ref.refs_4_), channel_id=1, source_target_pairs={{0,2},{2,0},{1,3},{3,1},{4,6},{6,4},{5,7},{7,5},{8,10},{10,8},{9,1... | collective-permute-start | bytes 1572872 | tf_op jit(solution)/shard_map/ppermute | solution.py:36
  22.4 0.0 all-to-all-done.parts_ref
  22.4 0.8 shard_map.28
  23.3 3.6 %all-to-all-start.1 = ((bf16[4,64,1024]{2,1,0:T(8,128)(2,1)}), bf16[4,64,1024]{2,1,0:T(8,128)(2,1)S(1)}, u32[]{:S(2)}, u32[]{:S(2)}) async-start(bf16[4,64,1024]{2,1,0:T(8,128)(2,1)} %shard_map.28), calls=%async_computation.1 | async-start | bytes 1048576 | tf_op jit(solution)/shard_map/all_to_all | solution.py:32
  26.9 4.0 %collective-permute-start.3 = (bf16[512,512]{1,0:T(8,128)(2,1)S(1)}, bf16[512,512]{1,0:T(8,128)(2,1)S(1)}, u32[]{:S(2)}, u32[]{:S(2)}) collective-permute-start(bf16[512,512]{1,0:T(8,128)(2,1)S(1)} %bitcast_multiply_fusion.a_ref.refs_0_), channel_id=1, source_target_pairs={{0,4},{4,0},{1,5},{5,1},{2,6},{6,2},{3,7},{7,3},{8,12},{12,8},{9,1... | collective-permute-start | bytes 1572872 | tf_op jit(solution)/shard_map/ppermute | solution.py:36
  30.9 0.0 collective-permute-done.b_ref.refs_1_
  30.9 4.2 %all-to-all-done.1 = bf16[4,64,1024]{2,1,0:T(8,128)(2,1)S(1)} async-done(((bf16[4,64,1024]{2,1,0:T(8,128)(2,1)}), bf16[4,64,1024]{2,1,0:T(8,128)(2,1)S(1)}, u32[]{:S(2)}, u32[]{:S(2)}) %all-to-all-start.1) | async-done | bytes 524320 | tf_op jit(solution)/shard_map/all_to_all | solution.py:32
  35.1 0.0 collective-permute-done.2.d_ref.refs_5_
  35.1 1.6 %shard_map.29 = bf16[8,2,32,512]{3,2,1,0:T(8,128)(2,1)} custom-call(bf16[256,1024]{1,0:T(8,128)(2,1)S(1)} %bitcast.20, bf16[512,512]{1,0:T(8,128)(2,1)S(1)} %bitcast_multiply_fusion.a_ref.refs_0_, bf16[512,512]{1,0:T(8,128)(2,1)S(1)} %collective-permute-done.b_ref.refs_1_, bf16[512,512]{1,0:T(8,128)(2,1)S(1)} %collective-permute-done.1.c_ref.refs_4_, ...), custom_call_target="tpu_custom_call" | custom-call | flops 536870912 | bytes 1048576 | tf_op jit(solution)/shard_map/pallas_call | solution.py:165
  36.6 10.0 %all-to-all-start.2 = ((bf16[8,64,512]{2,1,0:T(8,128)(2,1)}), bf16[8,64,512]{2,1,0:T(8,128)(2,1)S(1)}, u32[]{:S(2)}, u32[]{:S(2)}) async-start(bf16[8,64,512]{2,1,0:T(8,128)(2,1)} %bitcast.6), calls=%async_computation.2 | async-start | bytes 1048576 | tf_op jit(solution)/shard_map/all_to_all | solution.py:32
  46.7 0.0 collective-permute-done.3.refs_2_
  46.7 4.2 %collective-permute-start.5 = (bf16[512,512]{1,0:T(8,128)(2,1)S(1)}, bf16[512,512]{1,0:T(8,128)(2,1)}, u32[]{:S(2)}, u32[]{:S(2)}) collective-permute-start(bf16[512,512]{1,0:T(8,128)(2,1)S(1)} %collective-permute-done.3.refs_2_), channel_id=1, source_target_pairs={{0,32},{32,0},{1,33},{33,1},{2,34},{34,2},{3,35},{35,3},{4,36},{36... | collective-permute-start | bytes 1572872 | tf_op jit(solution)/shard_map/ppermute | solution.py:36
  50.8 3.7 %collective-permute-start.4 = (bf16[512,512]{1,0:T(8,128)(2,1)S(1)}, bf16[512,512]{1,0:T(8,128)(2,1)}, u32[]{:S(2)}, u32[]{:S(2)}) collective-permute-start(bf16[512,512]{1,0:T(8,128)(2,1)S(1)} %collective-permute-done.3.refs_2_), channel_id=1, source_target_pairs={{0,2},{2,0},{1,3},{3,1},{4,6},{6,4},{5,7},{7,5},{8,10},{10,8},{9,1... | collective-permute-start | bytes 1572872 | tf_op jit(solution)/shard_map/ppermute | solution.py:36
  54.6 6.6 %collective-permute-done.5.refs_6_ = bf16[512,512]{1,0:T(8,128)(2,1)} collective-permute-done((bf16[512,512]{1,0:T(8,128)(2,1)S(1)}, bf16[512,512]{1,0:T(8,128)(2,1)}, u32[]{:S(2)}, u32[]{:S(2)}) %collective-permute-start.5) | collective-permute-done | bytes 524320 | tf_op jit(solution)/shard_map/ppermute | solution.py:36
  61.2 4.5 %collective-permute-start.6 = (bf16[512,512]{1,0:T(8,128)(2,1)}, bf16[512,512]{1,0:T(8,128)(2,1)}, u32[]{:S(2)}, u32[]{:S(2)}) collective-permute-start(bf16[512,512]{1,0:T(8,128)(2,1)} %collective-permute-done.5.refs_6_), channel_id=1, source_target_pairs={{0,2},{2,0},{1,3},{3,1},{4,6},{6,4},{5,7},{7,5},{8,10},{10,8},{9,1... | collective-permute-start | bytes 1572872 | tf_op jit(solution)/shard_map/ppermute | solution.py:36
  65.7 0.0 all-to-all-done.2.parts_ref
  65.7 0.8 shard_map.30
  66.5 6.6 %all-to-all-start.3 = ((bf16[4,64,512]{2,1,0:T(8,128)(2,1)}), bf16[4,64,512]{2,1,0:T(8,128)(2,1)S(1)}, u32[]{:S(2)}, u32[]{:S(2)}) async-start(bf16[4,64,512]{2,1,0:T(8,128)(2,1)} %shard_map.30), calls=%async_computation.3 | async-start | bytes 524288 | tf_op jit(solution)/shard_map/all_to_all | solution.py:32
  73.1 0.0 collective-permute-done.4.refs_3_
  73.1 0.0 collective-permute-done.6.refs_7_
  73.1 9.9 %all-to-all-done.3 = bf16[4,64,512]{2,1,0:T(8,128)(2,1)S(1)} async-done(((bf16[4,64,512]{2,1,0:T(8,128)(2,1)}), bf16[4,64,512]{2,1,0:T(8,128)(2,1)S(1)}, u32[]{:S(2)}, u32[]{:S(2)}) %all-to-all-start.3) | async-done | bytes 262176 | tf_op jit(solution)/shard_map/all_to_all | solution.py:32
  83.0 2.1 %shard_map.31 = bf16[16,4,8,512]{3,2,1,0:T(8,128)(2,1)S(1)} custom-call(s32[1]{0:T(128)} %bitcast.1.place_ref, bf16[4,2,32,512]{3,2,1,0:T(8,128)(2,1)S(1)} %bitcast.21, bf16[512,512]{1,0:T(8,128)(2,1)S(1)} %bitcast_multiply_fusion.a_ref.refs_0_, bf16[512,512]{1,0:T(8,128)(2,1)S(1)} %collective-permute-done.b_ref.refs_1_, ...), custom_call_target="tpu_custom_call" | custom-call | flops 536870912 | bytes 1048576 | tf_op jit(solution)/shard_map/pallas_call | solution.py:172
  85.1 25.9 %all_to_all.25 = bf16[64,8,512]{2,1,0:T(8,128)(2,1)S(1)} all-to-all(bf16[64,8,512]{2,1,0:T(8,128)(2,1)S(1)} %bitcast.19), channel_id=1, replica_groups=mesh['x'=4,'h'=2,'p'=2,'w'=4,'q'=2,'c'=2,'l'=2] {'x','h','p','q','c'}, dimensions={0} | all-to-all | bytes 1048576 | tf_op jit(solution)/shard_map/all_to_all | solution.py:32
  111.0 0.0 copy-start.1
  111.0 0.1 convert_reduce_fusion
  111.1 0.8 copy-done.1
  111.8 0.7 fusion
Async XLA Ops:
  0.9 1.0 copy-start
  2.0 15.8 %collective-permute-start.1 = (bf16[512,512]{1,0:T(8,128)(2,1)S(1)}, bf16[512,512]{1,0:T(8,128)(2,1)S(1)}, u32[]{:S(2)}, u32[]{:S(2)}) collective-permute-start(bf16[512,512]{1,0:T(8,128)(2,1)S(1)} %bitcast_multiply_fusion.a_ref.refs_0_), channel_id=1, source_target_pairs={{0,32},{32,0},{1,33},{33,1},{2,34},{34,2},{3,35},{35,3},{4,36},{36... | collective-permute-start | bytes 1572872 | tf_op jit(solution)/shard_map/ppermute | solution.py:36
  7.7 14.7 %all-to-all-start = ((bf16[8,16,512]{2,1,0:T(8,128)(2,1)}), bf16[8,16,512]{2,1,0:T(8,128)(2,1)S(1)}, u32[]{:S(2)}, u32[]{:S(2)}) async-start(bf16[8,16,512]{2,1,0:T(8,128)(2,1)} %get-tuple-element.8), calls=%async_computation | async-start | bytes 262144 | tf_op jit(solution)/shard_map/all_to_all | solution.py:32
  15.8 15.1 %collective-permute-start = (bf16[512,512]{1,0:T(8,128)(2,1)S(1)}, bf16[512,512]{1,0:T(8,128)(2,1)S(1)}, u32[]{:S(2)}, u32[]{:S(2)}) collective-permute-start(bf16[512,512]{1,0:T(8,128)(2,1)S(1)} %bitcast_multiply_fusion.a_ref.refs_0_), channel_id=1, source_target_pairs={{0,2},{2,0},{1,3},{3,1},{4,6},{6,4},{5,7},{7,5},{8,10},{10,8},{9,1... | collective-permute-start | bytes 1572872 | tf_op jit(solution)/shard_map/ppermute | solution.py:36
  17.8 17.3 %collective-permute-start.2 = (bf16[512,512]{1,0:T(8,128)(2,1)S(1)}, bf16[512,512]{1,0:T(8,128)(2,1)S(1)}, u32[]{:S(2)}, u32[]{:S(2)}) collective-permute-start(bf16[512,512]{1,0:T(8,128)(2,1)S(1)} %collective-permute-done.1.c_ref.refs_4_), channel_id=1, source_target_pairs={{0,2},{2,0},{1,3},{3,1},{4,6},{6,4},{5,7},{7,5},{8,10},{10,8},{9,1... | collective-permute-start | bytes 1572872 | tf_op jit(solution)/shard_map/ppermute | solution.py:36
  23.3 11.8 %all-to-all-start.1 = ((bf16[4,64,1024]{2,1,0:T(8,128)(2,1)}), bf16[4,64,1024]{2,1,0:T(8,128)(2,1)S(1)}, u32[]{:S(2)}, u32[]{:S(2)}) async-start(bf16[4,64,1024]{2,1,0:T(8,128)(2,1)} %shard_map.28), calls=%async_computation.1 | async-start | bytes 1048576 | tf_op jit(solution)/shard_map/all_to_all | solution.py:32
  26.9 19.8 %collective-permute-start.3 = (bf16[512,512]{1,0:T(8,128)(2,1)S(1)}, bf16[512,512]{1,0:T(8,128)(2,1)S(1)}, u32[]{:S(2)}, u32[]{:S(2)}) collective-permute-start(bf16[512,512]{1,0:T(8,128)(2,1)S(1)} %bitcast_multiply_fusion.a_ref.refs_0_), channel_id=1, source_target_pairs={{0,4},{4,0},{1,5},{5,1},{2,6},{6,2},{3,7},{7,3},{8,12},{12,8},{9,1... | collective-permute-start | bytes 1572872 | tf_op jit(solution)/shard_map/ppermute | solution.py:36
  36.6 29.1 %all-to-all-start.2 = ((bf16[8,64,512]{2,1,0:T(8,128)(2,1)}), bf16[8,64,512]{2,1,0:T(8,128)(2,1)S(1)}, u32[]{:S(2)}, u32[]{:S(2)}) async-start(bf16[8,64,512]{2,1,0:T(8,128)(2,1)} %bitcast.6), calls=%async_computation.2 | async-start | bytes 1048576 | tf_op jit(solution)/shard_map/all_to_all | solution.py:32
  46.7 14.6 %collective-permute-start.5 = (bf16[512,512]{1,0:T(8,128)(2,1)S(1)}, bf16[512,512]{1,0:T(8,128)(2,1)}, u32[]{:S(2)}, u32[]{:S(2)}) collective-permute-start(bf16[512,512]{1,0:T(8,128)(2,1)S(1)} %collective-permute-done.3.refs_2_), channel_id=1, source_target_pairs={{0,32},{32,0},{1,33},{33,1},{2,34},{34,2},{3,35},{35,3},{4,36},{36... | collective-permute-start | bytes 1572872 | tf_op jit(solution)/shard_map/ppermute | solution.py:36
  50.8 22.3 %collective-permute-start.4 = (bf16[512,512]{1,0:T(8,128)(2,1)S(1)}, bf16[512,512]{1,0:T(8,128)(2,1)}, u32[]{:S(2)}, u32[]{:S(2)}) collective-permute-start(bf16[512,512]{1,0:T(8,128)(2,1)S(1)} %collective-permute-done.3.refs_2_), channel_id=1, source_target_pairs={{0,2},{2,0},{1,3},{3,1},{4,6},{6,4},{5,7},{7,5},{8,10},{10,8},{9,1... | collective-permute-start | bytes 1572872 | tf_op jit(solution)/shard_map/ppermute | solution.py:36
  61.2 11.9 %collective-permute-start.6 = (bf16[512,512]{1,0:T(8,128)(2,1)}, bf16[512,512]{1,0:T(8,128)(2,1)}, u32[]{:S(2)}, u32[]{:S(2)}) collective-permute-start(bf16[512,512]{1,0:T(8,128)(2,1)} %collective-permute-done.5.refs_6_), channel_id=1, source_target_pairs={{0,2},{2,0},{1,3},{3,1},{4,6},{6,4},{5,7},{7,5},{8,10},{10,8},{9,1... | collective-permute-start | bytes 1572872 | tf_op jit(solution)/shard_map/ppermute | solution.py:36
  66.5 16.5 %all-to-all-start.3 = ((bf16[4,64,512]{2,1,0:T(8,128)(2,1)}), bf16[4,64,512]{2,1,0:T(8,128)(2,1)S(1)}, u32[]{:S(2)}, u32[]{:S(2)}) async-start(bf16[4,64,512]{2,1,0:T(8,128)(2,1)} %shard_map.30), calls=%async_computation.3 | async-start | bytes 524288 | tf_op jit(solution)/shard_map/all_to_all | solution.py:32
  111.0 0.8 copy-start.1

commit v9 on v8

--- a/solution.py
+++ b/solution.py
@@ -47,7 +47,7 @@
     return tile * mask.reshape(width, width).astype(tile.dtype)
 
 
-def send_kernel(layer_ref, tile_ref, pattern_ref, out_ref, own_ref, rows_ref, kept_ref, sems):
+def send_kernel(layer_ref, tile_ref, pattern_ref, out_ref, rows_ref, kept_ref, sems):
     share, width = out_ref.shape[1:]
     blocks = pattern_ref.shape[1]
     height = 4 * share
@@ -73,7 +73,6 @@
     mask = jnp.dot(chosen.astype(jnp.float32), wide, preferred_element_type=jnp.float32)
     rows.wait()
     piece = (rows_ref[...].astype(jnp.float32) * mask).astype(out_ref.dtype)
-    own_ref[...] = piece
     for k in range(out_ref.shape[0]):
         p, c = k // 2 % 2, k % 2
         for q in range(2):
@@ -134,14 +133,11 @@
     height = 4 * nx * share
     flops = 8 * height * width * width
 
-    parts, own = pl.pallas_call(
+    parts = pl.pallas_call(
         send_kernel,
-        out_shape=(
-            jax.ShapeDtypeStruct((8, share, width), half),
-            jax.ShapeDtypeStruct((4 * share, width), half),
-        ),
+        out_shape=jax.ShapeDtypeStruct((8, share, width), half),
         in_specs=[SMEM, ANY, ANY],
-        out_specs=(VMEM, VMEM),
+        out_specs=VMEM,
         scratch_shapes=(
             pltpu.VMEM((4 * share, width), half),
             pltpu.VMEM(pattern.shape, jnp.int32),
@@ -154,6 +150,7 @@
     rows = exchange(rows(core, parts), "x").reshape(height, 2 * width)
 
     tile = masked(x_tiles[0], pattern[0])
+    own = lax.dynamic_slice_in_dim(tile, layer[0] * 4 * share, 4 * share, 0)
     below = swap(tile, "p")
     along = swap(tile, "q")
     corner = swap(along, "p")

time: 113 us -> 114 us (level)
  blocking collectives: 25.9 us -> 0 us
  waiting for transfers between devices: 20.7 us -> 37.4 us
  starting transfers between devices: 55.3 us -> 64.8 us
    all_to_all x1 -> x0, blocking collectives: 25.9 us -> none  [exchange(): return lax.all_to_all(blocks, axis, 0, 0, tiled=True)]
    all_to_all x4 -> x5, waiting for transfers between devices: 14.1 us -> 30.7 us  [exchange(): return lax.all_to_all(blocks, axis, 0, 0, tiled=True)]
    all_to_all x4 -> x5, starting transfers between devices: 28.3 us -> 37.7 us  [exchange(): return lax.all_to_all(blocks, axis, 0, 0, tiled=True)]
  transfers between devices with their start and end apart: 11 -> 12, of which waited for: 3 -> 4; matrix products, arithmetic and copies ran while one was open for 0% -> 0% of each run, Pallas kernels for 3% -> 3%
where the time goes in v9:
time: 114 us; the launch traced here: 113 us
  starting transfers between devices  64.8 us (57%)
  waiting for transfers between devices  37.4 us (33%)
  Pallas kernels  7.71 us (7%)
  other arithmetic  1.47 us (1%)
  local copies, waits for them, and re-layouts  1.23 us (1%)
    all_to_all x5, starting transfers between devices, exchange(): return lax.all_to_all(blocks, axis, 0, 0, tiled=True)  37.7 us
    all_to_all x5, waiting for transfers between devices, exchange(): return lax.all_to_all(blocks, axis, 0, 0, tiled=True)  30.7 us
    ppermute x7, starting transfers between devices, swap(): return lax.ppermute(tile, axis, ((0, 1), (1, 0)))  27.1 us
    ppermute x7, waiting for transfers between devices, swap(): return lax.ppermute(tile, axis, ((0, 1), (1, 0)))  6.67 us
    pallas_call x1, Pallas kernels, step(): parts = parts(place.reshape(1), squared, *tiles, *lower)  2.88 us
  transfers between devices with their start and end apart: 12, of which 4 were waited for; matrix products, arithmetic and copies ran while one was open for 0% of the time, Pallas kernels for 3%

profile of v9, /device:TPU:1, one launch (start us, length us, event | category | flops | bytes accessed | tf_op | source)
XLA Modules:
  0.0 112.7 jit_solution(16098494755914700909)
XLA Ops:
  0.0 0.7 convert_bitcast_fusion
  0.7 0.2 broadcast_in_dim.8
  0.9 0.0 copy-start
  0.9 0.6 convert_element_type.24
  1.5 0.4 copy-done
  1.9 0.1 bitcast_multiply_fusion.a_ref.refs_0_
  2.0 4.0 %collective-permute-start.1 = (bf16[512,512]{1,0:T(8,128)(2,1)S(1)}, bf16[512,512]{1,0:T(8,128)(2,1)S(1)}, u32[]{:S(2)}, u32[]{:S(2)}) collective-permute-start(bf16[512,512]{1,0:T(8,128)(2,1)S(1)} %bitcast_multiply_fusion.a_ref.refs_0_), channel_id=1, source_target_pairs={{0,32},{32,0},{1,33},{33,1},{2,34},{34,2},{3,35},{35,3},{4,36},{36... | collective-permute-start | bytes 1572872 | tf_op jit(solution)/shard_map/ppermute | solution.py:36
  6.0 1.7 %send.1 = bf16[8,16,512]{2,1,0:T(8,128)(2,1)} custom-call(s32[1]{0:T(128)} %bitcast.4.layer_ref, bf16[1,512,512]{2,1,0:T(8,128)(2,1)} %tile_ref.1, s32[1,8,8]{2,1,0:T(8,128)} %pattern_ref.1), custom_call_target="tpu_custom_call" | custom-call | tf_op jit(solution)/shard_map/send/pallas_call | solution.py:136
  7.7 8.0 %all-to-all-start = ((bf16[8,16,512]{2,1,0:T(8,128)(2,1)}), bf16[8,16,512]{2,1,0:T(8,128)(2,1)S(1)}, u32[]{:S(2)}, u32[]{:S(2)}) async-start(bf16[8,16,512]{2,1,0:T(8,128)(2,1)} %send.1), calls=%async_computation | async-start | bytes 262144 | tf_op jit(solution)/shard_map/all_to_all | solution.py:32
  15.7 2.0 %collective-permute-start = (bf16[512,512]{1,0:T(8,128)(2,1)S(1)}, bf16[512,512]{1,0:T(8,128)(2,1)S(1)}, u32[]{:S(2)}, u32[]{:S(2)}) collective-permute-start(bf16[512,512]{1,0:T(8,128)(2,1)S(1)} %bitcast_multiply_fusion.a_ref.refs_0_), channel_id=1, source_target_pairs={{0,2},{2,0},{1,3},{3,1},{4,6},{6,4},{5,7},{7,5},{8,10},{10,8},{9,1... | collective-permute-start | bytes 1572872 | tf_op jit(solution)/shard_map/ppermute | solution.py:36
  17.8 0.0 collective-permute-done.1.c_ref.refs_4_
  17.8 4.7 %collective-permute-start.2 = (bf16[512,512]{1,0:T(8,128)(2,1)S(1)}, bf16[512,512]{1,0:T(8,128)(2,1)S(1)}, u32[]{:S(2)}, u32[]{:S(2)}) collective-permute-start(bf16[512,512]{1,0:T(8,128)(2,1)S(1)} %collective-permute-done.1.c_ref.refs_4_), channel_id=1, source_target_pairs={{0,2},{2,0},{1,3},{3,1},{4,6},{6,4},{5,7},{7,5},{8,10},{10,8},{9,1... | collective-permute-start | bytes 1572872 | tf_op jit(solution)/shard_map/ppermute | solution.py:36
  22.5 0.0 all-to-all-done.parts_ref
  22.5 0.8 shard_map.28
  23.3 3.6 %all-to-all-start.1 = ((bf16[4,64,1024]{2,1,0:T(8,128)(2,1)}), bf16[4,64,1024]{2,1,0:T(8,128)(2,1)S(1)}, u32[]{:S(2)}, u32[]{:S(2)}) async-start(bf16[4,64,1024]{2,1,0:T(8,128)(2,1)} %shard_map.28), calls=%async_computation.1 | async-start | bytes 1048576 | tf_op jit(solution)/shard_map/all_to_all | solution.py:32
  26.9 4.0 %collective-permute-start.3 = (bf16[512,512]{1,0:T(8,128)(2,1)S(1)}, bf16[512,512]{1,0:T(8,128)(2,1)S(1)}, u32[]{:S(2)}, u32[]{:S(2)}) collective-permute-start(bf16[512,512]{1,0:T(8,128)(2,1)S(1)} %bitcast_multiply_fusion.a_ref.refs_0_), channel_id=1, source_target_pairs={{0,4},{4,0},{1,5},{5,1},{2,6},{6,2},{3,7},{7,3},{8,12},{12,8},{9,1... | collective-permute-start | bytes 1572872 | tf_op jit(solution)/shard_map/ppermute | solution.py:36
  30.9 0.0 collective-permute-done.b_ref.refs_1_
  30.9 4.2 %all-to-all-done.1 = bf16[4,64,1024]{2,1,0:T(8,128)(2,1)S(1)} async-done(((bf16[4,64,1024]{2,1,0:T(8,128)(2,1)}), bf16[4,64,1024]{2,1,0:T(8,128)(2,1)S(1)}, u32[]{:S(2)}, u32[]{:S(2)}) %all-to-all-start.1) | async-done | bytes 524320 | tf_op jit(solution)/shard_map/all_to_all | solution.py:32
  35.1 0.0 collective-permute-done.2.d_ref.refs_5_
  35.1 1.6 %shard_map.29 = bf16[8,2,32,512]{3,2,1,0:T(8,128)(2,1)} custom-call(bf16[256,1024]{1,0:T(8,128)(2,1)S(1)} %bitcast.19, bf16[512,512]{1,0:T(8,128)(2,1)S(1)} %bitcast_multiply_fusion.a_ref.refs_0_, bf16[512,512]{1,0:T(8,128)(2,1)S(1)} %collective-permute-done.b_ref.refs_1_, bf16[512,512]{1,0:T(8,128)(2,1)S(1)} %collective-permute-done.1.c_ref.refs_4_, ...), custom_call_target="tpu_custom_call" | custom-call | flops 536870912 | bytes 1048576 | tf_op jit(solution)/shard_map/pallas_call | solution.py:162
  36.6 10.0 %all-to-all-start.2 = ((bf16[8,64,512]{2,1,0:T(8,128)(2,1)}), bf16[8,64,512]{2,1,0:T(8,128)(2,1)S(1)}, u32[]{:S(2)}, u32[]{:S(2)}) async-start(bf16[8,64,512]{2,1,0:T(8,128)(2,1)} %bitcast.6), calls=%async_computation.2 | async-start | bytes 1048576 | tf_op jit(solution)/shard_map/all_to_all | solution.py:32
  46.7 0.0 collective-permute-done.3.refs_2_
  46.7 4.2 %collective-permute-start.5 = (bf16[512,512]{1,0:T(8,128)(2,1)S(1)}, bf16[512,512]{1,0:T(8,128)(2,1)}, u32[]{:S(2)}, u32[]{:S(2)}) collective-permute-start(bf16[512,512]{1,0:T(8,128)(2,1)S(1)} %collective-permute-done.3.refs_2_), channel_id=1, source_target_pairs={{0,32},{32,0},{1,33},{33,1},{2,34},{34,2},{3,35},{35,3},{4,36},{36... | collective-permute-start | bytes 1572872 | tf_op jit(solution)/shard_map/ppermute | solution.py:36
  50.8 3.7 %collective-permute-start.4 = (bf16[512,512]{1,0:T(8,128)(2,1)S(1)}, bf16[512,512]{1,0:T(8,128)(2,1)}, u32[]{:S(2)}, u32[]{:S(2)}) collective-permute-start(bf16[512,512]{1,0:T(8,128)(2,1)S(1)} %collective-permute-done.3.refs_2_), channel_id=1, source_target_pairs={{0,2},{2,0},{1,3},{3,1},{4,6},{6,4},{5,7},{7,5},{8,10},{10,8},{9,1... | collective-permute-start | bytes 1572872 | tf_op jit(solution)/shard_map/ppermute | solution.py:36
  54.6 6.6 %collective-permute-done.5.refs_6_ = bf16[512,512]{1,0:T(8,128)(2,1)} collective-permute-done((bf16[512,512]{1,0:T(8,128)(2,1)S(1)}, bf16[512,512]{1,0:T(8,128)(2,1)}, u32[]{:S(2)}, u32[]{:S(2)}) %collective-permute-start.5) | collective-permute-done | bytes 524320 | tf_op jit(solution)/shard_map/ppermute | solution.py:36
  61.2 4.5 %collective-permute-start.6 = (bf16[512,512]{1,0:T(8,128)(2,1)}, bf16[512,512]{1,0:T(8,128)(2,1)}, u32[]{:S(2)}, u32[]{:S(2)}) collective-permute-start(bf16[512,512]{1,0:T(8,128)(2,1)} %collective-permute-done.5.refs_6_), channel_id=1, source_target_pairs={{0,2},{2,0},{1,3},{3,1},{4,6},{6,4},{5,7},{7,5},{8,10},{10,8},{9,1... | collective-permute-start | bytes 1572872 | tf_op jit(solution)/shard_map/ppermute | solution.py:36
  65.7 0.0 all-to-all-done.2.parts_ref
  65.7 0.8 shard_map.30
  66.5 6.6 %all-to-all-start.3 = ((bf16[4,64,512]{2,1,0:T(8,128)(2,1)}), bf16[4,64,512]{2,1,0:T(8,128)(2,1)S(1)}, u32[]{:S(2)}, u32[]{:S(2)}) async-start(bf16[4,64,512]{2,1,0:T(8,128)(2,1)} %shard_map.30), calls=%async_computation.3 | async-start | bytes 524288 | tf_op jit(solution)/shard_map/all_to_all | solution.py:32
  73.1 0.0 collective-permute-done.4.refs_3_
  73.1 0.0 collective-permute-done.6.refs_7_
  73.1 9.9 %all-to-all-done.3 = bf16[4,64,512]{2,1,0:T(8,128)(2,1)S(1)} async-done(((bf16[4,64,512]{2,1,0:T(8,128)(2,1)}), bf16[4,64,512]{2,1,0:T(8,128)(2,1)S(1)}, u32[]{:S(2)}, u32[]{:S(2)}) %all-to-all-start.3) | async-done | bytes 262176 | tf_op jit(solution)/shard_map/all_to_all | solution.py:32
  83.0 2.9 %shard_map.31 = bf16[16,4,8,512]{3,2,1,0:T(8,128)(2,1)} custom-call(s32[1]{0:T(128)} %bitcast.2.place_ref, bf16[4,2,32,512]{3,2,1,0:T(8,128)(2,1)S(1)} %bitcast.20, bf16[512,512]{1,0:T(8,128)(2,1)S(1)} %bitcast_multiply_fusion.a_ref.refs_0_, bf16[512,512]{1,0:T(8,128)(2,1)S(1)} %collective-permute-done.b_ref.refs_1_, ...), custom_call_target="tpu_custom_call" | custom-call | flops 536870912 | bytes 1048576 | tf_op jit(solution)/shard_map/pallas_call | solution.py:169
  85.9 9.4 %all-to-all-start.4 = ((bf16[64,8,512]{2,1,0:T(8,128)(2,1)}), bf16[64,8,512]{2,1,0:T(8,128)(2,1)S(1)}, u32[]{:S(2)}, u32[]{:S(2)}) async-start(bf16[64,8,512]{2,1,0:T(8,128)(2,1)} %bitcast.8), calls=%async_computation.4 | async-start | bytes 1048576 | tf_op jit(solution)/shard_map/all_to_all | solution.py:32
  95.4 16.6 %all-to-all-done.4 = bf16[64,8,512]{2,1,0:T(8,128)(2,1)S(1)} async-done(((bf16[64,8,512]{2,1,0:T(8,128)(2,1)}), bf16[64,8,512]{2,1,0:T(8,128)(2,1)S(1)}, u32[]{:S(2)}, u32[]{:S(2)}) %all-to-all-start.4) | async-done | bytes 524320 | tf_op jit(solution)/shard_map/all_to_all | solution.py:32
  112.0 0.1 convert_reduce_fusion
  112.1 0.7 fusion
Async XLA Ops:
  0.9 1.0 copy-start
  2.0 15.7 %collective-permute-start.1 = (bf16[512,512]{1,0:T(8,128)(2,1)S(1)}, bf16[512,512]{1,0:T(8,128)(2,1)S(1)}, u32[]{:S(2)}, u32[]{:S(2)}) collective-permute-start(bf16[512,512]{1,0:T(8,128)(2,1)S(1)} %bitcast_multiply_fusion.a_ref.refs_0_), channel_id=1, source_target_pairs={{0,32},{32,0},{1,33},{33,1},{2,34},{34,2},{3,35},{35,3},{4,36},{36... | collective-permute-start | bytes 1572872 | tf_op jit(solution)/shard_map/ppermute | solution.py:36
  7.7 14.8 %all-to-all-start = ((bf16[8,16,512]{2,1,0:T(8,128)(2,1)}), bf16[8,16,512]{2,1,0:T(8,128)(2,1)S(1)}, u32[]{:S(2)}, u32[]{:S(2)}) async-start(bf16[8,16,512]{2,1,0:T(8,128)(2,1)} %send.1), calls=%async_computation | async-start | bytes 262144 | tf_op jit(solution)/shard_map/all_to_all | solution.py:32
  15.7 15.1 %collective-permute-start = (bf16[512,512]{1,0:T(8,128)(2,1)S(1)}, bf16[512,512]{1,0:T(8,128)(2,1)S(1)}, u32[]{:S(2)}, u32[]{:S(2)}) collective-permute-start(bf16[512,512]{1,0:T(8,128)(2,1)S(1)} %bitcast_multiply_fusion.a_ref.refs_0_), channel_id=1, source_target_pairs={{0,2},{2,0},{1,3},{3,1},{4,6},{6,4},{5,7},{7,5},{8,10},{10,8},{9,1... | collective-permute-start | bytes 1572872 | tf_op jit(solution)/shard_map/ppermute | solution.py:36
  17.8 17.3 %collective-permute-start.2 = (bf16[512,512]{1,0:T(8,128)(2,1)S(1)}, bf16[512,512]{1,0:T(8,128)(2,1)S(1)}, u32[]{:S(2)}, u32[]{:S(2)}) collective-permute-start(bf16[512,512]{1,0:T(8,128)(2,1)S(1)} %collective-permute-done.1.c_ref.refs_4_), channel_id=1, source_target_pairs={{0,2},{2,0},{1,3},{3,1},{4,6},{6,4},{5,7},{7,5},{8,10},{10,8},{9,1... | collective-permute-start | bytes 1572872 | tf_op jit(solution)/shard_map/ppermute | solution.py:36
  23.3 11.8 %all-to-all-start.1 = ((bf16[4,64,1024]{2,1,0:T(8,128)(2,1)}), bf16[4,64,1024]{2,1,0:T(8,128)(2,1)S(1)}, u32[]{:S(2)}, u32[]{:S(2)}) async-start(bf16[4,64,1024]{2,1,0:T(8,128)(2,1)} %shard_map.28), calls=%async_computation.1 | async-start | bytes 1048576 | tf_op jit(solution)/shard_map/all_to_all | solution.py:32
  26.9 19.8 %collective-permute-start.3 = (bf16[512,512]{1,0:T(8,128)(2,1)S(1)}, bf16[512,512]{1,0:T(8,128)(2,1)S(1)}, u32[]{:S(2)}, u32[]{:S(2)}) collective-permute-start(bf16[512,512]{1,0:T(8,128)(2,1)S(1)} %bitcast_multiply_fusion.a_ref.refs_0_), channel_id=1, source_target_pairs={{0,4},{4,0},{1,5},{5,1},{2,6},{6,2},{3,7},{7,3},{8,12},{12,8},{9,1... | collective-permute-start | bytes 1572872 | tf_op jit(solution)/shard_map/ppermute | solution.py:36
  36.6 29.1 %all-to-all-start.2 = ((bf16[8,64,512]{2,1,0:T(8,128)(2,1)}), bf16[8,64,512]{2,1,0:T(8,128)(2,1)S(1)}, u32[]{:S(2)}, u32[]{:S(2)}) async-start(bf16[8,64,512]{2,1,0:T(8,128)(2,1)} %bitcast.6), calls=%async_computation.2 | async-start | bytes 1048576 | tf_op jit(solution)/shard_map/all_to_all | solution.py:32
  46.7 14.6 %collective-permute-start.5 = (bf16[512,512]{1,0:T(8,128)(2,1)S(1)}, bf16[512,512]{1,0:T(8,128)(2,1)}, u32[]{:S(2)}, u32[]{:S(2)}) collective-permute-start(bf16[512,512]{1,0:T(8,128)(2,1)S(1)} %collective-permute-done.3.refs_2_), channel_id=1, source_target_pairs={{0,32},{32,0},{1,33},{33,1},{2,34},{34,2},{3,35},{35,3},{4,36},{36... | collective-permute-start | bytes 1572872 | tf_op jit(solution)/shard_map/ppermute | solution.py:36
  50.8 22.3 %collective-permute-start.4 = (bf16[512,512]{1,0:T(8,128)(2,1)S(1)}, bf16[512,512]{1,0:T(8,128)(2,1)}, u32[]{:S(2)}, u32[]{:S(2)}) collective-permute-start(bf16[512,512]{1,0:T(8,128)(2,1)S(1)} %collective-permute-done.3.refs_2_), channel_id=1, source_target_pairs={{0,2},{2,0},{1,3},{3,1},{4,6},{6,4},{5,7},{7,5},{8,10},{10,8},{9,1... | collective-permute-start | bytes 1572872 | tf_op jit(solution)/shard_map/ppermute | solution.py:36
  61.2 11.9 %collective-permute-start.6 = (bf16[512,512]{1,0:T(8,128)(2,1)}, bf16[512,512]{1,0:T(8,128)(2,1)}, u32[]{:S(2)}, u32[]{:S(2)}) collective-permute-start(bf16[512,512]{1,0:T(8,128)(2,1)} %collective-permute-done.5.refs_6_), channel_id=1, source_target_pairs={{0,2},{2,0},{1,3},{3,1},{4,6},{6,4},{5,7},{7,5},{8,10},{10,8},{9,1... | collective-permute-start | bytes 1572872 | tf_op jit(solution)/shard_map/ppermute | solution.py:36
  66.5 16.5 %all-to-all-start.3 = ((bf16[4,64,512]{2,1,0:T(8,128)(2,1)}), bf16[4,64,512]{2,1,0:T(8,128)(2,1)S(1)}, u32[]{:S(2)}, u32[]{:S(2)}) async-start(bf16[4,64,512]{2,1,0:T(8,128)(2,1)} %shard_map.30), calls=%async_computation.3 | async-start | bytes 524288 | tf_op jit(solution)/shard_map/all_to_all | solution.py:32
  85.9 26.1 %all-to-all-start.4 = ((bf16[64,8,512]{2,1,0:T(8,128)(2,1)}), bf16[64,8,512]{2,1,0:T(8,128)(2,1)S(1)}, u32[]{:S(2)}, u32[]{:S(2)}) async-start(bf16[64,8,512]{2,1,0:T(8,128)(2,1)} %bitcast.8), calls=%async_computation.4 | async-start | bytes 1048576 | tf_op jit(solution)/shard_map/all_to_all | solution.py:32

commit v10 on v7

--- a/solution.py
+++ b/solution.py
@@ -47,7 +47,7 @@
     return tile * mask.reshape(width, width).astype(tile.dtype)
 
 
-def send_kernel(layer_ref, tile_ref, pattern_ref, out_ref, own_ref, rows_ref, kept_ref, sems):
+def send_kernel(layer_ref, tile_ref, pattern_ref, out_ref, rows_ref, kept_ref, sems):
     share, width = out_ref.shape[1:]
     blocks = pattern_ref.shape[1]
     height = 4 * share
@@ -72,7 +72,6 @@
     mask = jnp.dot(chosen.astype(jnp.float32), wide, preferred_element_type=jnp.float32)
     rows.wait()
     piece = (rows_ref[...].astype(jnp.float32) * mask).astype(out_ref.dtype)
-    own_ref[...] = piece
     for k in range(out_ref.shape[0]):
         part = k % 4 * share
         out_ref[k] = piece[part : part + share]
@@ -105,8 +104,18 @@
     for k, (one, two) in enumerate(((a_ref, c_ref), (b_ref, d_ref))):
         part = jnp.dot(left, one[...], preferred_element_type=jnp.float32)
         part += jnp.dot(right, two[...], preferred_element_type=jnp.float32)
-        part = part.astype(out_ref.dtype).reshape(-1, out_ref.shape[2], width)
+        part = part.astype(out_ref.dtype).reshape(out_ref.shape[0], -1, width)
         out_ref[:, lax.bitwise_xor(core_ref[0], k)] = part
+
+
+def sum_kernel(parts_ref, out_ref):
+    share = out_ref.shape[1]
+    value = parts_ref[0].astype(jnp.float32)
+    for k in range(1, parts_ref.shape[0]):
+        value += parts_ref[k].astype(jnp.float32)
+    value = value.astype(out_ref.dtype)
+    for k in range(out_ref.shape[0]):
+        out_ref[k] = value[k % 2, k // 2 * share : (k // 2 + 1) * share]
 
 
 def step(x_tiles, pattern):
@@ -119,14 +128,11 @@
     height = 4 * nx * share
     flops = 8 * height * width * width
 
-    parts, own = pl.pallas_call(
+    parts = pl.pallas_call(
         send_kernel,
-        out_shape=(
-            jax.ShapeDtypeStruct((8, share, width), half),
-            jax.ShapeDtypeStruct((4 * share, width), half),
-        ),
+        out_shape=jax.ShapeDtypeStruct((8, share, width), half),
         in_specs=[SMEM, ANY, ANY],
-        out_specs=(VMEM, VMEM),
+        out_specs=VMEM,
         scratch_shapes=(
             pltpu.VMEM((4 * share, width), half),
             pltpu.VMEM(pattern.shape, jnp.int32),
@@ -134,11 +140,14 @@
         ),
         name="send",
     )(layer, x_tiles, pattern)
+    index = lax.axis_index("l").astype(jnp.uint32) * (4 * share)
+    parts, index = lax.optimization_barrier((parts, index))
     parts = exchange(parts, ("h", "p", "c"))
     rows = call(rows_kernel, (nx, 4 * share, 2 * width), half, [SMEM, VMEM])
     rows = exchange(rows(core, parts), "x").reshape(height, 2 * width)
 
     tile = masked(x_tiles[0], pattern[0])
+    own = lax.dynamic_slice(tile, (index, jnp.uint32(0)), (4 * share, width))
     below = swap(tile, "p")
     tiles = [tile, swap(tile, "c"), below, swap(below, "c")]
 
@@ -148,11 +157,13 @@
     squared = total(exchange(partial, "z")).astype(half)
     squared = jnp.broadcast_to(squared[None], (nz,) + squared.shape)
     squared = exchange(squared, "z").reshape(shape)
-    shape = (4 * nx, 2, share, width)
+    shape = (nx, 2, 4 * share, width)
     parts = call(second_kernel, shape, half, [SMEM] + [VMEM] * 5, flops)
-    parts = parts(core, squared, *tiles).reshape(8 * nx, share, width)
-    parts = exchange(parts, ("x", "h", "p", "c"))
-    cubed = total(parts.reshape(2 * nx, 4 * share, width))
+    parts = parts(core, squared, *tiles).reshape(nx, 8 * share, width)
+    parts = exchange(parts, "x").reshape(shape)
+    parts = call(sum_kernel, (8, share, width), half, [VMEM])(parts)
+    parts = exchange(parts, ("h", "p", "c"))
+    cubed = total(parts.reshape(2, 4 * share, width))
     signed = 1.5 * own.astype(jnp.float32) - 0.5 * cubed
     return signed.astype(half)[None]
 

time: 109 us -> 107 us (0.982)
  blocking collectives: 70.7 us -> 69.4 us
    all_to_all x3 -> x4, blocking collectives: 70.7 us -> 69.4 us  [exchange(): return lax.all_to_all(blocks, axis, 0, 0, tiled=True)]
    pallas_call x2 -> x3, Pallas kernels: 2.38 us -> 2.42 us  [the longest x1 1.65 us: step(): pl.pallas_call(send_kernel, out_shape=jax.ShapeDtypeStruct((8, share, wid...]
where the time goes in v10:
time: 107 us
  blocking collectives  69.4 us (65%)
  starting transfers between devices  22.3 us (21%)
  waiting for transfers between devices  8.2 us (8%)
  Pallas kernels  3.99 us (4%)
  other arithmetic  1.5 us (1%)
  local copies, waits for them, and re-layouts  1.27 us (1%)
    all_to_all x4, blocking collectives, exchange(): return lax.all_to_all(blocks, axis, 0, 0, tiled=True)  69.4 us
    all_to_all x2, starting transfers between devices, exchange(): return lax.all_to_all(blocks, axis, 0, 0, tiled=True)  11.6 us
    ppermute x3, starting transfers between devices, swap(): return lax.ppermute(tile, axis, ((0, 1), (1, 0)))  10.7 us
    all_to_all x2, waiting for transfers between devices, exchange(): return lax.all_to_all(blocks, axis, 0, 0, tiled=True)  8.2 us
  transfers between devices with their start and end apart: 5, of which 1 were waited for; matrix products, arithmetic and copies ran while one was open for 0% of the time, Pallas kernels for 1%

profile of v10, /device:TPU:1, one launch (start us, length us, event | category | flops | bytes accessed | tf_op | source)
XLA Modules:
  0.0 106.8 jit_solution(11234438615258837738)
XLA Ops:
  0.0 0.7 convert_bitcast_fusion
  0.7 0.2 broadcast_in_dim.6
  0.9 0.0 copy-start
  0.9 0.6 convert_element_type.29
  1.5 0.4 copy-done
  1.9 0.1 bitcast_multiply_fusion.a_ref
  2.0 4.0 %collective-permute-start.1 = (bf16[512,512]{1,0:T(8,128)(2,1)S(1)}, bf16[512,512]{1,0:T(8,128)(2,1)S(1)}, u32[]{:S(2)}, u32[]{:S(2)}) collective-permute-start(bf16[512,512]{1,0:T(8,128)(2,1)S(1)} %bitcast_multiply_fusion.a_ref), channel_id=1, source_target_pairs={{0,32},{32,0},{1,33},{33,1},{2,34},{34,2},{3,35},{35,3},{4,36},{36... | collective-permute-start | bytes 1572872 | tf_op jit(solution)/shard_map/ppermute | solution.py:36
  6.0 1.7 %send.1 = bf16[8,16,512]{2,1,0:T(8,128)(2,1)} custom-call(s32[1]{0:T(128)} %bitcast.2.layer_ref, bf16[1,512,512]{2,1,0:T(8,128)(2,1)} %tile_ref.1, s32[1,8,8]{2,1,0:T(8,128)} %pattern_ref.1), custom_call_target="tpu_custom_call" | custom-call | tf_op jit(solution)/shard_map/send/pallas_call | solution.py:131
  7.7 8.0 %all-to-all-start = ((bf16[8,16,512]{2,1,0:T(8,128)(2,1)}), bf16[8,16,512]{2,1,0:T(8,128)(2,1)S(1)}, u32[]{:S(2)}, u32[]{:S(2)}) async-start(bf16[8,16,512]{2,1,0:T(8,128)(2,1)} %send.1), calls=%async_computation | async-start | bytes 262144 | tf_op jit(solution)/shard_map/all_to_all | solution.py:32
  15.7 2.0 %collective-permute-start = (bf16[512,512]{1,0:T(8,128)(2,1)S(1)}, bf16[512,512]{1,0:T(8,128)(2,1)S(1)}, u32[]{:S(2)}, u32[]{:S(2)}) collective-permute-start(bf16[512,512]{1,0:T(8,128)(2,1)S(1)} %bitcast_multiply_fusion.a_ref), channel_id=1, source_target_pairs={{0,2},{2,0},{1,3},{3,1},{4,6},{6,4},{5,7},{7,5},{8,10},{10,8},{9,1... | collective-permute-start | bytes 1572872 | tf_op jit(solution)/shard_map/ppermute | solution.py:36
  17.7 0.0 collective-permute-done.1.c_ref
  17.8 4.7 %collective-permute-start.2 = (bf16[512,512]{1,0:T(8,128)(2,1)S(1)}, bf16[512,512]{1,0:T(8,128)(2,1)S(1)}, u32[]{:S(2)}, u32[]{:S(2)}) collective-permute-start(bf16[512,512]{1,0:T(8,128)(2,1)S(1)} %collective-permute-done.1.c_ref), channel_id=1, source_target_pairs={{0,2},{2,0},{1,3},{3,1},{4,6},{6,4},{5,7},{7,5},{8,10},{10,8},{9,1... | collective-permute-start | bytes 1572872 | tf_op jit(solution)/shard_map/ppermute | solution.py:36
  22.5 0.0 all-to-all-done.parts_ref
  22.5 0.8 shard_map.28
  23.3 3.6 %all-to-all-start.1 = ((bf16[4,64,1024]{2,1,0:T(8,128)(2,1)}), bf16[4,64,1024]{2,1,0:T(8,128)(2,1)S(1)}, u32[]{:S(2)}, u32[]{:S(2)}) async-start(bf16[4,64,1024]{2,1,0:T(8,128)(2,1)} %shard_map.28), calls=%async_computation.1 | async-start | bytes 1048576 | tf_op jit(solution)/shard_map/all_to_all | solution.py:32
  26.9 0.0 collective-permute-done.b_ref
  26.9 8.2 %all-to-all-done.1 = bf16[4,64,1024]{2,1,0:T(8,128)(2,1)S(1)} async-done(((bf16[4,64,1024]{2,1,0:T(8,128)(2,1)}), bf16[4,64,1024]{2,1,0:T(8,128)(2,1)S(1)}, u32[]{:S(2)}, u32[]{:S(2)}) %all-to-all-start.1) | async-done | bytes 524320 | tf_op jit(solution)/shard_map/all_to_all | solution.py:32
  35.1 0.0 collective-permute-done.2.d_ref
  35.1 0.7 shard_map.29
  35.8 24.3 %all_to_all.30 = bf16[8,64,512]{2,1,0:T(8,128)(2,1)S(1)} all-to-all(bf16[8,64,512]{2,1,0:T(8,128)(2,1)S(1)} %bitcast.23), channel_id=1, replica_groups=mesh['x'=4,'h'=2,'p'=2,'z'=8,'c'=2,'l'=2] {'z'}, dimensions={0} | all-to-all | bytes 1048576 | tf_op jit(solution)/shard_map/all_to_all | solution.py:32
  60.2 0.1 reduce_sum.21
  60.3 16.9 %all_to_all.31 = bf16[8,64,512]{2,1,0:T(8,128)(2,1)S(1)} all-to-all(bf16[8,64,512]{2,1,0:T(8,128)(2,1)S(1)} %broadcast_in_dim.7), channel_id=1, replica_groups=mesh['x'=4,'h'=2,'p'=2,'z'=8,'c'=2,'l'=2] {'z'}, dimensions={0} | all-to-all | bytes 1048576 | tf_op jit(solution)/shard_map/all_to_all | solution.py:32
  77.2 0.7 shard_map.30
  77.9 9.3 %all_to_all.32 = bf16[4,128,512]{2,1,0:T(8,128)(2,1)S(1)} all-to-all(bf16[4,128,512]{2,1,0:T(8,128)(2,1)S(1)} %bitcast.22), channel_id=1, replica_groups=mesh['x'=4,'h'=2,'p'=2,'z'=8,'c'=2,'l'=2] {'x'}, dimensions={0} | all-to-all | bytes 1048576 | tf_op jit(solution)/shard_map/all_to_all | solution.py:32
  87.3 0.1 shard_map.31
  87.3 18.8 %all_to_all.33 = bf16[8,16,512]{2,1,0:T(8,128)(2,1)S(1)} all-to-all(bf16[8,16,512]{2,1,0:T(8,128)(2,1)S(1)} %shard_map.31), channel_id=1, replica_groups=mesh['x'=4,'h'=2,'p'=2,'z'=8,'c'=2,'l'=2] {'h','p','c'}, dimensions={0} | all-to-all | bytes 262144 | tf_op jit(solution)/shard_map/all_to_all | solution.py:32
  106.2 0.7 fusion
  (2 shorter events, 0.1 us)
Async XLA Ops:
  0.9 1.0 copy-start
  2.0 15.7 %collective-permute-start.1 = (bf16[512,512]{1,0:T(8,128)(2,1)S(1)}, bf16[512,512]{1,0:T(8,128)(2,1)S(1)}, u32[]{:S(2)}, u32[]{:S(2)}) collective-permute-start(bf16[512,512]{1,0:T(8,128)(2,1)S(1)} %bitcast_multiply_fusion.a_ref), channel_id=1, source_target_pairs={{0,32},{32,0},{1,33},{33,1},{2,34},{34,2},{3,35},{35,3},{4,36},{36... | collective-permute-start | bytes 1572872 | tf_op jit(solution)/shard_map/ppermute | solution.py:36
  7.7 14.8 %all-to-all-start = ((bf16[8,16,512]{2,1,0:T(8,128)(2,1)}), bf16[8,16,512]{2,1,0:T(8,128)(2,1)S(1)}, u32[]{:S(2)}, u32[]{:S(2)}) async-start(bf16[8,16,512]{2,1,0:T(8,128)(2,1)} %send.1), calls=%async_computation | async-start | bytes 262144 | tf_op jit(solution)/shard_map/all_to_all | solution.py:32
  15.7 11.1 %collective-permute-start = (bf16[512,512]{1,0:T(8,128)(2,1)S(1)}, bf16[512,512]{1,0:T(8,128)(2,1)S(1)}, u32[]{:S(2)}, u32[]{:S(2)}) collective-permute-start(bf16[512,512]{1,0:T(8,128)(2,1)S(1)} %bitcast_multiply_fusion.a_ref), channel_id=1, source_target_pairs={{0,2},{2,0},{1,3},{3,1},{4,6},{6,4},{5,7},{7,5},{8,10},{10,8},{9,1... | collective-permute-start | bytes 1572872 | tf_op jit(solution)/shard_map/ppermute | solution.py:36
  17.8 17.3 %collective-permute-start.2 = (bf16[512,512]{1,0:T(8,128)(2,1)S(1)}, bf16[512,512]{1,0:T(8,128)(2,1)S(1)}, u32[]{:S(2)}, u32[]{:S(2)}) collective-permute-start(bf16[512,512]{1,0:T(8,128)(2,1)S(1)} %collective-permute-done.1.c_ref), channel_id=1, source_target_pairs={{0,2},{2,0},{1,3},{3,1},{4,6},{6,4},{5,7},{7,5},{8,10},{10,8},{9,1... | collective-permute-start | bytes 1572872 | tf_op jit(solution)/shard_map/ppermute | solution.py:36
  23.3 11.8 %all-to-all-start.1 = ((bf16[4,64,1024]{2,1,0:T(8,128)(2,1)}), bf16[4,64,1024]{2,1,0:T(8,128)(2,1)S(1)}, u32[]{:S(2)}, u32[]{:S(2)}) async-start(bf16[4,64,1024]{2,1,0:T(8,128)(2,1)} %shard_map.28), calls=%async_computation.1 | async-start | bytes 1048576 | tf_op jit(solution)/shard_map/all_to_all | solution.py:32

commit v11 on v10

--- a/solution.py
+++ b/solution.py
@@ -78,19 +78,19 @@
 
 
 def rows_kernel(core_ref, parts_ref, out_ref):
-    share, width = parts_ref.shape[1:]
+    share, _ = parts_ref.shape[1:]
     for k in range(parts_ref.shape[0] // 2):
         for side in range(2):
             piece = parts_ref[2 * k + lax.bitwise_xor(core_ref[0], side)]
             for far in range(out_ref.shape[0]):
-                rows, columns = pl.ds(k * share, share), pl.ds(side * width, width)
-                out_ref[far, rows, columns] = piece
+                out_ref[far, side, pl.ds(k * share, share)] = piece
 
 
 def first_kernel(rows_ref, a_ref, b_ref, c_ref, d_ref, out_ref):
     width = a_ref.shape[0]
     turned = (((1,), (1,)), ((), ()))
-    left, right = rows_ref[:, :width], rows_ref[:, width:]
+    left = rows_ref[:, 0].reshape(-1, width)
+    right = rows_ref[:, 1].reshape(-1, width)
     for k, (one, two) in enumerate(((a_ref, b_ref), (c_ref, d_ref))):
         part = lax.dot_general(left, one[...], turned, preferred_element_type=jnp.float32)
         part += lax.dot_general(right, two[...], turned, preferred_element_type=jnp.float32)
@@ -143,8 +143,9 @@
     index = lax.axis_index("l").astype(jnp.uint32) * (4 * share)
     parts, index = lax.optimization_barrier((parts, index))
     parts = exchange(parts, ("h", "p", "c"))
-    rows = call(rows_kernel, (nx, 4 * share, 2 * width), half, [SMEM, VMEM])
-    rows = exchange(rows(core, parts), "x").reshape(height, 2 * width)
+    shape = (nx, 2, 4 * share, width)
+    rows = call(rows_kernel, shape, half, [SMEM, VMEM])(core, parts)
+    rows = exchange(rows.reshape(nx, 8 * share, width), "x").reshape(shape)
 
     tile = masked(x_tiles[0], pattern[0])
     own = lax.dynamic_slice(tile, (index, jnp.uint32(0)), (4 * share, width))

time: 107 us -> 107 us (level)
  no operation moved by 1% of the time
where the time goes in v11:
time: 107 us
  blocking collectives  69.4 us (65%)
  starting transfers between devices  22.3 us (21%)
  waiting for transfers between devices  8.2 us (8%)
  Pallas kernels  3.99 us (4%)
  other arithmetic  1.5 us (1%)
  local copies, waits for them, and re-layouts  1.27 us (1%)
    all_to_all x4, blocking collectives, exchange(): return lax.all_to_all(blocks, axis, 0, 0, tiled=True)  69.4 us
    all_to_all x2, starting transfers between devices, exchange(): return lax.all_to_all(blocks, axis, 0, 0, tiled=True)  11.6 us
    ppermute x3, starting transfers between devices, swap(): return lax.ppermute(tile, axis, ((0, 1), (1, 0)))  10.7 us
    all_to_all x2, waiting for transfers between devices, exchange(): return lax.all_to_all(blocks, axis, 0, 0, tiled=True)  8.2 us
  transfers between devices with their start and end apart: 5, of which 1 were waited for; matrix products, arithmetic and copies ran while one was open for 0% of the time, Pallas kernels for 1%

profile of v11, /device:TPU:1, one launch (start us, length us, event | category | flops | bytes accessed | tf_op | source)
XLA Modules:
  0.0 106.8 jit_solution(9841319287167780495)
XLA Ops:
  0.0 0.7 convert_bitcast_fusion
  0.7 0.2 broadcast_in_dim.6
  0.9 0.0 copy-start
  0.9 0.6 convert_element_type.29
  1.5 0.4 copy-done
  1.9 0.1 bitcast_multiply_fusion.a_ref
  2.0 4.0 %collective-permute-start.1 = (bf16[512,512]{1,0:T(8,128)(2,1)S(1)}, bf16[512,512]{1,0:T(8,128)(2,1)S(1)}, u32[]{:S(2)}, u32[]{:S(2)}) collective-permute-start(bf16[512,512]{1,0:T(8,128)(2,1)S(1)} %bitcast_multiply_fusion.a_ref), channel_id=1, source_target_pairs={{0,32},{32,0},{1,33},{33,1},{2,34},{34,2},{3,35},{35,3},{4,36},{36... | collective-permute-start | bytes 1572872 | tf_op jit(solution)/shard_map/ppermute | solution.py:36
  6.0 1.7 %send.1 = bf16[8,16,512]{2,1,0:T(8,128)(2,1)} custom-call(s32[1]{0:T(128)} %bitcast.2.layer_ref, bf16[1,512,512]{2,1,0:T(8,128)(2,1)} %tile_ref.1, s32[1,8,8]{2,1,0:T(8,128)} %pattern_ref.1), custom_call_target="tpu_custom_call" | custom-call | tf_op jit(solution)/shard_map/send/pallas_call | solution.py:131
  7.7 8.0 %all-to-all-start = ((bf16[8,16,512]{2,1,0:T(8,128)(2,1)}), bf16[8,16,512]{2,1,0:T(8,128)(2,1)S(1)}, u32[]{:S(2)}, u32[]{:S(2)}) async-start(bf16[8,16,512]{2,1,0:T(8,128)(2,1)} %send.1), calls=%async_computation | async-start | bytes 262144 | tf_op jit(solution)/shard_map/all_to_all | solution.py:32
  15.7 2.0 %collective-permute-start = (bf16[512,512]{1,0:T(8,128)(2,1)S(1)}, bf16[512,512]{1,0:T(8,128)(2,1)S(1)}, u32[]{:S(2)}, u32[]{:S(2)}) collective-permute-start(bf16[512,512]{1,0:T(8,128)(2,1)S(1)} %bitcast_multiply_fusion.a_ref), channel_id=1, source_target_pairs={{0,2},{2,0},{1,3},{3,1},{4,6},{6,4},{5,7},{7,5},{8,10},{10,8},{9,1... | collective-permute-start | bytes 1572872 | tf_op jit(solution)/shard_map/ppermute | solution.py:36
  17.7 0.0 collective-permute-done.1.c_ref
  17.8 4.7 %collective-permute-start.2 = (bf16[512,512]{1,0:T(8,128)(2,1)S(1)}, bf16[512,512]{1,0:T(8,128)(2,1)S(1)}, u32[]{:S(2)}, u32[]{:S(2)}) collective-permute-start(bf16[512,512]{1,0:T(8,128)(2,1)S(1)} %collective-permute-done.1.c_ref), channel_id=1, source_target_pairs={{0,2},{2,0},{1,3},{3,1},{4,6},{6,4},{5,7},{7,5},{8,10},{10,8},{9,1... | collective-permute-start | bytes 1572872 | tf_op jit(solution)/shard_map/ppermute | solution.py:36
  22.5 0.0 all-to-all-done.parts_ref
  22.5 0.8 shard_map.28
  23.3 3.6 %all-to-all-start.1 = ((bf16[4,128,512]{2,1,0:T(8,128)(2,1)}), bf16[4,128,512]{2,1,0:T(8,128)(2,1)S(1)}, u32[]{:S(2)}, u32[]{:S(2)}) async-start(bf16[4,128,512]{2,1,0:T(8,128)(2,1)} %bitcast.4), calls=%async_computation.1 | async-start | bytes 1048576 | tf_op jit(solution)/shard_map/all_to_all | solution.py:32
  26.9 0.0 collective-permute-done.b_ref
  26.9 8.2 %all-to-all-done.1 = bf16[4,128,512]{2,1,0:T(8,128)(2,1)S(1)} async-done(((bf16[4,128,512]{2,1,0:T(8,128)(2,1)}), bf16[4,128,512]{2,1,0:T(8,128)(2,1)S(1)}, u32[]{:S(2)}, u32[]{:S(2)}) %all-to-all-start.1) | async-done | bytes 524320 | tf_op jit(solution)/shard_map/all_to_all | solution.py:32
  35.1 0.0 collective-permute-done.2.d_ref
  35.1 0.7 shard_map.29
  35.8 24.3 %all_to_all.30 = bf16[8,64,512]{2,1,0:T(8,128)(2,1)S(1)} all-to-all(bf16[8,64,512]{2,1,0:T(8,128)(2,1)S(1)} %bitcast.24), channel_id=1, replica_groups=mesh['x'=4,'h'=2,'p'=2,'z'=8,'c'=2,'l'=2] {'z'}, dimensions={0} | all-to-all | bytes 1048576 | tf_op jit(solution)/shard_map/all_to_all | solution.py:32
  60.2 0.1 reduce_sum.21
  60.3 16.9 %all_to_all.31 = bf16[8,64,512]{2,1,0:T(8,128)(2,1)S(1)} all-to-all(bf16[8,64,512]{2,1,0:T(8,128)(2,1)S(1)} %broadcast_in_dim.7), channel_id=1, replica_groups=mesh['x'=4,'h'=2,'p'=2,'z'=8,'c'=2,'l'=2] {'z'}, dimensions={0} | all-to-all | bytes 1048576 | tf_op jit(solution)/shard_map/all_to_all | solution.py:32
  77.2 0.7 shard_map.30
  77.9 9.3 %all_to_all.32 = bf16[4,128,512]{2,1,0:T(8,128)(2,1)S(1)} all-to-all(bf16[4,128,512]{2,1,0:T(8,128)(2,1)S(1)} %bitcast.23), channel_id=1, replica_groups=mesh['x'=4,'h'=2,'p'=2,'z'=8,'c'=2,'l'=2] {'x'}, dimensions={0} | all-to-all | bytes 1048576 | tf_op jit(solution)/shard_map/all_to_all | solution.py:32
  87.3 0.1 shard_map.31
  87.3 18.8 %all_to_all.33 = bf16[8,16,512]{2,1,0:T(8,128)(2,1)S(1)} all-to-all(bf16[8,16,512]{2,1,0:T(8,128)(2,1)S(1)} %shard_map.31), channel_id=1, replica_groups=mesh['x'=4,'h'=2,'p'=2,'z'=8,'c'=2,'l'=2] {'h','p','c'}, dimensions={0} | all-to-all | bytes 262144 | tf_op jit(solution)/shard_map/all_to_all | solution.py:32
  106.2 0.7 fusion
  (2 shorter events, 0.1 us)
Async XLA Ops:
  0.9 1.0 copy-start
  2.0 15.7 %collective-permute-start.1 = (bf16[512,512]{1,0:T(8,128)(2,1)S(1)}, bf16[512,512]{1,0:T(8,128)(2,1)S(1)}, u32[]{:S(2)}, u32[]{:S(2)}) collective-permute-start(bf16[512,512]{1,0:T(8,128)(2,1)S(1)} %bitcast_multiply_fusion.a_ref), channel_id=1, source_target_pairs={{0,32},{32,0},{1,33},{33,1},{2,34},{34,2},{3,35},{35,3},{4,36},{36... | collective-permute-start | bytes 1572872 | tf_op jit(solution)/shard_map/ppermute | solution.py:36
  7.7 14.8 %all-to-all-start = ((bf16[8,16,512]{2,1,0:T(8,128)(2,1)}), bf16[8,16,512]{2,1,0:T(8,128)(2,1)S(1)}, u32[]{:S(2)}, u32[]{:S(2)}) async-start(bf16[8,16,512]{2,1,0:T(8,128)(2,1)} %send.1), calls=%async_computation | async-start | bytes 262144 | tf_op jit(solution)/shard_map/all_to_all | solution.py:32
  15.7 11.1 %collective-permute-start = (bf16[512,512]{1,0:T(8,128)(2,1)S(1)}, bf16[512,512]{1,0:T(8,128)(2,1)S(1)}, u32[]{:S(2)}, u32[]{:S(2)}) collective-permute-start(bf16[512,512]{1,0:T(8,128)(2,1)S(1)} %bitcast_multiply_fusion.a_ref), channel_id=1, source_target_pairs={{0,2},{2,0},{1,3},{3,1},{4,6},{6,4},{5,7},{7,5},{8,10},{10,8},{9,1... | collective-permute-start | bytes 1572872 | tf_op jit(solution)/shard_map/ppermute | solution.py:36
  17.8 17.3 %collective-permute-start.2 = (bf16[512,512]{1,0:T(8,128)(2,1)S(1)}, bf16[512,512]{1,0:T(8,128)(2,1)S(1)}, u32[]{:S(2)}, u32[]{:S(2)}) collective-permute-start(bf16[512,512]{1,0:T(8,128)(2,1)S(1)} %collective-permute-done.1.c_ref), channel_id=1, source_target_pairs={{0,2},{2,0},{1,3},{3,1},{4,6},{6,4},{5,7},{7,5},{8,10},{10,8},{9,1... | collective-permute-start | bytes 1572872 | tf_op jit(solution)/shard_map/ppermute | solution.py:36
  23.3 11.8 %all-to-all-start.1 = ((bf16[4,128,512]{2,1,0:T(8,128)(2,1)}), bf16[4,128,512]{2,1,0:T(8,128)(2,1)S(1)}, u32[]{:S(2)}, u32[]{:S(2)}) async-start(bf16[4,128,512]{2,1,0:T(8,128)(2,1)} %bitcast.4), calls=%async_computation.1 | async-start | bytes 1048576 | tf_op jit(solution)/shard_map/all_to_all | solution.py:32
